TPU v7x, 32 devices: a whole 2x2x4 slice. The times are simulated.
32 devices in a mesh: sky: 8 (over z, y), batch: 4 (over x, core).
Axes of the slice: x: 2, y: 2, z: 4, core: 2. Of those that a mesh axis runs over, the one named last changes fastest.
Arguments:
- features: float32 [4, 8, 80, 1024], P('batch', 'sky'), may hold values from -0.1875 to 0.1875
- target: float32 [4, 8, 576, 1024], P('batch', 'sky'), may hold values from -2 to 2
- images: float32 [4, 8, 16, 80], P('batch', 'sky'), may hold values from -6 to 6
- layer_mask: int32 [4, 8, 16], P('batch', 'sky'), may hold values 0 or 1
- pair_list: int32 [4, 8, 9], P('batch', 'sky'), may hold values from 0 to 11, as said below
- ridge_weight: float32 [4, 8], P('batch', 'sky'), may hold values from 0.2 to 1
Outputs:
- transfer: float32 [4, 8, 720, 576], P('batch', 'sky')
- final_image: float32 [16, 96, 192], P(None, 'batch', 'sky')
Inputs may be any that keep to these rules, and one draw needn't show every extreme that they name: `pair_list`: the 9 entries of each output stamp are distinct candidate numbers.
All inputs are finite; a program needn't handle non-finite values. No bound on the sum of `layer_mask` on one device may be relied on, other than what follows from the above.
Results may differ from a plain program's by a relative error of at most 0.0003.
Values sent between devices are 32-bit elements; how exact they have to be, the bound alone decides.
No kernel may reach another device: no remote copies, remote signals or barrier semaphores. Data moves between devices by JAX's collectives and lax.ppermute only.
A program may use at most 128 MiB of HBM per device.

v0:
```python
import jax
import jax.numpy as jnp
import numpy as np
from jax import lax
from jax.sharding import PartitionSpec as P

NPIX = 80
FEAT = 1024
SIDE = 24
LAYERS = 16
NSEL = 9
FADE = 4
ORDER = 720
NOUT_PIX = 576


precise = lax.Precision.HIGHEST


def padded_2(cells, sides, width):
    for axis, dim in sides:
        count = lax.axis_size(axis)
        ends = count - 1
        head = lax.slice_in_dim(cells, 0, width, axis=dim)
        tail = lax.slice_in_dim(cells, cells.shape[dim] - width, cells.shape[dim], axis=dim)
        cells = jnp.concatenate(
            [
                lax.ppermute(tail, axis, [(i, (i + 1) % count) for i in range(ends)]),
                cells,
                lax.ppermute(head, axis, [((i + 1) % count, i) for i in range(ends)]),
            ],
            axis=dim,
        )
    return cells


def plan_blocks(batch_count):
    same_tile = [
        ((first_batch, 1), (second_batch, 1))
        for first_batch in range(batch_count)
        for second_batch in range(first_batch, batch_count)
    ]
    listing = []
    for row_tile in range(3):
        for col_tile in range(row_tile, 3):
            for first_batch in range(batch_count):
                for second_batch in range(batch_count):
                    if row_tile < col_tile or first_batch <= second_batch:
                        listing.append(((first_batch, row_tile), (second_batch, col_tile)))
    position = {}
    for number, entry in enumerate(listing):
        position[entry] = number
    padded = listing + [listing[0]] * (-len(listing) % batch_count)
    neighbour_count = len(same_tile) + batch_count * batch_count
    candidates = 3 * batch_count
    table_index = np.zeros((candidates, candidates), np.int32)
    table_flip = np.zeros((candidates, candidates), np.bool_)
    for row_cand in range(candidates):
        for col_cand in range(candidates):
            row_batch, row_tile = divmod(row_cand, 3)
            col_batch, col_tile = divmod(col_cand, 3)
            if row_tile < col_tile or (row_tile == col_tile and row_batch <= col_batch):
                table_index[row_cand, col_cand] = position[
                    (row_batch, row_tile), (col_batch, col_tile)
                ]
            else:
                table_index[row_cand, col_cand] = position[
                    (col_batch, col_tile), (row_batch, row_tile)
                ]
                table_flip[row_cand, col_cand] = True
    firsts = np.array([3 * entry[0][0] + entry[0][1] for entry in padded], np.int32)
    seconds = np.array([3 * entry[1][0] + entry[1][1] for entry in padded], np.int32)
    return (firsts, seconds, table_index, table_flip, neighbour_count, len(same_tile))


def local(features, target, images, layer_mask, pair_list, ridge_weight):
    batch_count = lax.axis_size("batch")
    candidates = 3 * batch_count
    masked = images * layer_mask[..., None].astype(jnp.float32)
    packed = jnp.concatenate(
        [features.reshape(1, 1, NPIX * FEAT), masked.reshape(1, 1, LAYERS * NPIX)], axis=2
    )
    tile_data = lax.all_gather(packed, "batch", axis=0, tiled=True)
    window = padded_2(tile_data, (("sky", 1),), 1)
    window = window.reshape(candidates, NPIX * FEAT + LAYERS * NPIX)
    window_feat = window[:, : NPIX * FEAT].reshape(candidates, NPIX, FEAT)
    window_image = window[:, NPIX * FEAT :].reshape(candidates, LAYERS, NPIX)
    firsts, seconds, table_index, table_flip, neighbour_count, same_count = plan_blocks(batch_count)
    per_device = firsts.shape[0] // batch_count
    device_pos = lax.axis_index("batch")
    first_rows = lax.dynamic_slice_in_dim(jnp.asarray(firsts), device_pos * per_device, per_device)
    second_rows = lax.dynamic_slice_in_dim(
        jnp.asarray(seconds), device_pos * per_device, per_device
    )
    first_feat = jnp.take(window_feat, first_rows, axis=0)
    second_feat = jnp.take(window_feat, second_rows, axis=0)
    formed = jnp.einsum("kif,kjf->kij", first_feat, second_feat, precision=precise)
    tile_blocks = lax.all_gather(formed, "batch", axis=0, tiled=True)
    chosen = pair_list.reshape(NSEL)
    picked_index = jnp.asarray(table_index)[chosen[:, None], chosen[None, :]]
    picked_flip = jnp.asarray(table_flip)[chosen[:, None], chosen[None, :]]
    picked = jnp.take(tile_blocks, picked_index.reshape(NSEL * NSEL), axis=0).reshape(
        NSEL, NSEL, NPIX, NPIX
    )
    picked = jnp.where(picked_flip[:, :, None, None], jnp.swapaxes(picked, 2, 3), picked)
    system = picked.transpose(0, 2, 1, 3).reshape(ORDER, ORDER)
    system = system + ridge_weight.reshape(()) * jnp.eye(ORDER, dtype=jnp.float32)
    chosen_feat = jnp.take(window_feat, chosen, axis=0).reshape(ORDER, FEAT)
    chosen_image = jnp.take(window_image, chosen, axis=0)
    right_sides = jnp.einsum(
        "if,jf->ij", chosen_feat, target.reshape(NOUT_PIX, FEAT), precision=precise
    )
    factor = jnp.linalg.cholesky(system)
    midway = lax.linalg.triangular_solve(factor, right_sides, left_side=True, lower=True)
    transfer = lax.linalg.triangular_solve(
        factor, midway, left_side=True, lower=True, transpose_a=True
    )
    coadded = jnp.einsum(
        "kio,kli->lo", transfer.reshape(NSEL, NPIX, NOUT_PIX), chosen_image, precision=precise
    )
    coadded = coadded.reshape(LAYERS, SIDE, SIDE)
    extended = padded_2(coadded, (("sky", 2), ("batch", 1)), FADE)
    east_strip = extended[:, FADE : FADE + SIDE, FADE + SIDE :]
    west_strip = extended[:, FADE : FADE + SIDE, :FADE]
    north_strip = extended[:, :FADE, FADE : FADE + SIDE]
    south_strip = extended[:, FADE + SIDE :, FADE : FADE + SIDE]
    fade_ramp = (jnp.arange(FADE, dtype=jnp.float32) + 1.0) / (FADE + 1.0)
    blended = coadded
    blended = blended.at[:, :, SIDE - FADE :].add(fade_ramp * east_strip)
    blended = blended.at[:, :, :FADE].add(fade_ramp[::-1] * west_strip)
    blended = blended.at[:, SIDE - FADE :, :].add(fade_ramp[:, None] * south_strip)
    blended = blended.at[:, :FADE, :].add(fade_ramp[::-1][:, None] * north_strip)
    return (transfer.reshape(1, 1, ORDER, NOUT_PIX), blended)


def solution(mesh):
    in_specs = (
        P("batch", "sky", None, None),
        P("batch", "sky", None, None),
        P("batch", "sky", None, None),
        P("batch", "sky", None),
        P("batch", "sky", None),
        P("batch", "sky"),
    )
    out_specs = (P("batch", "sky", None, None), P(None, "batch", "sky"))
    return jax.shard_map(local, mesh=mesh, in_specs=in_specs, out_specs=out_specs, check_vma=False)
```

profile of v0, /device:TPU:9, one launch (start us, length us, event | category | flops | bytes accessed | tf_op | source)
XLA Modules:
  0.0 494.1 jit_solution(13829790112872097387)
XLA Ops:
  11.3 19.9 %all-gather.3.cloned.1.call-done = f32[4,1,83200]{2,1,0:T(1,128)} async-done(((f32[1,1,83200]{2,1,0:T(1,128)}), f32[4,1,83200]{2,1,0:T(1,128)}) %all-gather.3.cloned.1.call-update) | async-done | bytes 1331216 | tf_op jit(solution)/shard_map/all_gather | solution.py:83
  31.3 3.1 collective-permute-start.1
  34.3 2.2 collective-permute-start
  37.3 55.1 %collective-permute-done.1 = f32[4,1,83200]{2,1,0:T(1,128)} collective-permute-done((f32[4,1,83200]{2,1,0:T(1,128)}, f32[4,1,83200]{2,1,0:T(1,128)}, u32[]{:S(2)}, u32[]{:S(2)}) %collective-permute-start.1) | collective-permute-done | bytes 1331232 | tf_op jit(solution)/shard_map/ppermute | solution.py:30
  93.0 7.1 %pad_maximum_fusion = f32[4,3,83200]{2,1,0:T(4,128)} fusion(f32[4,1,83200]{2,1,0:T(1,128)} %collective-permute-done.1, f32[4,1,83200]{2,1,0:T(1,128)} %all-gather.3.cloned.1.call-done, f32[4,1,83200]{2,1,0:T(1,128)} %collective-permute-done), kind=kLoop, calls=%fused_computation.16 | loop fusion | flops 1996800 | bytes 7987200 | tf_op jit(solution)/shard_map/concatenate | solution.py:26
  100.1 6.7 %reshape.391 = f32[12,83200]{1,0:T(8,128)} reshape(f32[4,3,83200]{2,1,0:T(4,128)} %pad_maximum_fusion) | data formatting | bytes 7987200 | tf_op jit(solution)/shard_map/reshape | solution.py:85
  106.9 2.5 slice-done
  109.4 3.0 copy.48
  112.4 2.4 slice.364
  114.8 5.8 %gather_fusion.6 = f32[20,80,1024]{2,1,0:T(8,128)} fusion(f32[12,80,1024]{2,1,0:T(8,128)} %slice.364, s32[1024]{0:T(1024)S(1)} %pad_clamp_fusion.2), kind=kCustom, calls=%fused_computation.1.clone | custom fusion | bytes 13107280 | tf_op jit(solution)/shard_map/jit(_take)/gather | solution.py:96
  120.7 5.8 %gather_fusion.5 = f32[20,80,1024]{2,1,0:T(8,128)} fusion(f32[12,80,1024]{2,1,0:T(8,128)} %slice.364, s32[1024]{0:T(1024)S(1)} %pad_clamp_fusion.3), kind=kCustom, calls=%fused_computation.clone | custom fusion | bytes 13107280 | tf_op jit(solution)/shard_map/jit(_take)/gather | solution.py:95
  126.5 12.6 %fusion = f32[20,80,80]{2,1,0:T(8,128)} fusion(f32[20,80,1024]{2,1,0:T(8,128)} %gather_fusion.6, f32[20,80,1024]{2,1,0:T(8,128)} %gather_fusion.5, pred[20]{0:T(512)(128)(4,1)S(1)} %get-tuple-element.75, pred[20]{0:T(512)(128)(4,1)S(1)} %get-tuple-element.115), kind=kOutput, calls=%fused_computation.9 | convolution fusion | flops 1576140800 | bytes 13619240 | tf_op jit(solution)/shard_map/kif,kjf->kij/dot_general | solution.py:97
  140.0 1.7 gather_fusion.1
  141.7 2.0 gather_fusion
  144.1 4.6 gather_fusion.3
  149.3 2.2 broadcast_select_fusion
  151.5 7.0 %fusion.9 = f32[720,576]{0,1:T(8,128)} fusion(f32[720,1024]{1,0:T(8,128)S(1)} %bitcast.156, f32[1,1,576,1024]{3,2,1,0:T(8,128)S(1)} %copy-done), kind=kOutput, calls=%fused_computation.21 | convolution fusion | flops 5096079360 | bytes 6967296 | tf_op jit(solution)/shard_map/if,jf->ij/dot_general | solution.py:110
  158.5 10.3 %all-gather.5.cloned.1.call-done = f32[80,80,80]{2,1,0:T(8,128)} async-done(((f32[20,80,80]{2,1,0:T(8,128)}), f32[80,80,80]{2,1,0:T(8,128)}) %all-gather.5.cloned.1.call-update) | async-done | bytes 2048016 | tf_op jit(solution)/shard_map/all_gather | solution.py:98
  168.8 4.4 gather_fusion.2
  173.3 5.9 %fusion.4 = f32[9,9,80,80]{2,1,3,0:T(8,128)} fusion(f32[9,9,80,80]{3,2,1,0:T(8,128)} %bitcast.152, pred[9,9]{1,0:T(8,128)(4,1)S(1)} %compare_and_fusion), kind=kLoop, calls=%fused_computation.14 | loop fusion | flops 518400 | bytes 4147281 | tf_op jit(solution)/shard_map/transpose | solution.py:105
  179.2 8.0 %copy.34 = f32[9,9,80,80]{3,1,2,0:T(8,128)} copy(f32[9,9,80,80]{2,1,3,0:T(8,128)} %fusion.4) | data formatting | bytes 4147200 | tf_op jit(solution)/shard_map/transpose | solution.py:105
  187.2 8.0 %fusion.5 = f32[9,80,9,80]{3,2,1,0:T(8,128)} fusion(f32[9,9,80,80]{3,1,2,0:T(8,128)} %copy.34, f32[9,9,80,80]{3,2,1,0:T(8,128)} %bitcast.153, pred[9,9]{1,0:T(8,128)(4,1)S(1)} %compare_and_fusion, pred[9,9]{1,0:T(8,128)(4,1)S(1)} %reshape.440), kind=kLoop, calls=%fused_computation.15 | loop fusion | flops 1036800 | bytes 6220962 | tf_op jit(solution)/shard_map/transpose | solution.py:106
  195.1 4.0 reshape.394
  199.2 1.5 select_add_fusion
  200.7 3.1 copy.35
  203.8 1.9 fusion.11
  207.1 11.7 %cholesky.165 = f32[128,128]{1,0:T(8,128)S(1)} custom-call(f32[128,128]{1,0:T(8,128)S(1)} %cholesky.427), custom_call_target="Cholesky" | custom-call | tf_op jit(solution)/shard_map/jit(cholesky)/cholesky | solution.py:113
  219.5 9.8 %custom-call.48 = f32[1,128,128]{1,2,0:T(8,128)S(1)} custom-call(f32[1,128,128]{2,1,0:T(8,128)S(1)} %get-tuple-element.96), custom_call_target="InvertDiagBlocksLowerTriangular" | custom-call | tf_op jit(solution)/shard_map/jit(cholesky)/cholesky | solution.py:113
  232.2 11.7 %cholesky.188 = f32[128,128]{1,0:T(8,128)S(1)} custom-call(f32[128,128]{1,0:T(8,128)S(1)} %cholesky.431), custom_call_target="Cholesky" | custom-call | tf_op jit(solution)/shard_map/jit(cholesky)/cholesky | solution.py:113
  244.6 10.2 %custom-call.49 = f32[1,128,128]{1,2,0:T(8,128)S(1)} custom-call(f32[1,128,128]{2,1,0:T(8,128)S(1)} %get-tuple-element.93), custom_call_target="InvertDiagBlocksLowerTriangular" | custom-call | tf_op jit(solution)/shard_map/jit(cholesky)/cholesky | solution.py:113
  256.6 11.7 %cholesky.354 = f32[128,128]{1,0:T(8,128)S(1)} custom-call(f32[128,128]{1,0:T(8,128)S(1)} %cholesky.436), custom_call_target="Cholesky" | custom-call | tf_op jit(solution)/shard_map/jit(cholesky)/cholesky | solution.py:113
  269.0 9.8 %custom-call.50 = f32[1,128,128]{1,2,0:T(8,128)S(1)} custom-call(f32[1,128,128]{2,1,0:T(8,128)S(1)} %get-tuple-element.90), custom_call_target="InvertDiagBlocksLowerTriangular" | custom-call | tf_op jit(solution)/shard_map/jit(cholesky)/cholesky | solution.py:113
  279.1 1.5 convolution_subtract_fusion.10
  280.7 11.9 %cholesky.373 = f32[128,128]{1,0:T(8,128)S(1)} custom-call(f32[128,128]{1,0:T(8,128)S(1)} %cholesky.441), custom_call_target="Cholesky" | custom-call | tf_op jit(solution)/shard_map/jit(cholesky)/cholesky | solution.py:113
  293.3 9.8 %custom-call.51 = f32[1,128,128]{1,2,0:T(8,128)S(1)} custom-call(f32[1,128,128]{2,1,0:T(8,128)S(1)} %get-tuple-element.87), custom_call_target="InvertDiagBlocksLowerTriangular" | custom-call | tf_op jit(solution)/shard_map/jit(cholesky)/cholesky | solution.py:113
  304.8 11.7 %cholesky.392 = f32[128,128]{1,0:T(8,128)S(1)} custom-call(f32[128,128]{1,0:T(8,128)S(1)} %cholesky.446), custom_call_target="Cholesky" | custom-call | tf_op jit(solution)/shard_map/jit(cholesky)/cholesky | solution.py:113
  317.1 9.8 %custom-call.52 = f32[1,128,128]{1,2,0:T(8,128)S(1)} custom-call(f32[1,128,128]{2,1,0:T(8,128)S(1)} %get-tuple-element.84), custom_call_target="InvertDiagBlocksLowerTriangular" | custom-call | tf_op jit(solution)/shard_map/jit(cholesky)/cholesky | solution.py:113
  328.3 7.3 %cholesky.413 = f32[80,80]{1,0:T(8,128)S(1)} custom-call(f32[80,80]{1,0:T(8,128)S(1)} %convolution_subtract_fusion.12), custom_call_target="Cholesky" | custom-call | tf_op jit(solution)/shard_map/jit(cholesky)/cholesky | solution.py:113
  341.6 14.1 %while.5 = (s32[]{:T(128)}, f32[720,720]{1,0:T(8,128)}, s32[5,2]{0,1:T(2,128)S(1)}, f32[5,128,128]{2,1,0:T(8,128)S(1)}, s32[]{:T(128)}) while((s32[]{:T(128)}, f32[720,720]{1,0:T(8,128)}, s32[5,2]{0,1:T(2,128)S(1)}, f32[5,128,128]{2,1,0:T(8,128)S(1)}, s32[]{:T(128)}) %tuple.75), condition=%wide.while_cond.4, body=%wide.while_body.4.sunk | while | flops 2 | bytes 131189 | solution.py:115
  342.2 2.2 bitcast_dynamic-update-slice_fusion.2
  345.1 2.2 bitcast_dynamic-update-slice_fusion.2
  347.9 2.2 bitcast_dynamic-update-slice_fusion.2
  350.7 2.2 bitcast_dynamic-update-slice_fusion.2
  353.5 2.2 bitcast_dynamic-update-slice_fusion.2
  355.9 59.2 %custom-call.53 = f32[6,128,128]{1,2,0:T(8,128)S(1)} custom-call(f32[6,128,128]{2,1,0:T(8,128)S(1)} %pad_maximum_fusion.1), custom_call_target="InvertDiagBlocksLowerTriangular" | custom-call | tf_op jit(solution)/shard_map/triangular_solve | solution.py:115
  418.1 1.5 convolution_subtract_fusion.5
  420.0 1.9 convolution_subtract_fusion.8
  422.3 2.0 fusion.31
  425.4 2.3 convolution_subtract_fusion.4
  428.6 1.7 convolution_subtract_fusion.3
  430.7 1.5 convolution_subtract_fusion.2
  432.7 1.8 convolution_subtract_fusion.7
  434.9 2.0 fusion.28
  437.4 2.5 convolution_subtract_fusion.1
  444.7 2.1 copy.42
  446.8 2.2 copy.43
  449.0 9.3 %convolution_bitcast_fusion = f32[16,24,24]{2,0,1:T(8,128)S(1)} fusion(f32[24,24,80,9]{2,1,0,3:T(8,128)} %bitcast.157, f32[9,16,80]{2,1,0:T(8,128)S(1)} %gather_fusion.4, pred[9]{0:T(512)(128)(4,1)S(1)} %compare_and_fusion.3), kind=kOutput, calls=%fused_computation.60 | convolution fusion | flops 79637760 | bytes 1741833 | tf_op jit(solution)/shard_map/kio,kli->lo/dot_general | solution.py:118
  458.4 3.1 collective-permute-start.2
  461.6 4.9 collective-permute-done.2
  466.6 4.0 collective-permute-start.3
  470.6 4.1 collective-permute-done.3
  474.8 3.7 scatter-add.14
  478.5 3.9 collective-permute-start.4
  482.9 2.1 collective-permute-start.5
  (126 shorter events, 39.6 us)
Async XLA Ops:
  7.2 144.3 %copy-start = (f32[1,1,576,1024]{3,2,1,0:T(8,128)S(1)}, f32[1,1,576,1024]{3,2,1,0:T(8,128)}, u32[]{:S(2)}) copy-start(f32[1,1,576,1024]{3,2,1,0:T(8,128)} %param.21) | copy-start | bytes 7077892
  7.2 24.1 %all-gather.3.cloned.1.call-start = ((), (), s32[]{:S(2)}) async-start(), calls=%async_computation | async-start | bytes 1664000 | tf_op jit(solution)/shard_map/all_gather | solution.py:83
  11.3 157.5 %all-gather.5.cloned.1.call-start = ((), (), s32[]{:S(2)}) async-start(), calls=%async_computation.1 | async-start | bytes 4096000 | tf_op jit(solution)/shard_map/all_gather | solution.py:98
  31.3 61.2 %collective-permute-start.1 = (f32[4,1,83200]{2,1,0:T(1,128)}, f32[4,1,83200]{2,1,0:T(1,128)}, u32[]{:S(2)}, u32[]{:S(2)}) collective-permute-start(f32[4,1,83200]{2,1,0:T(1,128)} %all-gather.3.cloned.1.call-done), channel_id=1, source_target_pairs={{4,0},{8,4},{12,8},{16,12},{20,16},{24,20},{28,24},{5,1},{9,5},{13... | collective-permute-start | bytes 3993608 | tf_op jit(solution)/shard_map/ppermute | solution.py:30
  34.3 58.7 %collective-permute-start = (f32[4,1,83200]{2,1,0:T(1,128)}, f32[4,1,83200]{2,1,0:T(1,128)}, u32[]{:S(2)}, u32[]{:S(2)}) collective-permute-start(f32[4,1,83200]{2,1,0:T(1,128)} %all-gather.3.cloned.1.call-done), channel_id=1, source_target_pairs={{0,4},{4,8},{8,12},{12,16},{16,20},{20,24},{24,28},{1,5},{5,9},{9,... | collective-permute-start | bytes 3993608 | tf_op jit(solution)/shard_map/ppermute | solution.py:28
  106.9 2.5 slice-start
  126.5 13.3 %copy-start.7 = (s32[1,1,9]{2,1,0:T(1,128)S(1)}, s32[1,1,9]{2,1,0:T(1,128)}, u32[]{:S(2)}) copy-start(s32[1,1,9]{2,1,0:T(1,128)} %param.24) | copy-start | bytes 112
  139.1 0.9 copy-start.2
  140.0 1.7 copy-start.3
  141.7 2.3 slice-start.1
  205.7 1.4 copy-start.6
  340.3 1.4 copy-start.4
  340.3 76.1 %copy-start.5 = (f32[720,576]{0,1:T(8,128)S(1)}, f32[720,576]{0,1:T(8,128)}, u32[]{:S(2)}) copy-start(f32[720,576]{0,1:T(8,128)} %fusion.9) | copy-start | bytes 4976644
  449.0 37.8 %copy-start.1 = (f32[1,1,576,1024]{3,2,1,0:T(8,128)S(1)}, f32[1,1,576,1024]{3,2,1,0:T(8,128)}, u32[]{:S(2)}) copy-start(f32[1,1,576,1024]{3,2,1,0:T(8,128)} %param.21) | copy-start | bytes 7077892
  458.4 8.1 %collective-permute-start.2 = (f32[16,24,4]{2,0,1:T(8,128)S(1)}, f32[16,24,4]{2,0,1:T(8,128)S(1)}, u32[]{:S(2)}, u32[]{:S(2)}) collective-permute-start(f32[16,24,4]{2,0,1:T(8,128)S(1)} %bitcast.159), channel_id=1, source_target_pairs={{4,0},{8,4},{12,8},{16,12},{20,16},{24,20},{28,24},{5,1},{9,5},{13... | collective-permute-start | bytes 18440 | tf_op jit(solution)/shard_map/ppermute | solution.py:30
  466.6 8.1 %collective-permute-start.3 = (f32[16,24,4]{2,0,1:T(8,128)S(1)}, f32[16,24,4]{2,0,1:T(8,128)S(1)}, u32[]{:S(2)}, u32[]{:S(2)}) collective-permute-start(f32[16,24,4]{2,0,1:T(8,128)S(1)} %get-tuple-element.81), channel_id=1, source_target_pairs={{0,4},{4,8},{8,12},{12,16},{16,20},{20,24},{24,28},{1,5},{5,9},{9,... | collective-permute-start | bytes 18440 | tf_op jit(solution)/shard_map/ppermute | solution.py:28
  478.5 6.5 %collective-permute-start.4 = (f32[16,4,32]{2,0,1:T(8,128)S(1)}, f32[16,4,32]{2,0,1:T(8,128)S(1)}, u32[]{:S(2)}, u32[]{:S(2)}) collective-permute-start(f32[16,4,32]{2,0,1:T(8,128)S(1)} %get-tuple-element.80), channel_id=1, source_target_pairs={{1,0},{2,1},{3,2},{5,4},{6,5},{7,6},{9,8},{10,9},{11,10},{13,12},{... | collective-permute-start | bytes 24584 | tf_op jit(solution)/shard_map/ppermute | solution.py:30
  482.9 3.1 collective-permute-start.5
Sparse Core Ops, SparseCore 0:
  11.4 19.8 all-gather.2
  139.2 29.5 all-gather.4
where the time goes:
time: 499 us; the launch traced here: 494 us
  other arithmetic  210 us (42%)
  waiting for transfers between devices  95.8 us (19%)
  local copies, waits for them, and re-layouts  86.7 us (17%)
  matrix products  63.9 us (13%)
  between operations  19.7 us (4%)
  starting transfers between devices  18.5 us (4%)
    another operation x23, other arithmetic, local(): factor = jnp.linalg.cholesky(system)  120 us
    ppermute x3, waiting for transfers between devices, padded_2(): lax.ppermute(head, axis, [((i + 1) % count, i) for i in range(ends)])  60 us
    another operation x7, other arithmetic, local(): lax.linalg.triangular_solve(factor, midway, left_side=True, lower=True, t...  59.5 us
    all_gather x1, waiting for transfers between devices, local(): tile_data = lax.all_gather(packed, 'batch', axis=0, tiled=True)  19.9 us
    another operation x16, local copies, waits for them, and re-layouts  14.1 us
    another operation x11, matrix products, local(): lax.linalg.triangular_solve(factor, right_sides, left_side=True, lower=True)  13 us
    dot_general x1, matrix products, local(): jnp.einsum('kif,kjf->kij', first_feat, second_feat, precision=precise)  12.6 us
    another operation x11, matrix products, local(): lax.linalg.triangular_solve(factor, midway, left_side=True, lower=True, t...  12.6 us
  transfers between devices with their start and end apart: 8, of which 7 were waited for; matrix products, arithmetic and copies ran while one was open for 4% of the time, Pallas kernels for 0%

commit v1 on v0

v1 whole, which is shorter than its diff:
```python
import functools
import jax
import jax.numpy as jnp
from jax import lax
from jax.experimental import pallas as pl
from jax.experimental.pallas import tpu as pltpu
from jax.sharding import PartitionSpec as P

f32 = jnp.float32
bf16 = jnp.bfloat16
LANE = 128
SUB = 8
FADE = 4


def split2(x):
    hi = x.astype(bf16)
    lo = (x - hi.astype(f32)).astype(bf16)
    return hi, lo


def dot(a, b, tb=False):
    dims = (((1,), (1 if tb else 0,)), ((), ()))
    return lax.dot_general(a, b, dims, preferred_element_type=f32)


def dot3(ah, al, bh, bl, tb=False):
    return dot(ah, bh, tb) + (dot(ah, bl, tb) + dot(al, bh, tb))


def panel_sweep(rows, q, sub, lane):
    base = q * SUB
    p = rows[q]
    cols = [jnp.broadcast_to(p[:, base + k : base + k + 1], (SUB, LANE)) for k in range(SUB)]
    inside = (lane >= base) & (lane < base + SUB)
    w = jnp.where(inside, jnp.where(lane - base == sub, 1.0, 0.0).astype(f32), p)
    for k in range(SUB):
        here = sub == k
        inv = 1.0 / jnp.broadcast_to(cols[k][k : k + 1, :], (SUB, LANE))
        h = jnp.where(here, -1.0, cols[k])
        for m in range(k + 1, SUB):
            r = jnp.broadcast_to(cols[m][k : k + 1, :], (SUB, LANE))
            cols[m] = jnp.where(here, 0.0, cols[m]) - (h * r) * inv
        r = jnp.broadcast_to(w[k : k + 1, :], (SUB, LANE))
        w = jnp.where(here, 0.0, w) - (h * r) * inv
    wk = [jnp.broadcast_to(w[k : k + 1, :], (SUB, LANE)) for k in range(SUB)]
    out = []
    count = len(rows)
    order = [(q + 1 + i) % count for i in range(count)]
    res = [None] * count
    for g in order:
        if g == q:
            res[g] = w
            continue
        a = rows[g]
        acc = [jnp.where(inside, 0.0, a), None]
        for k in range(SUB):
            t = jnp.broadcast_to(a[:, base + k : base + k + 1], (SUB, LANE)) * wk[k]
            s = k % 2
            acc[s] = (acc[s] - t) if acc[s] is not None else -t
        res[g] = acc[0] + acc[1]
    return res


def solve_kernel(sel_ref, ridge_ref, win_ref, img_ref, tgt_ref, out_ref, co_ref,
                 fsel, fh, fl, th, tl, s_ref, r_ref, sems, *, npix, nsel, feat, nout):
    order = npix * nsel
    nblk = -(-order // LANE)
    padded = nblk * LANE
    copies = []
    for k in range(nsel):
        cp = pltpu.make_async_copy(win_ref.at[sel_ref[k], pl.ds(0, npix)], fsel.at[pl.ds(k * npix, npix)], sems.at[k])
        cp.start()
        copies.append(cp)
    t = tgt_ref[...]
    hi, lo = split2(t)
    th[...] = hi
    tl[...] = lo
    if padded > order:
        fh[order:padded, :] = jnp.zeros((padded - order, feat), bf16)
        fl[order:padded, :] = jnp.zeros((padded - order, feat), bf16)
    for k in range(nsel):
        copies[k].wait()
        hi, lo = split2(fsel[k * npix : (k + 1) * npix, :])
        fh[k * npix : (k + 1) * npix, :] = hi
        fl[k * npix : (k + 1) * npix, :] = lo
    ridge = ridge_ref[0]
    sub = lax.broadcasted_iota(jnp.int32, (SUB, LANE), 0)
    lane = lax.broadcasted_iota(jnp.int32, (SUB, LANE), 1)

    def gram(c, width=1):
        lo_, hi_ = c * LANE, (c + width) * LANE
        g = dot3(fh[...], fl[...], fh[lo_:hi_, :], fl[lo_:hi_, :], True)
        for w in range(width):
            s_ref[c + w] = g[:, w * LANE : (w + 1) * LANE]

    def rhs():
        r_ref[...] = dot3(fh[...], fl[...], th[...], tl[...], True)

    def load_diag(c):
        top = c * LANE
        rows_here = min(order - top, LANE) // SUB
        rows = []
        for g in range(rows_here):
            a = s_ref[c, top + g * SUB : top + (g + 1) * SUB, :]
            rows.append(a + jnp.where(lane == sub + g * SUB, ridge, 0.0))
        return rows

    def apply(c, coef_h, coef_l, dh, dl, j, is_rhs=False):
        top = j * LANE
        size = min(order - top, LANE)
        if is_rhs:
            block = r_ref[top : top + size, :]
        else:
            block = s_ref[c, top : top + size, :]
        bh, bl = split2(block)
        w = dot3(dh, dl, bh, bl)
        wh, wl = split2(w)
        upd = dot3(coef_h, coef_l, wh, wl)
        if is_rhs:
            r_ref[...] = r_ref[...] - upd
            r_ref[top : top + size, :] = w
        else:
            s_ref[c] = s_ref[c] - upd
            s_ref[c, top : top + size, :] = w

    gram(0)
    work = []
    for c in range(1, nblk, 2):
        work.append(functools.partial(gram, c, min(2, nblk - c)))
    work.append(rhs)
    for j in range(nblk):
        rows = load_diag(j)
        count = len(rows)
        for q in range(count):
            rows = panel_sweep(rows, q, sub, lane)
            take = -(-len(work) // (count - q))
            for _ in range(take):
                work.pop(0)()
        while work:
            work.pop(0)()
        size = count * SUB
        d = jnp.concatenate(rows, axis=0)[:, :size] if size < LANE else jnp.concatenate(rows, axis=0)
        dh, dl = split2(d)
        coef = s_ref[j]
        if size < LANE:
            coef = coef[:, :size]
        ch, cl = split2(coef)
        if j + 1 < nblk:
            apply(j + 1, ch, cl, dh, dl, j)
        for c in range(j + 2, nblk):
            work.append(functools.partial(apply, c, ch, cl, dh, dl, j))
        work.append(functools.partial(apply, 0, ch, cl, dh, dl, j, True))
    while work:
        work.pop(0)()
    total = None
    for k in range(nsel):
        xh, xl = split2(r_ref[k * npix : (k + 1) * npix, :])
        ih, il = split2(img_ref[sel_ref[k]])
        part = dot3(ih, il, xh, xl)
        total = part if total is None else total + part
        out_ref[k * npix : (k + 1) * npix, :] = r_ref[k * npix : (k + 1) * npix, :]
    co_ref[...] = total


def solve(window, images, target, sel, ridge):
    npix, feat = images.shape[2], target.shape[1]
    nout = target.shape[0]
    nsel = sel.shape[0]
    order = npix * nsel
    nblk = -(-order // LANE)
    padded = nblk * LANE
    return pl.pallas_call(
        functools.partial(solve_kernel, npix=npix, nsel=nsel, feat=feat, nout=nout),
        out_shape=(
            jax.ShapeDtypeStruct((order, nout), f32),
            jax.ShapeDtypeStruct((images.shape[1], nout), f32),
        ),
        in_specs=[
            pl.BlockSpec(memory_space=pltpu.SMEM),
            pl.BlockSpec(memory_space=pltpu.SMEM),
            pl.BlockSpec(memory_space=pl.ANY),
            pl.BlockSpec(memory_space=pltpu.VMEM),
            pl.BlockSpec(memory_space=pltpu.VMEM),
        ],
        out_specs=(pl.BlockSpec(memory_space=pltpu.VMEM), pl.BlockSpec(memory_space=pltpu.VMEM)),
        scratch_shapes=[
            pltpu.VMEM((order, feat), f32),
            pltpu.VMEM((padded, feat), bf16),
            pltpu.VMEM((padded, feat), bf16),
            pltpu.VMEM((nout, feat), bf16),
            pltpu.VMEM((nout, feat), bf16),
            pltpu.VMEM((nblk, padded, LANE), f32),
            pltpu.VMEM((padded, nout), f32),
            pltpu.SemaphoreType.DMA((nsel,)),
        ],
        compiler_params=pltpu.CompilerParams(vmem_limit_bytes=60 << 20),
        name="solve",
    )(sel, ridge, window, images, target)


def swap(value, axis, bit):
    count = lax.axis_size(axis)
    return lax.ppermute(value, axis, [(i, i ^ bit) for i in range(count)])


def hop_two(value):
    count = lax.axis_size("sky")
    pairs = [(i, i + 2) for i in range(0, count - 2, 2)] + [(i, i - 2) for i in range(3, count, 2)]
    return lax.ppermute(value, "sky", pairs)


def gather_window(own):
    a1 = swap(own, "batch", 1)
    a2 = swap(own, "batch", 2)
    n0 = swap(own, "sky", 1)
    n2 = swap(n0, "batch", 2)
    d0 = hop_two(n0)
    d2 = swap(d0, "batch", 2)
    a3 = swap(a2, "batch", 1)
    n1 = swap(n0, "batch", 1)
    n3 = swap(n2, "batch", 1)
    d1 = swap(d0, "batch", 1)
    d3 = swap(d2, "batch", 1)
    return jnp.stack([own, a1, a2, a3, n0, n1, n2, n3, d0, d1, d2, d3])


def shift(value, axis, step):
    count = lax.axis_size(axis)
    return lax.ppermute(
        value, axis, [(i, i + step) for i in range(count) if 0 <= i + step < count]
    )


def local(features, target, images, layer_mask, pair_list, ridge_weight):
    npix, feat = features.shape[2:]
    layers = images.shape[2]
    nout = target.shape[2]
    side = int(round(nout**0.5))
    masked = (images * layer_mask[..., None].astype(f32)).reshape(layers, npix)
    extra = jnp.pad(masked.reshape(SUB, layers * npix // SUB), ((0, 0), (0, feat - layers * npix // SUB)))
    own = jnp.concatenate([features.reshape(npix, feat), extra], axis=0)
    window = gather_window(own)
    win_feat = window
    win_img = window[:, npix:, : layers * npix // SUB].reshape(-1, layers, npix)
    chosen = pair_list.reshape(-1)
    p, u = chosen // 3, chosen % 3
    odd = lax.axis_index("sky") % 2
    near = jnp.where(odd == 1, 0, 2)
    tile = jnp.where(u == 1, 0, jnp.where(u == near, 1, 2))
    slot = tile * 4 + (p ^ lax.axis_index("batch"))
    transfer, coadded = solve(win_feat, win_img, target.reshape(nout, feat), slot.astype(jnp.int32), ridge_weight.reshape(1))
    coadded = coadded.reshape(layers, side, side)
    east = shift(coadded[:, :, :FADE], "sky", -1)
    west = shift(coadded[:, :, side - FADE :], "sky", 1)
    south = shift(coadded[:, :FADE, :], "batch", -1)
    north = shift(coadded[:, side - FADE :, :], "batch", 1)
    ramp = (jnp.arange(FADE, dtype=f32) + 1.0) / (FADE + 1.0)
    back = ramp[::-1]
    rest = side - FADE
    blended = (
        coadded
        + jnp.pad(ramp * east, ((0, 0), (0, 0), (rest, 0)))
        + jnp.pad(back * west, ((0, 0), (0, 0), (0, rest)))
        + jnp.pad(ramp[:, None] * south, ((0, 0), (rest, 0), (0, 0)))
        + jnp.pad(back[:, None] * north, ((0, 0), (0, rest), (0, 0)))
    )
    return (transfer.reshape(1, 1, -1, nout), blended)


def solution(mesh):
    in_specs = (
        P("batch", "sky", None, None),
        P("batch", "sky", None, None),
        P("batch", "sky", None, None),
        P("batch", "sky", None),
        P("batch", "sky", None),
        P("batch", "sky"),
    )
    out_specs = (P("batch", "sky", None, None), P(None, "batch", "sky"))
    return jax.shard_map(local, mesh=mesh, in_specs=in_specs, out_specs=out_specs, check_vma=False)
```

time: 499 us -> 97.7 us (0.20)
  other arithmetic: 210 us -> 5.68 us
  local copies, waits for them, and re-layouts: 86.7 us -> 6.94 us
  waiting for transfers between devices: 95.8 us -> 22.9 us
  matrix products: 63.9 us -> 0 us
  Pallas kernels: 0 us -> 36.2 us
  between operations: 19.7 us -> 1.52 us
  starting transfers between devices: 18.5 us -> 24 us
    another operation x31 -> x0, other arithmetic: 179 us -> none  [the longest x23 120 us: local(): factor = jnp.linalg.cholesky(system)]
    ppermute x6 -> x15, waiting for transfers between devices: 65.5 us -> 22.9 us  [the longest x10 14.8 us: swap(): return lax.ppermute(value, axis, [(i, i ^ bit) for i in range(count)])]
    pallas_call x0 -> x1, Pallas kernels: none -> 36.2 us  [solve(): pl.pallas_call(functools.partial(solve_kernel, npix=npix, nsel=nsel, feat...]
    another operation x32 -> x0, matrix products: 34.9 us -> none  [the longest x11 13 us: local(): lax.linalg.triangular_solve(factor, right_sides, left_side=True, lower=True)]
    all_gather x2 -> x0, waiting for transfers between devices: 30.2 us -> none  [the longest x1 19.9 us: local(): tile_data = lax.all_gather(packed, 'batch', axis=0, tiled=True)]
    dot_general x3 -> x0, matrix products: 29 us -> none  [the longest x1 12.6 us: local(): jnp.einsum('kif,kjf->kij', first_feat, second_feat, precision=precise)]
    gather x9 -> x0, local copies, waits for them, and re-layouts: 25.1 us -> none  [the longest x1 5.82 us: local(): second_feat = jnp.take(window_feat, second_rows, axis=0)]
    another operation x28 -> x3, local copies, waits for them, and re-layouts: 17.2 us -> 0.19 us
  transfers between devices with their start and end apart: 8 -> 15, of which waited for: 7 -> 5; matrix products, arithmetic and copies ran while one was open for 4% -> 6% of each run, Pallas kernels for 0% -> 0%
where the time goes in v1:
time: 97.7 us; the launch traced here: 97.2 us
  Pallas kernels  36.2 us (37%)
  starting transfers between devices  24 us (25%)
  waiting for transfers between devices  22.9 us (23%)
  local copies, waits for them, and re-layouts  6.94 us (7%)
  other arithmetic  5.68 us (6%)
  between operations  1.52 us (2%)
    pallas_call x1, Pallas kernels, solve(): pl.pallas_call(functools.partial(solve_kernel, npix=npix, nsel=nsel, feat...  36.2 us
    ppermute x10, waiting for transfers between devices, swap(): return lax.ppermute(value, axis, [(i, i ^ bit) for i in range(count)])  14.8 us
    ppermute x4, starting transfers between devices, shift(): lax.ppermute(value, axis, [(i, i + step) for i in range(count) if 0 <= i...  12 us
    ppermute x10, starting transfers between devices, swap(): return lax.ppermute(value, axis, [(i, i ^ bit) for i in range(count)])  8.79 us
    ppermute x1, waiting for transfers between devices, hop_two(): return lax.ppermute(value, 'sky', pairs)  7.66 us
    unnamed x13, local copies, waits for them, and re-layouts  4.99 us
    ppermute x1, starting transfers between devices, hop_two(): return lax.ppermute(value, 'sky', pairs)  3.19 us
  transfers between devices with their start and end apart: 15, of which 5 were waited for; matrix products, arithmetic and copies ran while one was open for 6% of the time, Pallas kernels for 0%

profile of v1, /device:TPU:9, one launch (start us, length us, event | category | flops | bytes accessed | tf_op | source)
XLA Modules:
  0.0 97.2 jit_solution(14509355849953116223)
XLA Ops:
  0.6 0.7 convert_bitcast_fusion
  1.3 0.8 broadcast_multiply_fusion.4
  2.1 0.1 reshape_reshape.3
  2.1 1.0 %select_maximum_fusion = f32[88,1024]{1,0:T(8,128)S(1)} fusion(f32[8,160]{1,0:T(8,128)S(1)} %reshape_reshape.3, f32[80,1024]{1,0:T(8,128)} %bitcast.50), kind=kLoop, calls=%fused_computation | loop fusion | flops 270336 | bytes 693248 | tf_op jit(solution)/shard_map/concatenate | solution.py:242
  3.1 0.7 collective-permute-start
  3.9 1.2 %collective-permute-start.1 = (f32[88,1024]{1,0:T(8,128)S(1)}, f32[88,1024]{1,0:T(8,128)S(1)}, u32[]{:S(2)}, u32[]{:S(2)}) collective-permute-start(f32[88,1024]{1,0:T(8,128)S(1)} %select_maximum_fusion), channel_id=1, source_target_pairs={{0,2},{1,3},{2,0},{3,1},{4,6},{5,7},{6,4},{7,5},{8,10},{9,11},{10,... | collective-permute-start | bytes 1081352 | tf_op jit(solution)/shard_map/ppermute | solution.py:204
  5.1 1.2 %collective-permute-start.3 = (f32[88,1024]{1,0:T(8,128)S(1)}, f32[88,1024]{1,0:T(8,128)S(1)}, u32[]{:S(2)}, u32[]{:S(2)}) collective-permute-start(f32[88,1024]{1,0:T(8,128)S(1)} %select_maximum_fusion), channel_id=1, source_target_pairs={{0,4},{4,0},{8,12},{12,8},{16,20},{20,16},{24,28},{28,24},{1,5},{5... | collective-permute-start | bytes 1081352 | tf_op jit(solution)/shard_map/ppermute | solution.py:204
  6.3 0.1 reverse.4
  7.1 1.0 %bitcast_dynamic-update-slice_fusion.11 = f32[12,88,1024]{2,1,0:T(8,128)S(1)} fusion(f32[8,160]{1,0:T(8,128)S(1)} %reshape_reshape.3, f32[80,1024]{1,0:T(8,128)} %bitcast.51), kind=kLoop, calls=%fused_computation.13 | loop fusion | flops 270335 | bytes 693248
  8.1 1.3 %fusion.2.sel_ref = s32[9]{0:T(128)} fusion(s32[1,1,9]{2,1,0:T(1,128)} %param.10, s32[]{:T(128)S(6)} %axis_index.25, s32[]{:T(128)S(6)} %select_n.32), kind=kLoop, calls=%fused_computation.26 | loop fusion | flops 171 | bytes 80 | tf_op jit(solution)/shard_map/add | solution.py:251
  9.4 5.3 %collective-permute-done.3 = f32[88,1024]{1,0:T(8,128)S(1)} collective-permute-done((f32[88,1024]{1,0:T(8,128)S(1)}, f32[88,1024]{1,0:T(8,128)S(1)}, u32[]{:S(2)}, u32[]{:S(2)}) %collective-permute-start.3) | collective-permute-done | bytes 360480 | tf_op jit(solution)/shard_map/ppermute | solution.py:204
  14.7 1.2 %collective-permute-start.4 = (f32[88,1024]{1,0:T(8,128)S(1)}, f32[88,1024]{1,0:T(8,128)S(1)}, u32[]{:S(2)}, u32[]{:S(2)}) collective-permute-start(f32[88,1024]{1,0:T(8,128)S(1)} %collective-permute-done.3), channel_id=1, source_target_pairs={{0,1},{1,0},{2,3},{3,2},{4,5},{5,4},{6,7},{7,6},{8,9},{9,8},{10,11... | collective-permute-start | bytes 1081352 | tf_op jit(solution)/shard_map/ppermute | solution.py:204
  15.9 0.3 collective-permute-start.5
  16.2 3.2 %collective-permute-start.7 = (f32[88,1024]{1,0:T(8,128)S(1)}, f32[88,1024]{1,0:T(8,128)S(1)}, u32[]{:S(2)}, u32[]{:S(2)}) collective-permute-start(f32[88,1024]{1,0:T(8,128)S(1)} %collective-permute-done.3), channel_id=1, source_target_pairs={{0,8},{8,16},{16,24},{12,4},{20,12},{28,20},{1,9},{9,17},{17,25},{... | collective-permute-start | bytes 1081352 | tf_op jit(solution)/shard_map/ppermute | solution.py:210
  19.4 0.0 collective-permute-done.1
  19.4 0.6 collective-permute-start.2
  20.0 0.0 collective-permute-done
  20.1 7.7 %collective-permute-done.7 = f32[88,1024]{1,0:T(8,128)S(1)} collective-permute-done((f32[88,1024]{1,0:T(8,128)S(1)}, f32[88,1024]{1,0:T(8,128)S(1)}, u32[]{:S(2)}, u32[]{:S(2)}) %collective-permute-start.7) | collective-permute-done | bytes 360480 | tf_op jit(solution)/shard_map/ppermute | solution.py:210
  27.7 1.1 %collective-permute-start.8 = (f32[88,1024]{1,0:T(8,128)S(1)}, f32[88,1024]{1,0:T(8,128)S(1)}, u32[]{:S(2)}, u32[]{:S(2)}) collective-permute-start(f32[88,1024]{1,0:T(8,128)S(1)} %collective-permute-done.7), channel_id=1, source_target_pairs={{0,1},{1,0},{2,3},{3,2},{4,5},{5,4},{6,7},{7,6},{8,9},{9,8},{10,11... | collective-permute-start | bytes 1081352 | tf_op jit(solution)/shard_map/ppermute | solution.py:204
  28.9 1.2 %collective-permute-start.9 = (f32[88,1024]{1,0:T(8,128)S(1)}, f32[88,1024]{1,0:T(8,128)S(1)}, u32[]{:S(2)}, u32[]{:S(2)}) collective-permute-start(f32[88,1024]{1,0:T(8,128)S(1)} %collective-permute-done.7), channel_id=1, source_target_pairs={{0,2},{1,3},{2,0},{3,1},{4,6},{5,7},{6,4},{7,5},{8,10},{9,11},{10,... | collective-permute-start | bytes 1081352 | tf_op jit(solution)/shard_map/ppermute | solution.py:204
  30.1 0.0 collective-permute-done.5
  30.1 0.3 collective-permute-start.6
  30.4 0.0 collective-permute-done.2
  30.4 0.0 collective-permute-done.4
  30.5 8.3 %collective-permute-done.9 = f32[88,1024]{1,0:T(8,128)S(1)} collective-permute-done((f32[88,1024]{1,0:T(8,128)S(1)}, f32[88,1024]{1,0:T(8,128)S(1)}, u32[]{:S(2)}, u32[]{:S(2)}) %collective-permute-start.9) | collective-permute-done | bytes 360480 | tf_op jit(solution)/shard_map/ppermute | solution.py:204
  38.8 0.9 collective-permute-start.10
  39.7 0.0 collective-permute-done.6
  39.8 0.0 collective-permute-done.8
  39.9 1.2 %collective-permute-done.10 = f32[88,1024]{1,0:T(8,128)S(1)} collective-permute-done((f32[88,1024]{1,0:T(8,128)S(1)}, f32[88,1024]{1,0:T(8,128)S(1)}, u32[]{:S(2)}, u32[]{:S(2)}) %collective-permute-start.10) | collective-permute-done | bytes 360480 | tf_op jit(solution)/shard_map/ppermute | solution.py:204
  41.0 0.0 copy-start
  41.0 2.0 %copy-done = f32[12,88,1024]{2,1,0:T(8,128)} copy-done((f32[12,88,1024]{2,1,0:T(8,128)}, f32[12,88,1024]{2,1,0:T(8,128)S(1)}, u32[]{:S(2)}) %copy-start) | copy-done | bytes 4325400
  43.0 0.7 reshape.54.img_ref
  43.7 36.2 %solve.1 = (f32[720,576]{1,0:T(8,128)}, f32[16,576]{1,0:T(8,128)}) custom-call(s32[9]{0:T(128)} %fusion.2.sel_ref, f32[1]{0:T(128)} %bitcast.47.ridge_ref, f32[12,88,1024]{2,1,0:T(8,128)} %copy-done, f32[12,16,80]{2,1,0:T(8,128)} %reshape.54.img_ref, f32[576,1024]{1,0:T(8,128)} %bitcast.48), custom_call_target="tpu_custom_call" | custom-call | tf_op jit(solution)/shard_map/solve/pallas_call | solution.py:173
  79.9 0.9 reshape.57
  80.8 0.1 fusion.3
  81.0 3.1 %collective-permute-start.12 = (f32[16,24,4]{2,1,0:T(8,128)S(1)}, f32[16,24,4]{2,1,0:T(8,128)S(1)}, u32[]{:S(2)}, u32[]{:S(2)}) collective-permute-start(f32[16,24,4]{2,1,0:T(8,128)S(1)} %get-tuple-element.9), channel_id=1, source_target_pairs={{0,4},{4,8},{8,12},{12,16},{16,20},{20,24},{24,28},{1,5},{5,9},{9,... | collective-permute-start | bytes 18440 | tf_op jit(solution)/shard_map/ppermute | solution.py:230
  84.1 3.0 %collective-permute-start.11 = (f32[16,24,4]{2,1,0:T(8,128)S(1)}, f32[16,24,4]{2,1,0:T(8,128)S(1)}, u32[]{:S(2)}, u32[]{:S(2)}) collective-permute-start(f32[16,24,4]{2,1,0:T(8,128)S(1)} %get-tuple-element.8), channel_id=1, source_target_pairs={{4,0},{8,4},{12,8},{16,12},{20,16},{24,20},{28,24},{5,1},{9,5},{13... | collective-permute-start | bytes 18440 | tf_op jit(solution)/shard_map/ppermute | solution.py:230
  87.2 3.9 %collective-permute-start.14 = (f32[16,4,24]{2,1,0:T(4,128)S(1)}, f32[16,4,24]{2,1,0:T(4,128)S(1)}, u32[]{:S(2)}, u32[]{:S(2)}) collective-permute-start(f32[16,4,24]{2,1,0:T(4,128)S(1)} %get-tuple-element.11), channel_id=1, source_target_pairs={{0,1},{1,2},{2,3},{4,5},{5,6},{6,7},{8,9},{9,10},{10,11},{12,13},{... | collective-permute-start | bytes 18440 | tf_op jit(solution)/shard_map/ppermute | solution.py:230
  91.1 1.9 %collective-permute-start.13 = (f32[16,4,24]{2,1,0:T(4,128)S(1)}, f32[16,4,24]{2,1,0:T(4,128)S(1)}, u32[]{:S(2)}, u32[]{:S(2)}) collective-permute-start(f32[16,4,24]{2,1,0:T(4,128)S(1)} %get-tuple-element.10), channel_id=1, source_target_pairs={{1,0},{2,1},{3,2},{5,4},{6,5},{7,6},{9,8},{10,9},{11,10},{13,12},{... | collective-permute-start | bytes 18440 | tf_op jit(solution)/shard_map/ppermute | solution.py:230
  93.0 2.8 %copy.8 = f32[1,1,720,576]{2,3,1,0:T(8,128)} copy(f32[1,1,720,576]{3,2,1,0:T(8,128)} %bitcast.49) | data formatting | bytes 3317760
  95.8 0.0 collective-permute-done.12
  95.8 0.0 collective-permute-done.11
  95.9 0.0 collective-permute-done.14
  95.9 0.1 broadcast_multiply_fusion.2
  96.0 0.4 collective-permute-done.13
  96.3 0.1 broadcast_multiply_fusion.3
  96.4 0.8 pad_add_fusion
  (18 shorter events, 0.4 us)
Async XLA Ops:
  3.1 16.9 %collective-permute-start = (f32[88,1024]{1,0:T(8,128)S(1)}, f32[88,1024]{1,0:T(8,128)S(1)}, u32[]{:S(2)}, u32[]{:S(2)}) collective-permute-start(f32[88,1024]{1,0:T(8,128)S(1)} %select_maximum_fusion), channel_id=1, source_target_pairs={{0,1},{1,0},{2,3},{3,2},{4,5},{5,4},{6,7},{7,6},{8,9},{9,8},{10,11... | collective-permute-start | bytes 1081352 | tf_op jit(solution)/shard_map/ppermute | solution.py:204
  3.9 15.5 %collective-permute-start.1 = (f32[88,1024]{1,0:T(8,128)S(1)}, f32[88,1024]{1,0:T(8,128)S(1)}, u32[]{:S(2)}, u32[]{:S(2)}) collective-permute-start(f32[88,1024]{1,0:T(8,128)S(1)} %select_maximum_fusion), channel_id=1, source_target_pairs={{0,2},{1,3},{2,0},{3,1},{4,6},{5,7},{6,4},{7,5},{8,10},{9,11},{10,... | collective-permute-start | bytes 1081352 | tf_op jit(solution)/shard_map/ppermute | solution.py:204
  5.1 9.6 %collective-permute-start.3 = (f32[88,1024]{1,0:T(8,128)S(1)}, f32[88,1024]{1,0:T(8,128)S(1)}, u32[]{:S(2)}, u32[]{:S(2)}) collective-permute-start(f32[88,1024]{1,0:T(8,128)S(1)} %select_maximum_fusion), channel_id=1, source_target_pairs={{0,4},{4,0},{8,12},{12,8},{16,20},{20,16},{24,28},{28,24},{1,5},{5... | collective-permute-start | bytes 1081352 | tf_op jit(solution)/shard_map/ppermute | solution.py:204
  14.7 15.8 %collective-permute-start.4 = (f32[88,1024]{1,0:T(8,128)S(1)}, f32[88,1024]{1,0:T(8,128)S(1)}, u32[]{:S(2)}, u32[]{:S(2)}) collective-permute-start(f32[88,1024]{1,0:T(8,128)S(1)} %collective-permute-done.3), channel_id=1, source_target_pairs={{0,1},{1,0},{2,3},{3,2},{4,5},{5,4},{6,7},{7,6},{8,9},{9,8},{10,11... | collective-permute-start | bytes 1081352 | tf_op jit(solution)/shard_map/ppermute | solution.py:204
  15.9 14.2 %collective-permute-start.5 = (f32[88,1024]{1,0:T(8,128)S(1)}, f32[88,1024]{1,0:T(8,128)S(1)}, u32[]{:S(2)}, u32[]{:S(2)}) collective-permute-start(f32[88,1024]{1,0:T(8,128)S(1)} %collective-permute-done.3), channel_id=1, source_target_pairs={{0,2},{1,3},{2,0},{3,1},{4,6},{5,7},{6,4},{7,5},{8,10},{9,11},{10,... | collective-permute-start | bytes 1081352 | tf_op jit(solution)/shard_map/ppermute | solution.py:204
  16.2 11.6 %collective-permute-start.7 = (f32[88,1024]{1,0:T(8,128)S(1)}, f32[88,1024]{1,0:T(8,128)S(1)}, u32[]{:S(2)}, u32[]{:S(2)}) collective-permute-start(f32[88,1024]{1,0:T(8,128)S(1)} %collective-permute-done.3), channel_id=1, source_target_pairs={{0,8},{8,16},{16,24},{12,4},{20,12},{28,20},{1,9},{9,17},{17,25},{... | collective-permute-start | bytes 1081352 | tf_op jit(solution)/shard_map/ppermute | solution.py:210
  19.4 11.0 %collective-permute-start.2 = (f32[88,1024]{1,0:T(8,128)S(1)}, f32[88,1024]{1,0:T(8,128)S(1)}, u32[]{:S(2)}, u32[]{:S(2)}) collective-permute-start(f32[88,1024]{1,0:T(8,128)S(1)} %collective-permute-done.1), channel_id=1, source_target_pairs={{0,1},{1,0},{2,3},{3,2},{4,5},{5,4},{6,7},{7,6},{8,9},{9,8},{10,11... | collective-permute-start | bytes 1081352 | tf_op jit(solution)/shard_map/ppermute | solution.py:204
  27.7 12.0 %collective-permute-start.8 = (f32[88,1024]{1,0:T(8,128)S(1)}, f32[88,1024]{1,0:T(8,128)S(1)}, u32[]{:S(2)}, u32[]{:S(2)}) collective-permute-start(f32[88,1024]{1,0:T(8,128)S(1)} %collective-permute-done.7), channel_id=1, source_target_pairs={{0,1},{1,0},{2,3},{3,2},{4,5},{5,4},{6,7},{7,6},{8,9},{9,8},{10,11... | collective-permute-start | bytes 1081352 | tf_op jit(solution)/shard_map/ppermute | solution.py:204
  28.9 10.0 %collective-permute-start.9 = (f32[88,1024]{1,0:T(8,128)S(1)}, f32[88,1024]{1,0:T(8,128)S(1)}, u32[]{:S(2)}, u32[]{:S(2)}) collective-permute-start(f32[88,1024]{1,0:T(8,128)S(1)} %collective-permute-done.7), channel_id=1, source_target_pairs={{0,2},{1,3},{2,0},{3,1},{4,6},{5,7},{6,4},{7,5},{8,10},{9,11},{10,... | collective-permute-start | bytes 1081352 | tf_op jit(solution)/shard_map/ppermute | solution.py:204
  30.1 9.6 %collective-permute-start.6 = (f32[88,1024]{1,0:T(8,128)S(1)}, f32[88,1024]{1,0:T(8,128)S(1)}, u32[]{:S(2)}, u32[]{:S(2)}) collective-permute-start(f32[88,1024]{1,0:T(8,128)S(1)} %collective-permute-done.5), channel_id=1, source_target_pairs={{0,1},{1,0},{2,3},{3,2},{4,5},{5,4},{6,7},{7,6},{8,9},{9,8},{10,11... | collective-permute-start | bytes 1081352 | tf_op jit(solution)/shard_map/ppermute | solution.py:204
  38.8 2.2 %collective-permute-start.10 = (f32[88,1024]{1,0:T(8,128)S(1)}, f32[88,1024]{1,0:T(8,128)S(1)}, u32[]{:S(2)}, u32[]{:S(2)}) collective-permute-start(f32[88,1024]{1,0:T(8,128)S(1)} %collective-permute-done.9), channel_id=1, source_target_pairs={{0,1},{1,0},{2,3},{3,2},{4,5},{5,4},{6,7},{7,6},{8,9},{9,8},{10,11... | collective-permute-start | bytes 1081352 | tf_op jit(solution)/shard_map/ppermute | solution.py:204
  41.0 2.0 %copy-start = (f32[12,88,1024]{2,1,0:T(8,128)}, f32[12,88,1024]{2,1,0:T(8,128)S(1)}, u32[]{:S(2)}) copy-start(f32[12,88,1024]{2,1,0:T(8,128)S(1)} %bitcast_dynamic-update-slice_fusion.win_ref) | copy-start | bytes 12976132
  81.0 14.9 %collective-permute-start.12 = (f32[16,24,4]{2,1,0:T(8,128)S(1)}, f32[16,24,4]{2,1,0:T(8,128)S(1)}, u32[]{:S(2)}, u32[]{:S(2)}) collective-permute-start(f32[16,24,4]{2,1,0:T(8,128)S(1)} %get-tuple-element.9), channel_id=1, source_target_pairs={{0,4},{4,8},{8,12},{12,16},{16,20},{20,24},{24,28},{1,5},{5,9},{9,... | collective-permute-start | bytes 18440 | tf_op jit(solution)/shard_map/ppermute | solution.py:230
  84.1 11.7 %collective-permute-start.11 = (f32[16,24,4]{2,1,0:T(8,128)S(1)}, f32[16,24,4]{2,1,0:T(8,128)S(1)}, u32[]{:S(2)}, u32[]{:S(2)}) collective-permute-start(f32[16,24,4]{2,1,0:T(8,128)S(1)} %get-tuple-element.8), channel_id=1, source_target_pairs={{4,0},{8,4},{12,8},{16,12},{20,16},{24,20},{28,24},{5,1},{9,5},{13... | collective-permute-start | bytes 18440 | tf_op jit(solution)/shard_map/ppermute | solution.py:230
  87.2 8.7 %collective-permute-start.14 = (f32[16,4,24]{2,1,0:T(4,128)S(1)}, f32[16,4,24]{2,1,0:T(4,128)S(1)}, u32[]{:S(2)}, u32[]{:S(2)}) collective-permute-start(f32[16,4,24]{2,1,0:T(4,128)S(1)} %get-tuple-element.11), channel_id=1, source_target_pairs={{0,1},{1,2},{2,3},{4,5},{5,6},{6,7},{8,9},{9,10},{10,11},{12,13},{... | collective-permute-start | bytes 18440 | tf_op jit(solution)/shard_map/ppermute | solution.py:230
  91.1 5.2 %collective-permute-start.13 = (f32[16,4,24]{2,1,0:T(4,128)S(1)}, f32[16,4,24]{2,1,0:T(4,128)S(1)}, u32[]{:S(2)}, u32[]{:S(2)}) collective-permute-start(f32[16,4,24]{2,1,0:T(4,128)S(1)} %get-tuple-element.10), channel_id=1, source_target_pairs={{1,0},{2,1},{3,2},{5,4},{6,5},{7,6},{9,8},{10,9},{11,10},{13,12},{... | collective-permute-start | bytes 18440 | tf_op jit(solution)/shard_map/ppermute | solution.py:230

commit v2 on v1

v2 whole, which is shorter than its diff:
```python
import functools

import jax
import jax.numpy as jnp
import numpy as np
from jax import lax
from jax.experimental import pallas as pl
from jax.experimental.pallas import tpu as pltpu
from jax.sharding import PartitionSpec as P

f32 = jnp.float32
bf16 = jnp.bfloat16
LANE = 128
SUB = 8
FADE = 4
PHASES = (3, 3, 3)
ARRIVED = (6, 10, 12)
FLIP = (0, 1, 2, 0, 3, 1, 2, 0, 3, 1, 2, 3)
TILE = (0, 0, 0, 1, 0, 1, 1, 2, 1, 2, 2, 2)


def split2(x):
    hi = x.astype(bf16)
    lo = (x - hi.astype(f32)).astype(bf16)
    return hi, lo


def dot(a, b, tb=False):
    dims = (((1,), (1 if tb else 0,)), ((), ()))
    return lax.dot_general(a, b, dims, preferred_element_type=f32)


def dot3(a, b, tb=False):
    return dot(a[0], b[0], tb) + (dot(a[0], b[1], tb) + dot(a[1], b[0], tb))


def panel_sweep(rows, q, sub, lane):
    base = q * SUB
    p = rows[q]
    cols = [
        jnp.where(lane >= 0, jnp.broadcast_to(p[:, base + k : base + k + 1], (SUB, LANE)), 0.0)
        for k in range(SUB)
    ]
    inside = (lane >= base) & (lane < base + SUB)
    w = jnp.where(inside, jnp.where(lane - base == sub, 1.0, 0.0).astype(f32), p)
    for k in range(SUB):
        here = sub == k
        inv = 1.0 / jnp.broadcast_to(cols[k][k : k + 1, :], (SUB, LANE))
        h = jnp.where(here, -1.0, cols[k])
        for m in range(k + 1, SUB):
            r = jnp.broadcast_to(cols[m][k : k + 1, :], (SUB, LANE))
            cols[m] = jnp.where(here, 0.0, cols[m]) - (h * r) * inv
        r = jnp.broadcast_to(w[k : k + 1, :], (SUB, LANE))
        w = jnp.where(here, 0.0, w) - (h * r) * inv
    wk = [jnp.broadcast_to(w[k : k + 1, :], (SUB, LANE)) for k in range(SUB)]
    count = len(rows)
    res = [None] * count
    for step in range(count):
        g = (q + 1 + step) % count
        if g == q:
            res[g] = w
            continue
        a = rows[g]
        acc = [jnp.where(inside, 0.0, a), None]
        for k in range(SUB):
            t = jnp.broadcast_to(a[:, base + k : base + k + 1], (SUB, LANE)) * wk[k]
            s = k % 2
            acc[s] = (acc[s] - t) if acc[s] is not None else -t
        res[g] = acc[0] + acc[1]
    return res


def pack_kernel(mask_ref, feat_in, img_in, out_ref, feat_ref, img_ref, sems):
    npix, feat = feat_ref.shape
    layers = img_ref.shape[0]
    blocks = feat // LANE
    loads = [
        pltpu.make_async_copy(feat_in.at[0, 0], feat_ref, sems.at[0]),
        pltpu.make_async_copy(img_in.at[0, 0], img_ref, sems.at[1]),
    ]
    for cp in loads:
        cp.start()
    row = lax.broadcasted_iota(jnp.int32, (layers, npix), 0)
    keep = jnp.zeros((layers, npix), f32)
    for i in range(layers):
        keep = jnp.where(row == i, mask_ref[0, 0, i].astype(f32), keep)
    for cp in loads:
        cp.wait()
    for c in range(blocks):
        out_ref[c * npix : (c + 1) * npix, :] = feat_ref[:, c * LANE : (c + 1) * LANE]
    tail = blocks * npix
    out_ref[tail : tail + layers, :] = jnp.zeros((layers, LANE), f32)
    out_ref[tail : tail + layers, 0:npix] = img_ref[...] * keep


def pack(features, images, layer_mask):
    npix, feat = features.shape[2:]
    layers = images.shape[2]
    vm = pl.BlockSpec(memory_space=pltpu.VMEM)
    hb = pl.BlockSpec(memory_space=pltpu.HBM)
    return pl.pallas_call(
        pack_kernel,
        out_shape=jax.ShapeDtypeStruct((feat // LANE * npix + layers, LANE), f32),
        in_specs=[pl.BlockSpec(memory_space=pltpu.SMEM), hb, hb],
        out_specs=vm,
        scratch_shapes=[
            pltpu.VMEM((npix, feat), f32),
            pltpu.VMEM((layers, npix), f32),
            pltpu.SemaphoreType.DMA((2,)),
        ],
        compiler_params=pltpu.CompilerParams(vmem_limit_bytes=8 << 20),
        name="pack",
    )(layer_mask, features, images)


def halve_kernel(t_ref, hi_ref, lo_ref):
    hi, lo = split2(t_ref[0, 0])
    hi_ref[...] = hi
    lo_ref[...] = lo


def halve(target):
    nout, feat = target.shape[2:]
    vm = pl.BlockSpec(memory_space=pltpu.VMEM)
    shape = jax.ShapeDtypeStruct((nout, feat), bf16)
    return pl.pallas_call(
        halve_kernel,
        out_shape=(shape, shape),
        in_specs=[vm],
        out_specs=(vm, vm),
        compiler_params=pltpu.CompilerParams(vmem_limit_bytes=16 << 20),
        name="halve",
    )(target)


def stack_left(x):
    hi, lo = split2(x)
    return jnp.concatenate([hi, hi, lo], axis=1)


def stack_right(x):
    hi, lo = split2(x)
    return jnp.concatenate([hi, lo, hi], axis=0)


def chunks(width, step=256):
    return [slice(at, min(at + step, width)) for at in range(0, width, step)]


def phase_kernel(*refs, done, narr, last, npix, layers, nout, side):
    refs = list(refs)
    take = lambda count: [refs.pop(0) for _ in range(count)]
    rank_ref, ridge_ref, odd_ref = take(3)
    if last:
        (mask_ref,) = take(1)
    arrs = take(narr)
    t_in = take(2)
    old_in = [tuple(take(2)) for _ in done]
    p_in, w_in = take(2) if done else (None, None)
    e = sum(done)
    if last:
        z_out, v_out, co_ref, near_ref, far_ref, pair_ref, mid_ref = take(7)
    else:
        fh_out, fl_out, p_out, w_out = take(4)
    fsel, fh_ref, fl_ref, s_ref, d_ref, r_ref, th, tl = take(8)
    sems, sem = take(2)
    l = fsel.shape[0]
    n = l * npix
    before = e * npix
    if not last:
        p_ref, w_ref = take(2)
    else:
        img_ref, img_sems = take(2)
    if done:
        old = [tuple(take(2)) for _ in done]
        old_p, old_w, v_ref = take(3)
    feat_blocks = fh_ref.shape[1] // LANE
    body = feat_blocks * npix

    def picks(t):
        r = rank_ref[t]
        return r, (r >= e) & (r < e + l)

    def copy(t, r):
        return pltpu.make_async_copy(arrs[t], fsel.at[r - e], sems.at[t])

    def copy_img(t, r):
        return pltpu.make_async_copy(arrs[t].at[pl.ds(body, layers)], img_ref.at[r], img_sems.at[t])

    for t in range(narr):
        r, hit = picks(t)

        @pl.when(hit)
        def _():
            copy(t, r).start()

    pairs = []
    for src, dst in zip(old_in, old if done else []):
        pairs += [(src[0], dst[0]), (src[1], dst[1])]
    early = len(pairs)
    if done:
        pairs += [(p_in, old_p), (w_in, old_w)]
    pairs += [(t_in[0], th), (t_in[1], tl)]
    loads = [pltpu.make_async_copy(x, y, sem.at[i]) for i, (x, y) in enumerate(pairs)]
    for cp in loads:
        cp.start()
    if last:
        for t in range(narr):
            r = rank_ref[t]

            @pl.when(r >= 0)
            def _():
                copy_img(t, r).start()

    for t in range(narr):
        r, hit = picks(t)

        @pl.when(hit)
        def _():
            copy(t, r).wait()

    for i in range(l):
        for c in range(feat_blocks):
            hi, lo = split2(fsel[i, c * npix : (c + 1) * npix, :])
            fh_ref[i * npix : (i + 1) * npix, c * LANE : (c + 1) * LANE] = hi
            fl_ref[i * npix : (i + 1) * npix, c * LANE : (c + 1) * LANE] = lo
    stores = []
    at = len(pairs)
    if not last:
        stores = [
            pltpu.make_async_copy(fh_ref, fh_out, sem.at[at]),
            pltpu.make_async_copy(fl_ref, fl_out, sem.at[at + 1]),
        ]
        for cp in stores:
            cp.start()
    first = early + (1 if done else 0)
    for cp in loads[:first]:
        cp.wait()
    mine = (fh_ref[...], fl_ref[...])
    ridge = ridge_ref[0, 0]
    sub = lax.broadcasted_iota(jnp.int32, (SUB, LANE), 0)
    lane = lax.broadcasted_iota(jnp.int32, (SUB, LANE), 1)
    system = dot3(mine, mine, True)
    cross = []
    if done:
        tops = [sum(done[:i]) * npix for i in range(len(done) + 1)]
        parts = [(x[...], y[...]) for x, y in old]
        gel = jnp.concatenate([dot3(part, mine, True) for part in parts], axis=0)
        v = dot3(split2(old_p[...]), split2(gel))
        v_ref[...] = v
        for i, part in enumerate(parts):
            g = split2(dot3(mine, part, True))
            cross.append((slice(tops[i], tops[i + 1]), g))
        for rows, g in cross:
            system = system - dot3(g, split2(v[rows, :]))
    d_ref[:, 0:npix] = system[0:npix, 0:npix]
    for c in range(l):
        s_ref[c, :, 0:npix] = system[:, c * npix : (c + 1) * npix]

    for cp in loads[first:]:
        cp.wait()
    if last:
        for t in range(narr):
            r = rank_ref[t]

            @pl.when(r >= 0)
            def _():
                copy_img(t, r).wait()

    work = []
    feat = feat_blocks * LANE

    def right_sides(cut, deep, fresh):
        part = dot3(
            (fh_ref[:, deep], fl_ref[:, deep]), (th[cut, deep], tl[cut, deep]), True
        )
        r_ref[:, cut] = part if fresh else r_ref[:, cut] + part

    def cross_right(cut, rows, g):
        r_ref[:, cut] = r_ref[:, cut] - dot3(g, split2(old_w[rows, cut]))

    for cut in chunks(nout):
        for deep in chunks(feat):
            work.append(functools.partial(right_sides, cut, deep, deep.start == 0))
        for rows, g in cross:
            work.append(functools.partial(cross_right, cut, rows, g))

    picture = {}
    if last:

        def base(cut):
            total = None
            for i in range(e):
                part = dot(
                    stack_left(img_ref[i][:, 0:npix]), stack_right(old_w[i * npix : (i + 1) * npix, cut])
                )
                total = part if total is None else total + part
            picture[cut.start] = total

        def effective():
            ours = jnp.concatenate([img_ref[e + i][:, 0:npix] for i in range(l)], axis=1)
            for i in range(e):
                ours = ours - dot(
                    stack_left(img_ref[i][:, 0:npix]), stack_right(v_ref[i * npix : (i + 1) * npix, :])
                )
            picture["rest"] = split2(ours)

        for cut in chunks(nout):
            work.append(functools.partial(base, cut))
        work.append(effective)

    def update(c, coef, d, j):
        rows = slice(j * npix, (j + 1) * npix)
        w = dot(d, stack_right(s_ref[c, rows, 0:npix]))
        s_ref[c, :, 0:npix] = s_ref[c, :, 0:npix] - dot(coef, stack_right(w))
        s_ref[c, rows, 0:npix] = w

    def update_right(coef, d, j, cut):
        rows = slice(j * npix, (j + 1) * npix)
        w = dot(d, stack_right(r_ref[rows, cut]))
        r_ref[:, cut] = r_ref[:, cut] - dot(coef, stack_right(w))
        r_ref[rows, cut] = w

    def update_own(coef, full, j):
        rows = slice(j * npix, (j + 1) * npix)
        s_ref[j, :, 0:npix] = -dot(coef, stack_right(full))
        s_ref[j, rows, 0:npix] = full

    for j in range(l):
        cut = slice(j * npix, (j + 1) * npix)
        after = slice((j + 1) * npix, (j + 2) * npix)
        rows = []
        for g in range(npix // SUB):
            at_row = slice(g * SUB, (g + 1) * SUB)
            rows.append(d_ref[at_row, :] + jnp.where(lane == sub + g * SUB, ridge, 0.0))
        count = len(rows)
        for q in range(count):
            rows = panel_sweep(rows, q, sub, lane)
            for _ in range(-(-len(work) // (count - q))):
                work.pop(0)()
        while work:
            work.pop(0)()
        full = jnp.concatenate(rows, axis=0)[:, :npix]
        if j + 1 < l:
            w = dot3(split2(full), split2(s_ref[j + 1, cut, 0:npix]))
            step = dot3(split2(s_ref[j, after, 0:npix]), split2(w))
            d_ref[:, 0:npix] = s_ref[j + 1, after, 0:npix] - step
        d = stack_left(full)
        coef = stack_left(s_ref[j, :, 0:npix])
        for c in list(range(j + 1, l)) + list(range(j)):
            if c > j or not last:
                work.append(functools.partial(update, c, coef, d, j))
        for part in chunks(nout):
            work.append(functools.partial(update_right, coef, d, j, part))
        if not last:
            work.append(functools.partial(update_own, coef, full, j))
    while work:
        work.pop(0)()
    z = r_ref[...]
    z2 = split2(z)
    if last:
        stores = [
            pltpu.make_async_copy(r_ref, z_out, sem.at[at]),
            pltpu.make_async_copy(v_ref, v_out, sem.at[at + 1]),
        ]
        for cp in stores:
            cp.start()
        base_total = jnp.concatenate([picture[cut.start] for cut in chunks(nout)], axis=1)
        total = base_total + dot3(picture["rest"], z2)
        send(total, co_ref, near_ref, far_ref, pair_ref, mid_ref, mask_ref, odd_ref, side)
        for cp in stores:
            cp.wait()
        return
    q_flat = jnp.concatenate([s_ref[c, :, 0:npix] for c in range(l)], axis=1)
    w_ref[before : before + n, :] = z
    if done:
        v2 = split2(v_ref[...])
        w_ref[0:before, :] = old_w[...] - dot3(v2, z2)
        q2 = split2(q_flat)
        vq = dot3(v2, q2)
        second = dot3(q2, v2, True)
        first = old_p[...] + dot3(split2(vq), v2, True)
        p_ref[0:before, :] = jnp.concatenate([first, -vq], axis=1)
        p_ref[before : before + n, :] = jnp.concatenate([-second, q_flat], axis=1)
    else:
        p_ref[...] = q_flat
    more = [
        pltpu.make_async_copy(p_ref, p_out, sem.at[at + 2]),
        pltpu.make_async_copy(w_ref, w_out, sem.at[at + 3]),
    ]
    for cp in more:
        cp.start()
    for cp in stores + more:
        cp.wait()


def send(total, co_ref, near_ref, far_ref, pair_ref, mid_ref, mask_ref, odd_ref, side):
    layers, nout = total.shape
    rest = side - FADE
    span = FADE * side
    co_ref[...] = total
    none = jnp.zeros((layers, rest), f32)
    to_west = jnp.concatenate([none, total[:, : nout - rest]], axis=1) * mask_ref[0:1, :]
    to_east = jnp.concatenate([total[:, rest:], none], axis=1) * mask_ref[1:2, :]
    to_north = total[:, 0:span] * mask_ref[2:3, 0:span]
    to_south = total[:, nout - span :] * mask_ref[3:4, 0:span]
    sky_odd, batch_odd = odd_ref[0] == 1, odd_ref[1] == 1
    near_ref[...] = jnp.where(sky_odd, to_west, to_east)
    far_ref[...] = jnp.where(sky_odd, to_east, to_west)
    pair_ref[...] = jnp.where(batch_odd, to_north, to_south)
    mid_ref[...] = jnp.where(batch_odd, to_south, to_north)


def fade_masks(nout, side):
    ramp = (np.arange(FADE, dtype=np.float32) + np.float32(1.0)) / np.float32(FADE + 1.0)
    column = np.arange(nout) % side
    rest = side - FADE
    masks = np.zeros((4, nout), np.float32)
    masks[0] = np.where(column >= rest, ramp[np.maximum(column - rest, 0)], 0.0)
    masks[1] = np.where(column < FADE, ramp[::-1][np.minimum(column, FADE - 1)], 0.0)
    masks[2, : FADE * side] = np.repeat(ramp, side)
    masks[3, : FADE * side] = np.repeat(ramp[::-1], side)
    return masks


def phase(number, rank, ridge, odd, masks, arrs, t2, old, state, shapes):
    npix, layers, nout, side, feat = shapes
    done = PHASES[:number]
    l = PHASES[number]
    last = number == len(PHASES) - 1
    e = sum(done)
    n, size = l * npix, (e + l) * npix
    vm = pl.BlockSpec(memory_space=pltpu.VMEM)
    sm = pl.BlockSpec(memory_space=pltpu.SMEM)
    hb = pl.BlockSpec(memory_space=pltpu.HBM)
    args = [rank, ridge, odd]
    specs = [sm, sm, sm]
    if last:
        args += [masks]
        specs += [vm]
    args += list(arrs) + list(t2)
    for pair in old:
        args += list(pair)
    if done:
        args += list(state)
    specs += [hb] * (len(args) - len(specs))
    real = lambda *shape: jax.ShapeDtypeStruct(shape, f32)
    half = jax.ShapeDtypeStruct((n, feat), bf16)
    if last:
        outs = (
            real(n, nout),
            real(e * npix, n),
            real(layers, nout),
            real(layers, nout),
            real(layers, nout),
            real(layers, FADE * side),
            real(layers, FADE * side),
        )
        out_specs = (hb, hb, vm, vm, vm, vm, vm)
    else:
        outs = (half, half, real(size, size), real(size, nout))
        out_specs = (hb, hb, hb, hb)
    fh = pltpu.VMEM((n, feat), bf16)
    tgt = pltpu.VMEM((nout, feat), bf16)
    scratch = [
        pltpu.VMEM((l,) + arrs[0].shape, f32),
        fh,
        fh,
        pltpu.VMEM((l, n, LANE), f32),
        pltpu.VMEM((npix, LANE), f32),
        pltpu.VMEM((n, nout), f32),
        tgt,
        tgt,
        pltpu.SemaphoreType.DMA((len(arrs),)),
        pltpu.SemaphoreType.DMA((2 * len(done) + 8,)),
    ]
    if last:
        scratch += [
            pltpu.VMEM((e + l, layers, LANE), f32),
            pltpu.SemaphoreType.DMA((len(arrs),)),
        ]
    else:
        scratch += [pltpu.VMEM((size, size), f32), pltpu.VMEM((size, nout), f32)]
    if done:
        for count in done:
            scratch += [pltpu.VMEM((count * npix, feat), bf16)] * 2
        scratch += [
            pltpu.VMEM((e * npix, e * npix), f32),
            pltpu.VMEM((e * npix, nout), f32),
            pltpu.VMEM((e * npix, n), f32),
        ]
    return pl.pallas_call(
        functools.partial(
            phase_kernel,
            done=done,
            narr=len(arrs),
            last=last,
            npix=npix,
            layers=layers,
            nout=nout,
            side=side,
        ),
        out_shape=outs,
        in_specs=specs,
        out_specs=out_specs,
        scratch_shapes=scratch,
        compiler_params=pltpu.CompilerParams(vmem_limit_bytes=40 << 20),
        cost_estimate=pl.CostEstimate(
            flops=2_000_000_000 * l, transcendentals=0, bytes_accessed=4_000_000
        ),
        name="phase%d" % number,
    )(*args)


def close_kernel(pos_ref, w_in, v_in, z_in, out_ref, w_ref, v_ref, x_ref, sems):
    before = w_ref.shape[0]
    n = z_in.shape[0]
    count = pos_ref.shape[0]
    npix = (before + n) // count
    loads = [
        pltpu.make_async_copy(v_in, v_ref, sems.at[0]),
        pltpu.make_async_copy(z_in, x_ref.at[pl.ds(before, n)], sems.at[1]),
        pltpu.make_async_copy(w_in, w_ref, sems.at[2]),
    ]
    for cp in loads:
        cp.start()
    for cp in loads:
        cp.wait()
    z2 = split2(x_ref[before : before + n, :])
    x_ref[0:before, :] = w_ref[...] - dot3(split2(v_ref[...]), z2)
    for i in range(count):
        src = pl.multiple_of(pos_ref[i] * npix, SUB)
        out_ref[i * npix : (i + 1) * npix, :] = x_ref[pl.ds(src, npix), :]


def close(pos, w, v, z):
    before, nout = w.shape
    n = z.shape[0]
    hb = pl.BlockSpec(memory_space=pltpu.HBM)
    vm = pl.BlockSpec(memory_space=pltpu.VMEM)
    return pl.pallas_call(
        close_kernel,
        out_shape=jax.ShapeDtypeStruct((before + n, nout), f32),
        in_specs=[pl.BlockSpec(memory_space=pltpu.SMEM), hb, hb, hb],
        out_specs=vm,
        scratch_shapes=[
            pltpu.VMEM((before, nout), f32),
            pltpu.VMEM((before, n), f32),
            pltpu.VMEM((before + n, nout), f32),
            pltpu.SemaphoreType.DMA((3,)),
        ],
        compiler_params=pltpu.CompilerParams(vmem_limit_bytes=20 << 20),
        cost_estimate=pl.CostEstimate(
            flops=500_000_000, transcendentals=0, bytes_accessed=6_000_000
        ),
        name="close",
    )(pos, w, v, z)


def blend_kernel(odd_ref, co_ref, near_ref, far_ref, pair_ref, mid_ref, out_ref):
    layers, side, _ = out_ref.shape
    nout = co_ref.shape[1]
    span = FADE * side
    batch_odd = odd_ref[1] == 1
    pair, mid = pair_ref[...], mid_ref[...]
    south = jnp.where(batch_odd, mid, pair)
    north = jnp.where(batch_odd, pair, mid)
    none = jnp.zeros((layers, nout - 2 * span), f32)
    total = co_ref[...] + near_ref[...] + far_ref[...] + jnp.concatenate([north, none, south], axis=1)
    for r in range(side):
        out_ref[:, r, :] = total[:, r * side : (r + 1) * side]


def blend(odd, co, strips, side):
    vm = pl.BlockSpec(memory_space=pltpu.VMEM)
    return pl.pallas_call(
        blend_kernel,
        out_shape=jax.ShapeDtypeStruct((co.shape[0], side, side), f32),
        in_specs=[pl.BlockSpec(memory_space=pltpu.SMEM)] + [vm] * 5,
        out_specs=vm,
        compiler_params=pltpu.CompilerParams(vmem_limit_bytes=8 << 20),
        name="blend",
    )(odd, co, *strips)


def swap(value, axis, bit):
    count = lax.axis_size(axis)
    return lax.ppermute(value, axis, [(i, i ^ bit) for i in range(count)])


def between(value, axis):
    count = lax.axis_size(axis)
    pairs = [(i, i + 1) for i in range(1, count - 1, 2)]
    return lax.ppermute(value, axis, pairs + [(j, i) for i, j in pairs])


def hop_two(value):
    count = lax.axis_size("sky")
    pairs = [(i, i + 2) for i in range(0, count - 2, 2)] + [(i, i - 2) for i in range(3, count, 2)]
    return lax.ppermute(value, "sky", pairs)


def local(features, target, images, layer_mask, pair_list, ridge_weight):
    npix, feat = features.shape[2:]
    layers = images.shape[2]
    nout = target.shape[2]
    side = int(round(nout**0.5))
    shapes = (npix, layers, nout, side, feat)
    sky_at, batch_at = lax.axis_index("sky"), lax.axis_index("batch")
    own = pack(features, images, layer_mask)
    n0 = swap(own, "sky", 1)
    a2 = swap(own, "batch", 2)
    a1 = swap(own, "batch", 1)
    t2 = halve(target)
    chosen = pair_list.reshape(-1)
    odd = sky_at % 2
    tiles = jnp.asarray(TILE, jnp.int32)
    column = jnp.where(tiles == 0, 1, jnp.where((tiles == 1) == (odd == 0), 2, 0))
    names = 3 * (jnp.asarray(FLIP, jnp.int32) ^ batch_at) + column
    match = (names[:, None] == chosen[None, :]).astype(jnp.int32)
    hit = jnp.sum(match, axis=1)
    order = jnp.arange(names.shape[0])
    count = jnp.sum(jnp.where(order[None, :] < order[:, None], hit[None, :], 0), axis=1)
    rank = jnp.where(hit > 0, count, -1).astype(jnp.int32)
    pos = jnp.sum(match * count[:, None], axis=0).astype(jnp.int32)
    parity = jnp.stack([odd, batch_at % 2]).astype(jnp.int32)

    masks = jnp.asarray(fade_masks(nout, side))
    common = (rank, ridge_weight, parity, masks)
    d0 = hop_two(n0)
    n2 = swap(n0, "batch", 2)
    a3 = swap(a2, "batch", 1)
    n1 = swap(n0, "batch", 1)
    arrs = [own, a1, a2, n0, a3, n1]
    fa_h, fa_l, p, w = phase(0, *common, arrs, t2, [], None, shapes)
    n2, d0, fa_h = lax.optimization_barrier((n2, d0, fa_h))
    d2 = swap(d0, "batch", 2)
    n3 = swap(n2, "batch", 1)
    d1 = swap(d0, "batch", 1)
    arrs += [n2, d0, n3, d1]
    fb_h, fb_l, p, w = phase(1, *common, arrs, t2, [(fa_h, fa_l)], (p, w), shapes)
    d2, fb_h = lax.optimization_barrier((d2, fb_h))
    d3 = swap(d2, "batch", 1)
    arrs += [d2, d3]
    olds = [(fa_h, fa_l), (fb_h, fb_l)]
    z, v, co, near, far, pair, mid = phase(2, *common, arrs, t2, olds, (p, w), shapes)
    near = swap(near, "sky", 1)
    far = between(far, "sky")
    pair = swap(pair, "batch", 1)
    mid = between(mid, "batch")
    transfer = close(pos, w, v, z)
    image = blend(parity, co, (near, far, pair, mid), side)
    return (transfer.reshape(1, 1, -1, nout), image)


def solution(mesh):
    in_specs = (
        P("batch", "sky", None, None),
        P("batch", "sky", None, None),
        P("batch", "sky", None, None),
        P("batch", "sky", None),
        P("batch", "sky", None),
        P("batch", "sky"),
    )
    out_specs = (P("batch", "sky", None, None), P(None, "batch", "sky"))
    return jax.shard_map(local, mesh=mesh, in_specs=in_specs, out_specs=out_specs, check_vma=False)
```

time: 97.7 us -> 78.5 us (0.80)
  waiting for transfers between devices: 22.9 us -> 3.84 us
  Pallas kernels: 36.2 us -> 46.2 us
  starting transfers between devices: 24 us -> 18.4 us
  other arithmetic: 5.68 us -> 1.16 us
    ppermute x10 -> x12, waiting for transfers between devices: 14.8 us -> 3.83 us  [swap(): return lax.ppermute(value, axis, [(i, i ^ bit) for i in range(count)])]
    pallas_call x1 -> x7, Pallas kernels: 36.2 us -> 46.2 us  [the longest x3 41.2 us: phase(): pl.pallas_call(functools.partial(phase_kernel, done=done, narr=len(arrs),...]
    ppermute x1, waiting for transfers between devices: 7.66 us -> 0.01 us  [hop_two(): return lax.ppermute(value, 'sky', pairs)]
    ppermute x4 -> x2, starting transfers between devices: 12 us -> 5.53 us  [between(): return lax.ppermute(value, axis, pairs + [(j, i) for i, j in pairs])]
    unnamed x13 -> x17, local copies, waits for them, and re-layouts: 4.99 us -> 6.75 us
    reshape x2 -> x0, local copies, waits for them, and re-layouts: 1.62 us -> none  [the longest x1 0.9 us: local(): coadded = coadded.reshape(layers, side, side)]
    add x2 -> x1, other arithmetic: 2.06 us -> 0.69 us  [local(): names = 3 * (jnp.asarray(FLIP, jnp.int32) ^ batch_at) + column]
    unnamed x1 -> x0, other arithmetic: 1 us -> none
  transfers between devices with their start and end apart: 15 -> 15, of which waited for: 5 -> 4; matrix products, arithmetic and copies ran while one was open for 6% -> 4% of each run, Pallas kernels for 0% -> 35%
where the time goes in v2:
time: 78.5 us; the launch traced here: 77.8 us
  Pallas kernels  46.2 us (59%)
  starting transfers between devices  18.4 us (23%)
  local copies, waits for them, and re-layouts  6.75 us (9%)
  waiting for transfers between devices  3.84 us (5%)
  between operations  1.45 us (2%)
  other arithmetic  1.16 us (1%)
    pallas_call x3, Pallas kernels, phase(): pl.pallas_call(functools.partial(phase_kernel, done=done, narr=len(arrs),...  41.2 us
    ppermute x12, starting transfers between devices, swap(): return lax.ppermute(value, axis, [(i, i ^ bit) for i in range(count)])  9.68 us
    unnamed x17, local copies, waits for them, and re-layouts  6.75 us
    ppermute x2, starting transfers between devices, between(): return lax.ppermute(value, axis, pairs + [(j, i) for i, j in pairs])  5.53 us
    ppermute x12, waiting for transfers between devices, swap(): return lax.ppermute(value, axis, [(i, i ^ bit) for i in range(count)])  3.83 us
    ppermute x1, starting transfers between devices, hop_two(): return lax.ppermute(value, 'sky', pairs)  3.19 us
    pallas_call x1, Pallas kernels, close(): pl.pallas_call(close_kernel, out_shape=jax.ShapeDtypeStruct((before + n,...  2.22 us
    pallas_call x1, Pallas kernels, blend(): pl.pallas_call(blend_kernel, out_shape=jax.ShapeDtypeStruct((co.shape[0],...  1.72 us
  transfers between devices with their start and end apart: 15, of which 4 were waited for; matrix products, arithmetic and copies ran while one was open for 4% of the time, Pallas kernels for 35%

profile of v2, /device:TPU:9, one launch (start us, length us, event | category | flops | bytes accessed | tf_op | source)
XLA Modules:
  0.0 77.8 jit_solution(18209397359966137914)
XLA Ops:
  0.6 0.0 copy-start.1
  0.6 1.0 %copy-done.1 = f32[1,1,80,1024]{3,2,1,0:T(8,128)S(1)} copy-done((f32[1,1,80,1024]{3,2,1,0:T(8,128)S(1)}, f32[1,1,80,1024]{3,2,1,0:T(8,128)}, u32[]{:S(2)}) %copy-start.1) | copy-done | bytes 327704
  1.6 0.0 copy-start.2
  1.6 0.7 copy-done.2
  2.3 0.0 copy-start.3
  2.3 0.7 copy-done.3
  3.0 0.0 copy-start.7
  3.0 0.7 pack.1.refs_3_.refs_4_
  3.7 1.3 %collective-permute-start.2 = (f32[656,128]{1,0:T(8,128)S(1)}, f32[656,128]{1,0:T(8,128)S(1)}, u32[]{:S(2)}, u32[]{:S(2)}) collective-permute-start(f32[656,128]{1,0:T(8,128)S(1)} %pack.1.refs_3_.refs_4_), channel_id=1, source_target_pairs={{0,4},{4,0},{8,12},{12,8},{16,20},{20,16},{24,28},{28,24},{1,5},{5... | collective-permute-start | bytes 1007624 | tf_op jit(solution)/shard_map/ppermute | solution.py:588
  5.0 1.2 %collective-permute-start.1 = (f32[656,128]{1,0:T(8,128)S(1)}, f32[656,128]{1,0:T(8,128)S(1)}, u32[]{:S(2)}, u32[]{:S(2)}) collective-permute-start(f32[656,128]{1,0:T(8,128)S(1)} %pack.1.refs_3_.refs_4_), channel_id=1, source_target_pairs={{0,2},{1,3},{2,0},{3,1},{4,6},{5,7},{6,4},{7,5},{8,10},{9,11},{10,... | collective-permute-start | bytes 1007624 | tf_op jit(solution)/shard_map/ppermute | solution.py:588
  6.2 1.2 %collective-permute-start = (f32[656,128]{1,0:T(8,128)S(1)}, f32[656,128]{1,0:T(8,128)}, u32[]{:S(2)}, u32[]{:S(2)}) collective-permute-start(f32[656,128]{1,0:T(8,128)S(1)} %pack.1.refs_3_.refs_4_), channel_id=1, source_target_pairs={{0,1},{1,0},{2,3},{3,2},{4,5},{5,4},{6,7},{7,6},{8,9},{9,8},{10,11... | collective-permute-start | bytes 1007624 | tf_op jit(solution)/shard_map/ppermute | solution.py:588
  7.4 0.7 fusion.3
  8.8 0.0 copy-start
  8.8 1.7 %copy-done = f32[1,1,576,1024]{3,2,1,0:T(8,128)S(1)} copy-done((f32[1,1,576,1024]{3,2,1,0:T(8,128)S(1)}, f32[1,1,576,1024]{3,2,1,0:T(8,128)}, u32[]{:S(2)}) %copy-start) | copy-done | bytes 2359320
  10.4 0.3 halve.1
  10.8 0.0 copy-done.7
  10.8 0.2 fusion
  11.0 0.1 select_reduce_fusion
  11.1 1.4 %collective-permute-done.2.refs_6_.refs_7_ = f32[656,128]{1,0:T(8,128)S(1)} collective-permute-done((f32[656,128]{1,0:T(8,128)S(1)}, f32[656,128]{1,0:T(8,128)S(1)}, u32[]{:S(2)}, u32[]{:S(2)}) %collective-permute-start.2) | collective-permute-done | bytes 335904 | tf_op jit(solution)/shard_map/ppermute | solution.py:588
  12.5 1.5 %collective-permute-start.4 = (f32[656,128]{1,0:T(8,128)S(1)}, f32[656,128]{1,0:T(8,128)S(1)}, u32[]{:S(2)}, u32[]{:S(2)}) collective-permute-start(f32[656,128]{1,0:T(8,128)S(1)} %collective-permute-done.2.refs_6_.refs_7_), channel_id=1, source_target_pairs={{0,1},{1,0},{2,3},{3,2},{4,5},{5,4},{6,7},{7,6},{8,9},{9,8},{10,11... | collective-permute-start | bytes 1007624 | tf_op jit(solution)/shard_map/ppermute | solution.py:588
  14.0 0.0 collective-permute-done.1.refs_5_.refs_6_
  14.0 0.0 copy-start.4
  14.0 1.2 %collective-permute-start.3 = (f32[656,128]{1,0:T(8,128)S(1)}, f32[656,128]{1,0:T(8,128)S(1)}, u32[]{:S(2)}, u32[]{:S(2)}) collective-permute-start(f32[656,128]{1,0:T(8,128)S(1)} %collective-permute-done.1.refs_5_.refs_6_), channel_id=1, source_target_pairs={{0,1},{1,0},{2,3},{3,2},{4,5},{5,4},{6,7},{7,6},{8,9},{9,8},{10,11... | collective-permute-start | bytes 1007624 | tf_op jit(solution)/shard_map/ppermute | solution.py:588
  15.3 0.1 pad_add_fusion.refs_2_.odd_ref
  15.4 3.2 %collective-permute-start.6 = (f32[656,128]{1,0:T(8,128)S(1)}, f32[656,128]{1,0:T(8,128)S(1)}, u32[]{:S(2)}, u32[]{:S(2)}) collective-permute-start(f32[656,128]{1,0:T(8,128)S(1)} %collective-permute-done.2.refs_6_.refs_7_), channel_id=1, source_target_pairs={{0,8},{8,16},{16,24},{12,4},{20,12},{28,20},{1,9},{9,17},{17,25},{... | collective-permute-start | bytes 1007624 | tf_op jit(solution)/shard_map/ppermute | solution.py:600
  18.6 1.3 %collective-permute-start.5 = (f32[656,128]{1,0:T(8,128)S(1)}, f32[656,128]{1,0:T(8,128)S(1)}, u32[]{:S(2)}, u32[]{:S(2)}) collective-permute-start(f32[656,128]{1,0:T(8,128)S(1)} %collective-permute-done.2.refs_6_.refs_7_), channel_id=1, source_target_pairs={{0,2},{1,3},{2,0},{3,1},{4,6},{5,7},{6,4},{7,5},{8,10},{9,11},{10,... | collective-permute-start | bytes 1007624 | tf_op jit(solution)/shard_map/ppermute | solution.py:588
  19.8 0.0 collective-permute-done.refs_4_.refs_5_
  19.8 0.0 collective-permute-done.4.refs_8_.refs_9_
  19.8 0.0 collective-permute-done.3.refs_7_.refs_8_
  19.9 10.5 %phase0.1 = (bf16[240,1024]{1,0:T(8,128)(2,1)S(1)}, bf16[240,1024]{1,0:T(8,128)(2,1)S(1)}, f32[240,240]{1,0:T(8,128)S(1)}, f32[240,576]{1,0:T(8,128)S(1)}) custom-call(s32[12]{0:T(128)S(1)} %compare_select_fusion.1.refs_0_, f32[1,1]{1,0:T(1,128)S(6)} %copy.13.refs_1_, s32[2]{0:T(128)S(1)} %pad_add_fusion.refs_2_.odd_ref, ...), custom_call_target="tpu_custom_call" | custom-call | flops 6000000000 | bytes 4000000 | tf_op jit(solution)/shard_map/phase0/pallas_call | solution.py:492
  30.3 0.0 collective-permute-done.6.refs_10_.refs_11_
  30.3 0.0 collective-permute-done.5.refs_9_.refs_10_
  30.3 0.4 collective-permute-start.7
  30.8 0.2 collective-permute-start.8
  30.9 0.4 collective-permute-start.9
  31.3 0.7 collective-permute-done.7.refs_11_.refs_12_
  32.0 0.5 collective-permute-done.8.refs_12_.refs_13_
  32.5 0.0 copy-done.4
  32.5 0.0 copy-start.6
  32.5 14.0 %phase1.1 = (bf16[240,1024]{1,0:T(8,128)(2,1)S(1)}, bf16[240,1024]{1,0:T(8,128)(2,1)S(1)}, f32[480,480]{1,0:T(8,128)S(1)}, f32[480,576]{1,0:T(8,128)S(1)}) custom-call(s32[12]{0:T(128)S(1)} %compare_select_fusion.1.refs_0_, f32[1,1]{1,0:T(1,128)S(6)} %copy.13.refs_1_, s32[2]{0:T(128)S(1)} %pad_add_fusion.refs_2_.odd_ref, ...), custom_call_target="tpu_custom_call" | custom-call | flops 6000000000 | bytes 4000000 | tf_op jit(solution)/shard_map/phase1/pallas_call | solution.py:492
  46.5 0.0 collective-permute-done.9.refs_14_
  46.5 0.4 collective-permute-start.10
  46.9 0.1 fusion.1.pos_ref
  47.0 1.2 %collective-permute-done.10.refs_15_ = f32[656,128]{1,0:T(8,128)S(1)} collective-permute-done((f32[656,128]{1,0:T(8,128)S(1)}, f32[656,128]{1,0:T(8,128)S(1)}, u32[]{:S(2)}, u32[]{:S(2)}) %collective-permute-start.10) | collective-permute-done | bytes 335904 | tf_op jit(solution)/shard_map/ppermute | solution.py:588
  48.2 0.0 copy-done.6
  48.2 0.0 copy-start.5
  48.2 1.0 %copy-done.5 = f32[656,128]{1,0:T(8,128)S(1)} copy-done((f32[656,128]{1,0:T(8,128)S(1)}, f32[656,128]{1,0:T(8,128)}, u32[]{:S(2)}) %copy-start.5) | copy-done | bytes 335896
  49.2 16.8 %phase2.1 = (f32[240,576]{1,0:T(8,128)S(1)}, f32[480,240]{1,0:T(8,128)S(1)}, f32[16,576]{1,0:T(8,128)S(1)}, f32[16,576]{1,0:T(8,128)}, f32[16,576]{1,0:T(8,128)S...) custom-call(s32[12]{0:T(128)S(1)} %compare_select_fusion.1.refs_0_, f32[1,1]{1,0:T(1,128)S(6)} %copy.13.refs_1_, ...), custom_call_target="tpu_custom_call" | custom-call | flops 6000000000 | bytes 4000000 | tf_op jit(solution)/shard_map/phase2/pallas_call | solution.py:492
  66.0 0.4 collective-permute-start.13
  66.4 2.4 %collective-permute-start.14 = (f32[16,96]{1,0:T(8,128)S(1)}, f32[16,96]{1,0:T(8,128)S(1)}, u32[]{:S(2)}, u32[]{:S(2)}) collective-permute-start(f32[16,96]{1,0:T(8,128)S(1)} %get-tuple-element.45), channel_id=1, source_target_pairs={{1,2},{2,1},{5,6},{6,5},{9,10},{10,9},{13,14},{14,13},{17,18},{18,... | collective-permute-start | bytes 18440 | tf_op jit(solution)/shard_map/ppermute | solution.py:594
  68.8 0.1 collective-permute-start.11
  68.9 3.1 %collective-permute-start.12 = (f32[16,576]{1,0:T(8,128)S(1)}, f32[16,576]{1,0:T(8,128)S(1)}, u32[]{:S(2)}, u32[]{:S(2)}) collective-permute-start(f32[16,576]{1,0:T(8,128)S(1)} %get-tuple-element.43), channel_id=1, source_target_pairs={{4,8},{12,16},{20,24},{8,4},{16,12},{24,20},{5,9},{13,17},{21,25},... | collective-permute-start | bytes 110600 | tf_op jit(solution)/shard_map/ppermute | solution.py:594
  72.0 2.2 %close.1 = f32[720,576]{1,0:T(8,128)S(1)} custom-call(s32[9]{0:T(128)S(1)} %fusion.1.pos_ref, f32[480,576]{1,0:T(8,128)S(1)} %get-tuple-element.33.refs_23_.w_in, f32[480,240]{1,0:T(8,128)S(1)} %get-tuple-element.39.v_in, f32[240,576]{1,0:T(8,128)S(1)} %get-tuple-element.40.z_in), custom_call_target="tpu_custom_call" | custom-call | flops 500000000 | bytes 6000000 | tf_op jit(solution)/shard_map/close/pallas_call | solution.py:541
  74.3 1.8 %copy.12 = f32[1,1,720,576]{2,3,1,0:T(8,128)} copy(f32[1,1,720,576]{3,2,1,0:T(8,128)S(1)} %bitcast.4) | data formatting | bytes 3317760
  76.0 0.0 collective-permute-done.13.pair_ref
  76.0 0.0 collective-permute-done.14.mid_ref
  76.0 0.0 collective-permute-done.11.near_ref
  76.0 0.0 collective-permute-done.12.far_ref
  76.1 1.7 %blend.1 = f32[16,24,24]{2,1,0:T(8,128)} custom-call(s32[2]{0:T(128)S(1)} %pad_add_fusion.refs_2_.odd_ref, f32[16,576]{1,0:T(8,128)S(1)} %get-tuple-element.41.co_ref, f32[16,576]{1,0:T(8,128)S(1)} %collective-permute-done.11.near_ref, f32[16,576]{1,0:T(8,128)S(1)} %collective-permute-done.12.far_ref, f32[16,96]{1,0:T(8,128)S(1)} %collective-permute-done.13.pair_ref, ...), custom_call_target="tpu_custom_call" | custom-call | tf_op jit(solution)/shard_map/blend/pallas_call | solution.py:576
  (1 shorter events, 0.0 us)
Async XLA Ops:
  0.6 1.0 %copy-start.1 = (f32[1,1,80,1024]{3,2,1,0:T(8,128)S(1)}, f32[1,1,80,1024]{3,2,1,0:T(8,128)}, u32[]{:S(2)}) copy-start(f32[1,1,80,1024]{3,2,1,0:T(8,128)} %feat_in.1) | copy-start | bytes 983044
  1.6 0.7 copy-start.2
  2.3 0.7 copy-start.3
  3.0 7.8 %copy-start.7 = (s32[1,1,9]{2,1,0:T(1,128)S(1)}, s32[1,1,9]{2,1,0:T(1,128)}, u32[]{:S(2)}) copy-start(s32[1,1,9]{2,1,0:T(1,128)} %param.13) | copy-start | bytes 112
  3.7 8.8 %collective-permute-start.2 = (f32[656,128]{1,0:T(8,128)S(1)}, f32[656,128]{1,0:T(8,128)S(1)}, u32[]{:S(2)}, u32[]{:S(2)}) collective-permute-start(f32[656,128]{1,0:T(8,128)S(1)} %pack.1.refs_3_.refs_4_), channel_id=1, source_target_pairs={{0,4},{4,0},{8,12},{12,8},{16,20},{20,16},{24,28},{28,24},{1,5},{5... | collective-permute-start | bytes 1007624 | tf_op jit(solution)/shard_map/ppermute | solution.py:588
  5.0 9.1 %collective-permute-start.1 = (f32[656,128]{1,0:T(8,128)S(1)}, f32[656,128]{1,0:T(8,128)S(1)}, u32[]{:S(2)}, u32[]{:S(2)}) collective-permute-start(f32[656,128]{1,0:T(8,128)S(1)} %pack.1.refs_3_.refs_4_), channel_id=1, source_target_pairs={{0,2},{1,3},{2,0},{3,1},{4,6},{5,7},{6,4},{7,5},{8,10},{9,11},{10,... | collective-permute-start | bytes 1007624 | tf_op jit(solution)/shard_map/ppermute | solution.py:588
  6.2 13.7 %collective-permute-start = (f32[656,128]{1,0:T(8,128)S(1)}, f32[656,128]{1,0:T(8,128)}, u32[]{:S(2)}, u32[]{:S(2)}) collective-permute-start(f32[656,128]{1,0:T(8,128)S(1)} %pack.1.refs_3_.refs_4_), channel_id=1, source_target_pairs={{0,1},{1,0},{2,3},{3,2},{4,5},{5,4},{6,7},{7,6},{8,9},{9,8},{10,11... | collective-permute-start | bytes 1007624 | tf_op jit(solution)/shard_map/ppermute | solution.py:588
  8.8 1.7 %copy-start = (f32[1,1,576,1024]{3,2,1,0:T(8,128)S(1)}, f32[1,1,576,1024]{3,2,1,0:T(8,128)}, u32[]{:S(2)}) copy-start(f32[1,1,576,1024]{3,2,1,0:T(8,128)} %t_ref.1) | copy-start | bytes 7077892
  12.5 7.3 %collective-permute-start.4 = (f32[656,128]{1,0:T(8,128)S(1)}, f32[656,128]{1,0:T(8,128)S(1)}, u32[]{:S(2)}, u32[]{:S(2)}) collective-permute-start(f32[656,128]{1,0:T(8,128)S(1)} %collective-permute-done.2.refs_6_.refs_7_), channel_id=1, source_target_pairs={{0,1},{1,0},{2,3},{3,2},{4,5},{5,4},{6,7},{7,6},{8,9},{9,8},{10,11... | collective-permute-start | bytes 1007624 | tf_op jit(solution)/shard_map/ppermute | solution.py:588
  14.0 18.5 %copy-start.4 = (f32[656,128]{1,0:T(8,128)}, f32[656,128]{1,0:T(8,128)S(1)}, u32[]{:S(2)}) copy-start(f32[656,128]{1,0:T(8,128)S(1)} %collective-permute-done.1.refs_5_.refs_6_) | copy-start | bytes 1007620
  14.0 5.8 %collective-permute-start.3 = (f32[656,128]{1,0:T(8,128)S(1)}, f32[656,128]{1,0:T(8,128)S(1)}, u32[]{:S(2)}, u32[]{:S(2)}) collective-permute-start(f32[656,128]{1,0:T(8,128)S(1)} %collective-permute-done.1.refs_5_.refs_6_), channel_id=1, source_target_pairs={{0,1},{1,0},{2,3},{3,2},{4,5},{5,4},{6,7},{7,6},{8,9},{9,8},{10,11... | collective-permute-start | bytes 1007624 | tf_op jit(solution)/shard_map/ppermute | solution.py:588
  15.4 15.0 %collective-permute-start.6 = (f32[656,128]{1,0:T(8,128)S(1)}, f32[656,128]{1,0:T(8,128)S(1)}, u32[]{:S(2)}, u32[]{:S(2)}) collective-permute-start(f32[656,128]{1,0:T(8,128)S(1)} %collective-permute-done.2.refs_6_.refs_7_), channel_id=1, source_target_pairs={{0,8},{8,16},{16,24},{12,4},{20,12},{28,20},{1,9},{9,17},{17,25},{... | collective-permute-start | bytes 1007624 | tf_op jit(solution)/shard_map/ppermute | solution.py:600
  18.6 11.8 %collective-permute-start.5 = (f32[656,128]{1,0:T(8,128)S(1)}, f32[656,128]{1,0:T(8,128)S(1)}, u32[]{:S(2)}, u32[]{:S(2)}) collective-permute-start(f32[656,128]{1,0:T(8,128)S(1)} %collective-permute-done.2.refs_6_.refs_7_), channel_id=1, source_target_pairs={{0,2},{1,3},{2,0},{3,1},{4,6},{5,7},{6,4},{7,5},{8,10},{9,11},{10,... | collective-permute-start | bytes 1007624 | tf_op jit(solution)/shard_map/ppermute | solution.py:588
  30.3 1.7 %collective-permute-start.7 = (f32[656,128]{1,0:T(8,128)S(1)}, f32[656,128]{1,0:T(8,128)S(1)}, u32[]{:S(2)}, u32[]{:S(2)}) collective-permute-start(f32[656,128]{1,0:T(8,128)S(1)} %collective-permute-done.5.refs_9_.refs_10_), channel_id=1, source_target_pairs={{0,1},{1,0},{2,3},{3,2},{4,5},{5,4},{6,7},{7,6},{8,9},{9,8},{10,11... | collective-permute-start | bytes 1007624 | tf_op jit(solution)/shard_map/ppermute | solution.py:588
  30.8 1.8 %collective-permute-start.8 = (f32[656,128]{1,0:T(8,128)S(1)}, f32[656,128]{1,0:T(8,128)S(1)}, u32[]{:S(2)}, u32[]{:S(2)}) collective-permute-start(f32[656,128]{1,0:T(8,128)S(1)} %collective-permute-done.6.refs_10_.refs_11_), channel_id=1, source_target_pairs={{0,1},{1,0},{2,3},{3,2},{4,5},{5,4},{6,7},{7,6},{8,9},{9,8},{10,11... | collective-permute-start | bytes 1007624 | tf_op jit(solution)/shard_map/ppermute | solution.py:588
  30.9 15.6 %collective-permute-start.9 = (f32[656,128]{1,0:T(8,128)S(1)}, f32[656,128]{1,0:T(8,128)S(1)}, u32[]{:S(2)}, u32[]{:S(2)}) collective-permute-start(f32[656,128]{1,0:T(8,128)S(1)} %collective-permute-done.6.refs_10_.refs_11_), channel_id=1, source_target_pairs={{0,2},{1,3},{2,0},{3,1},{4,6},{5,7},{6,4},{7,5},{8,10},{9,11},{10,... | collective-permute-start | bytes 1007624 | tf_op jit(solution)/shard_map/ppermute | solution.py:588
  32.5 15.7 %copy-start.6 = (f32[4,576]{1,0:T(4,128)S(1)}, f32[4,576]{1,0:T(4,128)}, u32[]{:S(2)}) copy-start(f32[4,576]{1,0:T(4,128)} %constant.43.clone.refs_3_) | copy-start | bytes 27652
  46.5 1.7 %collective-permute-start.10 = (f32[656,128]{1,0:T(8,128)S(1)}, f32[656,128]{1,0:T(8,128)S(1)}, u32[]{:S(2)}, u32[]{:S(2)}) collective-permute-start(f32[656,128]{1,0:T(8,128)S(1)} %collective-permute-done.9.refs_14_), channel_id=1, source_target_pairs={{0,1},{1,0},{2,3},{3,2},{4,5},{5,4},{6,7},{7,6},{8,9},{9,8},{10,11... | collective-permute-start | bytes 1007624 | tf_op jit(solution)/shard_map/ppermute | solution.py:588
  48.2 1.0 %copy-start.5 = (f32[656,128]{1,0:T(8,128)S(1)}, f32[656,128]{1,0:T(8,128)}, u32[]{:S(2)}) copy-start(f32[656,128]{1,0:T(8,128)} %copy-done.4) | copy-start | bytes 1007620
  66.0 10.1 %collective-permute-start.13 = (f32[16,96]{1,0:T(8,128)}, f32[16,96]{1,0:T(8,128)S(1)}, u32[]{:S(2)}, u32[]{:S(2)}) collective-permute-start(f32[16,96]{1,0:T(8,128)} %get-tuple-element.44), channel_id=1, source_target_pairs={{0,1},{1,0},{2,3},{3,2},{4,5},{5,4},{6,7},{7,6},{8,9},{9,8},{10,11... | collective-permute-start | bytes 18440 | tf_op jit(solution)/shard_map/ppermute | solution.py:588
  66.4 9.6 %collective-permute-start.14 = (f32[16,96]{1,0:T(8,128)S(1)}, f32[16,96]{1,0:T(8,128)S(1)}, u32[]{:S(2)}, u32[]{:S(2)}) collective-permute-start(f32[16,96]{1,0:T(8,128)S(1)} %get-tuple-element.45), channel_id=1, source_target_pairs={{1,2},{2,1},{5,6},{6,5},{9,10},{10,9},{13,14},{14,13},{17,18},{18,... | collective-permute-start | bytes 18440 | tf_op jit(solution)/shard_map/ppermute | solution.py:594
  68.8 7.2 %collective-permute-start.11 = (f32[16,576]{1,0:T(8,128)}, f32[16,576]{1,0:T(8,128)S(1)}, u32[]{:S(2)}, u32[]{:S(2)}) collective-permute-start(f32[16,576]{1,0:T(8,128)} %get-tuple-element.42), channel_id=1, source_target_pairs={{0,4},{4,0},{8,12},{12,8},{16,20},{20,16},{24,28},{28,24},{1,5},{5... | collective-permute-start | bytes 110600 | tf_op jit(solution)/shard_map/ppermute | solution.py:588
  68.9 7.2 %collective-permute-start.12 = (f32[16,576]{1,0:T(8,128)S(1)}, f32[16,576]{1,0:T(8,128)S(1)}, u32[]{:S(2)}, u32[]{:S(2)}) collective-permute-start(f32[16,576]{1,0:T(8,128)S(1)} %get-tuple-element.43), channel_id=1, source_target_pairs={{4,8},{12,16},{20,24},{8,4},{16,12},{24,20},{5,9},{13,17},{21,25},... | collective-permute-start | bytes 110600 | tf_op jit(solution)/shard_map/ppermute | solution.py:594

commit v3 on v2

--- a/solution.py
+++ b/solution.py
@@ -37,46 +37,56 @@
 def panel_sweep(rows, q, sub, lane):
     base = q * SUB
     p = rows[q]
-    cols = [
-        jnp.where(lane >= 0, jnp.broadcast_to(p[:, base + k : base + k + 1], (SUB, LANE)), 0.0)
-        for k in range(SUB)
-    ]
+    wide = lambda x: jnp.broadcast_to(x, (SUB, LANE))
+    cols = [jnp.where(lane >= 0, wide(p[:, base + k : base + k + 1]), 0.0) for k in range(SUB)]
     inside = (lane >= base) & (lane < base + SUB)
     w = jnp.where(inside, jnp.where(lane - base == sub, 1.0, 0.0).astype(f32), p)
-    for k in range(SUB):
-        here = sub == k
-        inv = 1.0 / jnp.broadcast_to(cols[k][k : k + 1, :], (SUB, LANE))
-        h = jnp.where(here, -1.0, cols[k])
-        for m in range(k + 1, SUB):
-            r = jnp.broadcast_to(cols[m][k : k + 1, :], (SUB, LANE))
-            cols[m] = jnp.where(here, 0.0, cols[m]) - (h * r) * inv
-        r = jnp.broadcast_to(w[k : k + 1, :], (SUB, LANE))
-        w = jnp.where(here, 0.0, w) - (h * r) * inv
-    wk = [jnp.broadcast_to(w[k : k + 1, :], (SUB, LANE)) for k in range(SUB)]
+    for k in range(0, SUB, 2):
+        first, second = sub == k, sub == k + 1
+        both = first | second
+        a, d = wide(cols[k][k : k + 1]), wide(cols[k][k + 1 : k + 2])
+        b, c = wide(cols[k + 1][k : k + 1]), wide(cols[k + 1][k + 1 : k + 2])
+        r = 1.0 / (a * c - b * d)
+        h1 = jnp.where(first, -1.0, jnp.where(second, 0.0, cols[k]))
+        h2 = jnp.where(second, -1.0, jnp.where(first, 0.0, cols[k + 1]))
+
+        def step(x):
+            r1, r2 = wide(x[k : k + 1]), wide(x[k + 1 : k + 2])
+            t = h1 * (c * r1 - b * r2) + h2 * (a * r2 - d * r1)
+            return jnp.where(both, 0.0, x) - t * r
+
+        for m in range(k + 2, SUB):
+            cols[m] = step(cols[m])
+        w = step(w)
+    wk = [wide(w[k : k + 1]) for k in range(SUB)]
     count = len(rows)
     res = [None] * count
-    for step in range(count):
-        g = (q + 1 + step) % count
+    for step_at in range(count):
+        g = (q + 1 + step_at) % count
         if g == q:
             res[g] = w
             continue
-        a = rows[g]
-        acc = [jnp.where(inside, 0.0, a), None]
-        for k in range(SUB):
-            t = jnp.broadcast_to(a[:, base + k : base + k + 1], (SUB, LANE)) * wk[k]
-            s = k % 2
-            acc[s] = (acc[s] - t) if acc[s] is not None else -t
-        res[g] = acc[0] + acc[1]
+        x = rows[g]
+        terms = [wide(x[:, base + k : base + k + 1]) * wk[k] for k in range(SUB)]
+        while len(terms) > 1:
+            terms = [terms[i] + terms[i + 1] for i in range(0, len(terms), 2)]
+        res[g] = jnp.where(inside, 0.0, x) - terms[0]
     return res
 
 
-def pack_kernel(mask_ref, feat_in, img_in, out_ref, feat_ref, img_ref, sems):
-    npix, feat = feat_ref.shape
+def pack_kernel(mask_ref, feat_in, img_in, out_ref, img_ref, sems):
+    npix, feat = feat_in.shape[2:]
     layers = img_ref.shape[0]
     blocks = feat // LANE
+    first = pltpu.make_async_copy(img_in.at[0, 0], img_ref, sems.at[blocks])
+    first.start()
     loads = [
-        pltpu.make_async_copy(feat_in.at[0, 0], feat_ref, sems.at[0]),
-        pltpu.make_async_copy(img_in.at[0, 0], img_ref, sems.at[1]),
+        pltpu.make_async_copy(
+            feat_in.at[0, 0, :, pl.ds(c * LANE, LANE)],
+            out_ref.at[pl.ds(c * npix, npix)],
+            sems.at[c],
+        )
+        for c in range(blocks)
     ]
     for cp in loads:
         cp.start()
@@ -84,13 +94,12 @@
     keep = jnp.zeros((layers, npix), f32)
     for i in range(layers):
         keep = jnp.where(row == i, mask_ref[0, 0, i].astype(f32), keep)
+    tail = blocks * npix
+    out_ref[tail : tail + layers, :] = jnp.zeros((layers, LANE), f32)
+    first.wait()
+    out_ref[tail : tail + layers, 0:npix] = img_ref[...] * keep
     for cp in loads:
         cp.wait()
-    for c in range(blocks):
-        out_ref[c * npix : (c + 1) * npix, :] = feat_ref[:, c * LANE : (c + 1) * LANE]
-    tail = blocks * npix
-    out_ref[tail : tail + layers, :] = jnp.zeros((layers, LANE), f32)
-    out_ref[tail : tail + layers, 0:npix] = img_ref[...] * keep
 
 
 def pack(features, images, layer_mask):
@@ -98,19 +107,19 @@
     layers = images.shape[2]
     vm = pl.BlockSpec(memory_space=pltpu.VMEM)
     hb = pl.BlockSpec(memory_space=pltpu.HBM)
+    outside = lambda x: pltpu.with_memory_space_constraint(x, pltpu.HBM)
     return pl.pallas_call(
         pack_kernel,
         out_shape=jax.ShapeDtypeStruct((feat // LANE * npix + layers, LANE), f32),
         in_specs=[pl.BlockSpec(memory_space=pltpu.SMEM), hb, hb],
         out_specs=vm,
         scratch_shapes=[
-            pltpu.VMEM((npix, feat), f32),
             pltpu.VMEM((layers, npix), f32),
-            pltpu.SemaphoreType.DMA((2,)),
+            pltpu.SemaphoreType.DMA((feat // LANE + 1,)),
         ],
         compiler_params=pltpu.CompilerParams(vmem_limit_bytes=8 << 20),
         name="pack",
-    )(layer_mask, features, images)
+    )(outside(layer_mask), outside(features), outside(images))
 
 
 def halve_kernel(t_ref, hi_ref, lo_ref):
@@ -153,119 +162,63 @@
     rank_ref, ridge_ref, odd_ref = take(3)
     if last:
         (mask_ref,) = take(1)
-    arrs = take(narr)
-    t_in = take(2)
-    old_in = [tuple(take(2)) for _ in done]
-    p_in, w_in = take(2) if done else (None, None)
+    arrs = dict(zip(range(sum(done), narr), take(narr - sum(done))))
+    th, tl = take(2)
+    old = [tuple(take(2)) for _ in done]
+    old_p, old_w = take(2) if done else (None, None)
     e = sum(done)
-    if last:
-        z_out, v_out, co_ref, near_ref, far_ref, pair_ref, mid_ref = take(7)
+    old_img = take(len(done)) if last else []
+    if last:
+        r_ref, v_ref, co_ref, near_ref, far_ref, pair_ref, mid_ref = take(7)
+        fh_ref, fl_ref, s_ref, d_ref, img_ref = take(5)
     else:
-        fh_out, fl_out, p_out, w_out = take(4)
-    fsel, fh_ref, fl_ref, s_ref, d_ref, r_ref, th, tl = take(8)
-    sems, sem = take(2)
-    l = fsel.shape[0]
-    n = l * npix
+        fh_ref, fl_ref, p_ref, w_ref, img_ref = take(5)
+        s_ref, d_ref, r_ref = take(3)
+        if done:
+            (v_ref,) = take(1)
+    n = fh_ref.shape[0]
+    l = n // npix
     before = e * npix
-    if not last:
-        p_ref, w_ref = take(2)
-    else:
-        img_ref, img_sems = take(2)
-    if done:
-        old = [tuple(take(2)) for _ in done]
-        old_p, old_w, v_ref = take(3)
     feat_blocks = fh_ref.shape[1] // LANE
     body = feat_blocks * npix
 
-    def picks(t):
+    for t in arrs:
         r = rank_ref[t]
-        return r, (r >= e) & (r < e + l)
-
-    def copy(t, r):
-        return pltpu.make_async_copy(arrs[t], fsel.at[r - e], sems.at[t])
-
-    def copy_img(t, r):
-        return pltpu.make_async_copy(arrs[t].at[pl.ds(body, layers)], img_ref.at[r], img_sems.at[t])
-
-    for t in range(narr):
-        r, hit = picks(t)
-
-        @pl.when(hit)
+
+        @pl.when((r >= e) & (r < e + l))
         def _():
-            copy(t, r).start()
-
-    pairs = []
-    for src, dst in zip(old_in, old if done else []):
-        pairs += [(src[0], dst[0]), (src[1], dst[1])]
-    early = len(pairs)
-    if done:
-        pairs += [(p_in, old_p), (w_in, old_w)]
-    pairs += [(t_in[0], th), (t_in[1], tl)]
-    loads = [pltpu.make_async_copy(x, y, sem.at[i]) for i, (x, y) in enumerate(pairs)]
-    for cp in loads:
-        cp.start()
-    if last:
-        for t in range(narr):
-            r = rank_ref[t]
-
-            @pl.when(r >= 0)
-            def _():
-                copy_img(t, r).start()
-
-    for t in range(narr):
-        r, hit = picks(t)
-
-        @pl.when(hit)
-        def _():
-            copy(t, r).wait()
-
-    for i in range(l):
-        for c in range(feat_blocks):
-            hi, lo = split2(fsel[i, c * npix : (c + 1) * npix, :])
-            fh_ref[i * npix : (i + 1) * npix, c * LANE : (c + 1) * LANE] = hi
-            fl_ref[i * npix : (i + 1) * npix, c * LANE : (c + 1) * LANE] = lo
-    stores = []
-    at = len(pairs)
-    if not last:
-        stores = [
-            pltpu.make_async_copy(fh_ref, fh_out, sem.at[at]),
-            pltpu.make_async_copy(fl_ref, fl_out, sem.at[at + 1]),
-        ]
-        for cp in stores:
-            cp.start()
-    first = early + (1 if done else 0)
-    for cp in loads[:first]:
-        cp.wait()
-    mine = (fh_ref[...], fl_ref[...])
+            to = pl.ds(pl.multiple_of((r - e) * npix, 2 * SUB), npix)
+            for c in range(feat_blocks):
+                hi, lo = split2(arrs[t][c * npix : (c + 1) * npix, :])
+                fh_ref[to, c * LANE : (c + 1) * LANE] = hi
+                fl_ref[to, c * LANE : (c + 1) * LANE] = lo
+            img_ref[r - e] = arrs[t][body : body + layers, :]
+
+
+    mine_h, mine_l = fh_ref[...], fl_ref[...]
     ridge = ridge_ref[0, 0]
     sub = lax.broadcasted_iota(jnp.int32, (SUB, LANE), 0)
     lane = lax.broadcasted_iota(jnp.int32, (SUB, LANE), 1)
-    system = dot3(mine, mine, True)
+    pieces = []
+    for xh, xl in old + [(fh_ref, fl_ref)]:
+        xh, xl = xh[...], xl[...]
+        both = dot(jnp.concatenate([xh, xl], axis=0), mine_h, True)
+        pieces.append(both[: xh.shape[0]] + (both[xh.shape[0] :] + dot(xh, mine_l, True)))
+    system = pieces[-1]
     cross = []
     if done:
         tops = [sum(done[:i]) * npix for i in range(len(done) + 1)]
-        parts = [(x[...], y[...]) for x, y in old]
-        gel = jnp.concatenate([dot3(part, mine, True) for part in parts], axis=0)
+        gel = jnp.concatenate(pieces[:-1], axis=0)
         v = dot3(split2(old_p[...]), split2(gel))
         v_ref[...] = v
-        for i, part in enumerate(parts):
-            g = split2(dot3(mine, part, True))
-            cross.append((slice(tops[i], tops[i + 1]), g))
+        for i in range(len(done)):
+            rows = slice(tops[i], tops[i + 1])
+            cross.append((rows, split2(gel[rows].T)))
         for rows, g in cross:
-            system = system - dot3(g, split2(v[rows, :]))
+            system = system - dot3(g, split2(v[rows]))
     d_ref[:, 0:npix] = system[0:npix, 0:npix]
     for c in range(l):
         s_ref[c, :, 0:npix] = system[:, c * npix : (c + 1) * npix]
-
-    for cp in loads[first:]:
-        cp.wait()
-    if last:
-        for t in range(narr):
-            r = rank_ref[t]
-
-            @pl.when(r >= 0)
-            def _():
-                copy_img(t, r).wait()
 
     work = []
     feat = feat_blocks * LANE
@@ -287,27 +240,29 @@
 
     picture = {}
     if last:
+        faces = [ref[i][:, 0:npix] for ref, count in zip(old_img, done) for i in range(count)]
+        faces += [img_ref[i][:, 0:npix] for i in range(l)]
 
         def base(cut):
             total = None
             for i in range(e):
                 part = dot(
-                    stack_left(img_ref[i][:, 0:npix]), stack_right(old_w[i * npix : (i + 1) * npix, cut])
+                    stack_left(faces[i]), stack_right(old_w[i * npix : (i + 1) * npix, cut])
                 )
                 total = part if total is None else total + part
             picture[cut.start] = total
 
         def effective():
-            ours = jnp.concatenate([img_ref[e + i][:, 0:npix] for i in range(l)], axis=1)
+            ours = jnp.concatenate(faces[e:], axis=1)
             for i in range(e):
                 ours = ours - dot(
-                    stack_left(img_ref[i][:, 0:npix]), stack_right(v_ref[i * npix : (i + 1) * npix, :])
+                    stack_left(faces[i]), stack_right(v_ref[i * npix : (i + 1) * npix, :])
                 )
             picture["rest"] = split2(ours)
 
-        for cut in chunks(nout):
-            work.append(functools.partial(base, cut))
-        work.append(effective)
+        later = [functools.partial(base, cut) for cut in chunks(nout)] + [effective]
+    else:
+        later = []
 
     def update(c, coef, d, j):
         rows = slice(j * npix, (j + 1) * npix)
@@ -354,22 +309,16 @@
             work.append(functools.partial(update_right, coef, d, j, part))
         if not last:
             work.append(functools.partial(update_own, coef, full, j))
+        work += later
+        later = []
     while work:
         work.pop(0)()
     z = r_ref[...]
     z2 = split2(z)
     if last:
-        stores = [
-            pltpu.make_async_copy(r_ref, z_out, sem.at[at]),
-            pltpu.make_async_copy(v_ref, v_out, sem.at[at + 1]),
-        ]
-        for cp in stores:
-            cp.start()
         base_total = jnp.concatenate([picture[cut.start] for cut in chunks(nout)], axis=1)
         total = base_total + dot3(picture["rest"], z2)
         send(total, co_ref, near_ref, far_ref, pair_ref, mid_ref, mask_ref, odd_ref, side)
-        for cp in stores:
-            cp.wait()
         return
     q_flat = jnp.concatenate([s_ref[c, :, 0:npix] for c in range(l)], axis=1)
     w_ref[before : before + n, :] = z
@@ -384,14 +333,6 @@
         p_ref[before : before + n, :] = jnp.concatenate([-second, q_flat], axis=1)
     else:
         p_ref[...] = q_flat
-    more = [
-        pltpu.make_async_copy(p_ref, p_out, sem.at[at + 2]),
-        pltpu.make_async_copy(w_ref, w_out, sem.at[at + 3]),
-    ]
-    for cp in more:
-        cp.start()
-    for cp in stores + more:
-        cp.wait()
 
 
 def send(total, co_ref, near_ref, far_ref, pair_ref, mid_ref, mask_ref, odd_ref, side):
@@ -423,7 +364,7 @@
     return masks
 
 
-def phase(number, rank, ridge, odd, masks, arrs, t2, old, state, shapes):
+def phase(number, rank, ridge, odd, masks, arrs, t2, old, state, faces, shapes):
     npix, layers, nout, side, feat = shapes
     done = PHASES[:number]
     l = PHASES[number]
@@ -432,18 +373,18 @@
     n, size = l * npix, (e + l) * npix
     vm = pl.BlockSpec(memory_space=pltpu.VMEM)
     sm = pl.BlockSpec(memory_space=pltpu.SMEM)
-    hb = pl.BlockSpec(memory_space=pltpu.HBM)
     args = [rank, ridge, odd]
     specs = [sm, sm, sm]
     if last:
         args += [masks]
-        specs += [vm]
-    args += list(arrs) + list(t2)
+    args += list(arrs[e:]) + list(t2)
     for pair in old:
         args += list(pair)
     if done:
         args += list(state)
-    specs += [hb] * (len(args) - len(specs))
+    if last:
+        args += list(faces)
+    specs += [vm] * (len(args) - len(specs))
     real = lambda *shape: jax.ShapeDtypeStruct(shape, f32)
     half = jax.ShapeDtypeStruct((n, feat), bf16)
     if last:
@@ -456,39 +397,18 @@
             real(layers, FADE * side),
             real(layers, FADE * side),
         )
-        out_specs = (hb, hb, vm, vm, vm, vm, vm)
+        scratch = [pltpu.VMEM((n, feat), bf16)] * 2
     else:
-        outs = (half, half, real(size, size), real(size, nout))
-        out_specs = (hb, hb, hb, hb)
-    fh = pltpu.VMEM((n, feat), bf16)
-    tgt = pltpu.VMEM((nout, feat), bf16)
-    scratch = [
-        pltpu.VMEM((l,) + arrs[0].shape, f32),
-        fh,
-        fh,
-        pltpu.VMEM((l, n, LANE), f32),
-        pltpu.VMEM((npix, LANE), f32),
-        pltpu.VMEM((n, nout), f32),
-        tgt,
-        tgt,
-        pltpu.SemaphoreType.DMA((len(arrs),)),
-        pltpu.SemaphoreType.DMA((2 * len(done) + 8,)),
-    ]
-    if last:
-        scratch += [
-            pltpu.VMEM((e + l, layers, LANE), f32),
-            pltpu.SemaphoreType.DMA((len(arrs),)),
-        ]
+        outs = (half, half, real(size, size), real(size, nout), real(l, layers, LANE))
+        scratch = []
+    scratch += [pltpu.VMEM((l, n, LANE), f32), pltpu.VMEM((npix, LANE), f32)]
+    if last:
+        scratch += [pltpu.VMEM((l, layers, LANE), f32)]
     else:
-        scratch += [pltpu.VMEM((size, size), f32), pltpu.VMEM((size, nout), f32)]
-    if done:
-        for count in done:
-            scratch += [pltpu.VMEM((count * npix, feat), bf16)] * 2
-        scratch += [
-            pltpu.VMEM((e * npix, e * npix), f32),
-            pltpu.VMEM((e * npix, nout), f32),
-            pltpu.VMEM((e * npix, n), f32),
-        ]
+        scratch += [pltpu.VMEM((n, nout), f32)]
+        if done:
+            scratch += [pltpu.VMEM((e * npix, n), f32)]
+    out_specs = tuple(vm for _ in outs)
     return pl.pallas_call(
         functools.partial(
             phase_kernel,
@@ -504,7 +424,7 @@
         in_specs=specs,
         out_specs=out_specs,
         scratch_shapes=scratch,
-        compiler_params=pltpu.CompilerParams(vmem_limit_bytes=40 << 20),
+        compiler_params=pltpu.CompilerParams(vmem_limit_bytes=16 << 20),
         cost_estimate=pl.CostEstimate(
             flops=2_000_000_000 * l, transcendentals=0, bytes_accessed=4_000_000
         ),
@@ -512,22 +432,14 @@
     )(*args)
 
 
-def close_kernel(pos_ref, w_in, v_in, z_in, out_ref, w_ref, v_ref, x_ref, sems):
+def close_kernel(pos_ref, w_ref, v_ref, z_ref, out_ref, x_ref):
     before = w_ref.shape[0]
-    n = z_in.shape[0]
+    n = z_ref.shape[0]
     count = pos_ref.shape[0]
     npix = (before + n) // count
-    loads = [
-        pltpu.make_async_copy(v_in, v_ref, sems.at[0]),
-        pltpu.make_async_copy(z_in, x_ref.at[pl.ds(before, n)], sems.at[1]),
-        pltpu.make_async_copy(w_in, w_ref, sems.at[2]),
-    ]
-    for cp in loads:
-        cp.start()
-    for cp in loads:
-        cp.wait()
-    z2 = split2(x_ref[before : before + n, :])
-    x_ref[0:before, :] = w_ref[...] - dot3(split2(v_ref[...]), z2)
+    z = z_ref[...]
+    x_ref[before : before + n, :] = z
+    x_ref[0:before, :] = w_ref[...] - dot3(split2(v_ref[...]), split2(z))
     for i in range(count):
         src = pl.multiple_of(pos_ref[i] * npix, SUB)
         out_ref[i * npix : (i + 1) * npix, :] = x_ref[pl.ds(src, npix), :]
@@ -536,19 +448,13 @@
 def close(pos, w, v, z):
     before, nout = w.shape
     n = z.shape[0]
-    hb = pl.BlockSpec(memory_space=pltpu.HBM)
     vm = pl.BlockSpec(memory_space=pltpu.VMEM)
     return pl.pallas_call(
         close_kernel,
         out_shape=jax.ShapeDtypeStruct((before + n, nout), f32),
-        in_specs=[pl.BlockSpec(memory_space=pltpu.SMEM), hb, hb, hb],
+        in_specs=[pl.BlockSpec(memory_space=pltpu.SMEM), vm, vm, vm],
         out_specs=vm,
-        scratch_shapes=[
-            pltpu.VMEM((before, nout), f32),
-            pltpu.VMEM((before, n), f32),
-            pltpu.VMEM((before + n, nout), f32),
-            pltpu.SemaphoreType.DMA((3,)),
-        ],
+        scratch_shapes=[pltpu.VMEM((before + n, nout), f32)],
         compiler_params=pltpu.CompilerParams(vmem_limit_bytes=20 << 20),
         cost_estimate=pl.CostEstimate(
             flops=500_000_000, transcendentals=0, bytes_accessed=6_000_000
@@ -632,18 +538,20 @@
     a3 = swap(a2, "batch", 1)
     n1 = swap(n0, "batch", 1)
     arrs = [own, a1, a2, n0, a3, n1]
-    fa_h, fa_l, p, w = phase(0, *common, arrs, t2, [], None, shapes)
+    fa_h, fa_l, p, w, ia = phase(0, *common, arrs, t2, [], None, [], shapes)
     n2, d0, fa_h = lax.optimization_barrier((n2, d0, fa_h))
     d2 = swap(d0, "batch", 2)
     n3 = swap(n2, "batch", 1)
     d1 = swap(d0, "batch", 1)
-    arrs += [n2, d0, n3, d1]
-    fb_h, fb_l, p, w = phase(1, *common, arrs, t2, [(fa_h, fa_l)], (p, w), shapes)
+    arrs += [n2, d0, n3]
+    fb_h, fb_l, p, w, ib = phase(1, *common, arrs, t2, [(fa_h, fa_l)], (p, w), [], shapes)
     d2, fb_h = lax.optimization_barrier((d2, fb_h))
     d3 = swap(d2, "batch", 1)
-    arrs += [d2, d3]
+    arrs += [d1, d2, d3]
     olds = [(fa_h, fa_l), (fb_h, fb_l)]
-    z, v, co, near, far, pair, mid = phase(2, *common, arrs, t2, olds, (p, w), shapes)
+    z, v, co, near, far, pair, mid = phase(
+        2, *common, arrs, t2, olds, (p, w), [ia, ib], shapes
+    )
     near = swap(near, "sky", 1)
     far = between(far, "sky")
     pair = swap(pair, "batch", 1)

time: 78.5 us -> 62.5 us (0.80)
  Pallas kernels: 46.2 us -> 33 us
  local copies, waits for them, and re-layouts: 6.75 us -> 3.45 us
    pallas_call x3, Pallas kernels: 41.2 us -> 27.7 us  [phase(): pl.pallas_call(functools.partial(phase_kernel, done=done, narr=len(arrs),...]
    unnamed x17 -> x7, local copies, waits for them, and re-layouts: 6.75 us -> 3.45 us
    pallas_call x1, Pallas kernels: 0.71 us -> 1.81 us  [pack(): pl.pallas_call(pack_kernel, out_shape=jax.ShapeDtypeStruct((feat // LANE...]
  transfers between devices with their start and end apart: 15 -> 15, of which waited for: 4 -> 3; matrix products, arithmetic and copies ran while one was open for 4% -> 5% of each run, Pallas kernels for 35% -> 32%
where the time goes in v3:
time: 62.5 us; the launch traced here: 62.2 us
  Pallas kernels  33 us (53%)
  starting transfers between devices  18.6 us (30%)
  waiting for transfers between devices  4.5 us (7%)
  local copies, waits for them, and re-layouts  3.45 us (6%)
  between operations  1.45 us (2%)
  other arithmetic  1.16 us (2%)
    pallas_call x3, Pallas kernels, phase(): pl.pallas_call(functools.partial(phase_kernel, done=done, narr=len(arrs),...  27.7 us
    ppermute x12, starting transfers between devices, swap(): return lax.ppermute(value, axis, [(i, i ^ bit) for i in range(count)])  9.75 us
    ppermute x2, starting transfers between devices, between(): return lax.ppermute(value, axis, pairs + [(j, i) for i, j in pairs])  5.69 us
    ppermute x12, waiting for transfers between devices, swap(): return lax.ppermute(value, axis, [(i, i ^ bit) for i in range(count)])  4.5 us
    unnamed x7, local copies, waits for them, and re-layouts  3.45 us
    ppermute x1, starting transfers between devices, hop_two(): return lax.ppermute(value, 'sky', pairs)  3.19 us
    pallas_call x1, Pallas kernels, pack(): pl.pallas_call(pack_kernel, out_shape=jax.ShapeDtypeStruct((feat // LANE...  1.81 us
    pallas_call x1, Pallas kernels, blend(): pl.pallas_call(blend_kernel, out_shape=jax.ShapeDtypeStruct((co.shape[0],...  1.72 us
  transfers between devices with their start and end apart: 15, of which 3 were waited for; matrix products, arithmetic and copies ran while one was open for 5% of the time, Pallas kernels for 32%

profile of v3, /device:TPU:9, one launch (start us, length us, event | category | flops | bytes accessed | tf_op | source)
XLA Modules:
  0.0 62.2 jit_solution(10955534841310449169)
XLA Ops:
  0.6 0.0 copy-start.2
  0.6 1.8 %pack.1.refs_3_ = f32[656,128]{1,0:T(8,128)S(1)} custom-call(s32[1,1,16]{2,1,0:T(1,128)} %mask_ref.1, f32[1,1,80,1024]{3,2,1,0:T(8,128)} %feat_in.1, f32[1,1,16,80]{3,2,1,0:T(8,128)} %img_in.1), custom_call_target="tpu_custom_call" | custom-call | tf_op jit(solution)/shard_map/pack/pallas_call | solution.py:111
  2.5 1.3 %collective-permute-start = (f32[656,128]{1,0:T(8,128)S(1)}, f32[656,128]{1,0:T(8,128)S(1)}, u32[]{:S(2)}, u32[]{:S(2)}) collective-permute-start(f32[656,128]{1,0:T(8,128)S(1)} %pack.1.refs_3_), channel_id=1, source_target_pairs={{0,4},{4,0},{8,12},{12,8},{16,20},{20,16},{24,28},{28,24},{1,5},{5... | collective-permute-start | bytes 1007624 | tf_op jit(solution)/shard_map/ppermute | solution.py:494
  3.8 1.2 %collective-permute-start.1 = (f32[656,128]{1,0:T(8,128)S(1)}, f32[656,128]{1,0:T(8,128)S(1)}, u32[]{:S(2)}, u32[]{:S(2)}) collective-permute-start(f32[656,128]{1,0:T(8,128)S(1)} %pack.1.refs_3_), channel_id=1, source_target_pairs={{0,2},{1,3},{2,0},{3,1},{4,6},{5,7},{6,4},{7,5},{8,10},{9,11},{10,... | collective-permute-start | bytes 1007624 | tf_op jit(solution)/shard_map/ppermute | solution.py:494
  5.0 1.2 %collective-permute-start.6 = (f32[656,128]{1,0:T(8,128)S(1)}, f32[656,128]{1,0:T(8,128)}, u32[]{:S(2)}, u32[]{:S(2)}) collective-permute-start(f32[656,128]{1,0:T(8,128)S(1)} %pack.1.refs_3_), channel_id=1, source_target_pairs={{0,1},{1,0},{2,3},{3,2},{4,5},{5,4},{6,7},{7,6},{8,9},{9,8},{10,11... | collective-permute-start | bytes 1007624 | tf_op jit(solution)/shard_map/ppermute | solution.py:494
  6.2 0.7 %fusion.3 = s32[12]{0:T(128)S(1)} fusion(pred[12]{0:T(512)(128)(4,1)} %constant.50, pred[12]{0:T(512)(128)(4,1)} %constant.51, pred[]{:T(512)S(6)} %eq.35, s32[12]{0:T(128)} %constant.42.clone, s32[]{:T(128)S(6)} %axis_index.22), kind=kLoop, calls=%fused_computation.9 | loop fusion | flops 72 | bytes 125 | tf_op jit(solution)/shard_map/add | solution.py:525
  7.6 0.0 copy-start
  7.6 1.7 %copy-done = f32[1,1,576,1024]{3,2,1,0:T(8,128)S(1)} copy-done((f32[1,1,576,1024]{3,2,1,0:T(8,128)S(1)}, f32[1,1,576,1024]{3,2,1,0:T(8,128)}, u32[]{:S(2)}) %copy-start) | copy-done | bytes 2359320
  9.2 0.3 halve.1
  9.6 0.0 copy-done.2
  9.6 0.2 fusion
  9.8 0.1 select_reduce_fusion
  9.9 2.4 %collective-permute-done.1.refs_5_ = f32[656,128]{1,0:T(8,128)S(1)} collective-permute-done((f32[656,128]{1,0:T(8,128)S(1)}, f32[656,128]{1,0:T(8,128)S(1)}, u32[]{:S(2)}, u32[]{:S(2)}) %collective-permute-start.1) | collective-permute-done | bytes 335904 | tf_op jit(solution)/shard_map/ppermute | solution.py:494
  12.3 1.8 %collective-permute-start.2 = (f32[656,128]{1,0:T(8,128)S(1)}, f32[656,128]{1,0:T(8,128)S(1)}, u32[]{:S(2)}, u32[]{:S(2)}) collective-permute-start(f32[656,128]{1,0:T(8,128)S(1)} %collective-permute-done.1.refs_5_), channel_id=1, source_target_pairs={{0,1},{1,0},{2,3},{3,2},{4,5},{5,4},{6,7},{7,6},{8,9},{9,8},{10,11... | collective-permute-start | bytes 1007624 | tf_op jit(solution)/shard_map/ppermute | solution.py:494
  14.1 0.0 collective-permute-done.refs_6_.refs_3_
  14.1 0.0 collective-permute-start.3
  14.1 0.1 pad_add_fusion.refs_2_.odd_ref
  14.2 1.2 %collective-permute-start.4 = (f32[656,128]{1,0:T(8,128)S(1)}, f32[656,128]{1,0:T(8,128)S(1)}, u32[]{:S(2)}, u32[]{:S(2)}) collective-permute-start(f32[656,128]{1,0:T(8,128)S(1)} %collective-permute-done.refs_6_.refs_3_), channel_id=1, source_target_pairs={{0,2},{1,3},{2,0},{3,1},{4,6},{5,7},{6,4},{7,5},{8,10},{9,11},{10,... | collective-permute-start | bytes 1007624 | tf_op jit(solution)/shard_map/ppermute | solution.py:494
  15.4 3.2 %collective-permute-start.5 = (f32[656,128]{1,0:T(8,128)S(1)}, f32[656,128]{1,0:T(8,128)S(1)}, u32[]{:S(2)}, u32[]{:S(2)}) collective-permute-start(f32[656,128]{1,0:T(8,128)S(1)} %collective-permute-done.refs_6_.refs_3_), channel_id=1, source_target_pairs={{0,8},{8,16},{16,24},{12,4},{20,12},{28,20},{1,9},{9,17},{17,25},{... | collective-permute-start | bytes 1007624 | tf_op jit(solution)/shard_map/ppermute | solution.py:506
  18.6 0.0 collective-permute-done.6.refs_4_
  18.6 0.0 collective-permute-done.2.refs_7_.refs_4_
  18.6 0.0 collective-permute-done.3.refs_8_.refs_5_
  18.6 8.4 %phase0.1 = (bf16[240,1024]{1,0:T(8,128)(2,1)S(1)}, bf16[240,1024]{1,0:T(8,128)(2,1)S(1)}, f32[240,240]{1,0:T(8,128)S(1)}, f32[240,576]{1,0:T(8,128)S(1)}, f32[3,16,128]{2,1,0:T(8,128)S(1)}) custom-call(s32[12]{0:T(128)S(1)} %compare_select_fusion.1.refs_0_, f32[1,1]{1,0:T(1,128)S(6)} %copy.13.refs_1_, s32[2]{0:T(128)S(1)} %pad_add_fusion.refs_2_.odd_ref, ...), custom_call_target="tpu_custom_call" | custom-call | flops 6000000000 | bytes 4000000 | tf_op jit(solution)/shard_map/phase0/pallas_call | solution.py:412
  27.0 0.0 collective-permute-done.4.refs_6_.refs_4_
  27.0 0.0 collective-permute-done.5.refs_7_.refs_5_
  27.0 1.1 %collective-permute-start.7 = (f32[656,128]{1,0:T(8,128)S(1)}, f32[656,128]{1,0:T(8,128)S(1)}, u32[]{:S(2)}, u32[]{:S(2)}) collective-permute-start(f32[656,128]{1,0:T(8,128)S(1)} %collective-permute-done.4.refs_6_.refs_4_), channel_id=1, source_target_pairs={{0,1},{1,0},{2,3},{3,2},{4,5},{5,4},{6,7},{7,6},{8,9},{9,8},{10,11... | collective-permute-start | bytes 1007624 | tf_op jit(solution)/shard_map/ppermute | solution.py:494
  28.1 0.1 collective-permute-start.8
  28.2 0.3 collective-permute-start.9
  28.4 0.9 %collective-permute-done.7.refs_8_.refs_6_ = f32[656,128]{1,0:T(8,128)S(1)} collective-permute-done((f32[656,128]{1,0:T(8,128)S(1)}, f32[656,128]{1,0:T(8,128)S(1)}, u32[]{:S(2)}, u32[]{:S(2)}) %collective-permute-start.7) | collective-permute-done | bytes 335904 | tf_op jit(solution)/shard_map/ppermute | solution.py:494
  29.4 0.0 copy-start.1
  29.4 9.5 %phase1.1 = (bf16[240,1024]{1,0:T(8,128)(2,1)S(1)}, bf16[240,1024]{1,0:T(8,128)(2,1)S(1)}, f32[480,480]{1,0:T(8,128)S(1)}, f32[480,576]{1,0:T(8,128)S(1)}, f32[3,16,128]{2,1,0:T(8,128)S(1)}) custom-call(s32[12]{0:T(128)S(1)} %compare_select_fusion.1.refs_0_, f32[1,1]{1,0:T(1,128)S(6)} %copy.13.refs_1_, s32[2]{0:T(128)S(1)} %pad_add_fusion.refs_2_.odd_ref, ...), custom_call_target="tpu_custom_call" | custom-call | flops 6000000000 | bytes 4000000 | tf_op jit(solution)/shard_map/phase1/pallas_call | solution.py:412
  38.9 0.0 collective-permute-done.9.refs_8_
  38.9 0.5 collective-permute-start.10
  39.3 0.1 fusion.1.pos_ref
  39.4 0.0 collective-permute-done.8.refs_7_
  39.4 1.2 %collective-permute-done.10.refs_9_ = f32[656,128]{1,0:T(8,128)S(1)} collective-permute-done((f32[656,128]{1,0:T(8,128)S(1)}, f32[656,128]{1,0:T(8,128)S(1)}, u32[]{:S(2)}, u32[]{:S(2)}) %collective-permute-start.10) | collective-permute-done | bytes 335904 | tf_op jit(solution)/shard_map/ppermute | solution.py:494
  40.6 0.0 copy-done.1
  40.6 9.8 %phase2.1 = (f32[240,576]{1,0:T(8,128)S(1)}, f32[480,240]{1,0:T(8,128)S(1)}, f32[16,576]{1,0:T(8,128)S(1)}, f32[16,576]{1,0:T(8,128)S(1)}, f32[16,576]{1,0:T(8,1...) custom-call(s32[12]{0:T(128)S(1)} %compare_select_fusion.1.refs_0_, f32[1,1]{1,0:T(1,128)S(6)} %copy.13.refs_1_, ...), custom_call_target="tpu_custom_call" | custom-call | flops 6000000000 | bytes 4000000 | tf_op jit(solution)/shard_map/phase2/pallas_call | solution.py:412
  50.4 0.1 collective-permute-start.11
  50.5 3.2 %collective-permute-start.12 = (f32[16,576]{1,0:T(8,128)S(1)}, f32[16,576]{1,0:T(8,128)S(1)}, u32[]{:S(2)}, u32[]{:S(2)}) collective-permute-start(f32[16,576]{1,0:T(8,128)S(1)} %get-tuple-element.47), channel_id=1, source_target_pairs={{4,8},{12,16},{20,24},{8,4},{16,12},{24,20},{5,9},{13,17},{21,25},... | collective-permute-start | bytes 110600 | tf_op jit(solution)/shard_map/ppermute | solution.py:500
  53.7 1.0 %collective-permute-start.13 = (f32[16,96]{1,0:T(8,128)S(1)}, f32[16,96]{1,0:T(8,128)S(1)}, u32[]{:S(2)}, u32[]{:S(2)}) collective-permute-start(f32[16,96]{1,0:T(8,128)S(1)} %get-tuple-element.48), channel_id=1, source_target_pairs={{0,1},{1,0},{2,3},{3,2},{4,5},{5,4},{6,7},{7,6},{8,9},{9,8},{10,11... | collective-permute-start | bytes 18440 | tf_op jit(solution)/shard_map/ppermute | solution.py:494
  54.7 2.4 %collective-permute-start.14 = (f32[16,96]{1,0:T(8,128)S(1)}, f32[16,96]{1,0:T(8,128)S(1)}, u32[]{:S(2)}, u32[]{:S(2)}) collective-permute-start(f32[16,96]{1,0:T(8,128)S(1)} %get-tuple-element.49), channel_id=1, source_target_pairs={{1,2},{2,1},{5,6},{6,5},{9,10},{10,9},{13,14},{14,13},{17,18},{18,... | collective-permute-start | bytes 18440 | tf_op jit(solution)/shard_map/ppermute | solution.py:500
  57.2 1.5 %close.1 = f32[720,576]{1,0:T(8,128)S(1)} custom-call(s32[9]{0:T(128)S(1)} %fusion.1.pos_ref, f32[480,576]{1,0:T(8,128)S(1)} %get-tuple-element.35.refs_17_.w_ref, f32[480,240]{1,0:T(8,128)S(1)} %get-tuple-element.43.v_ref, f32[240,576]{1,0:T(8,128)S(1)} %get-tuple-element.44.z_ref), custom_call_target="tpu_custom_call" | custom-call | flops 500000000 | bytes 6000000 | tf_op jit(solution)/shard_map/close/pallas_call | solution.py:452
  58.7 1.8 %copy.12 = f32[1,1,720,576]{2,3,1,0:T(8,128)} copy(f32[1,1,720,576]{3,2,1,0:T(8,128)S(1)} %bitcast.4) | data formatting | bytes 3317760
  60.4 0.0 collective-permute-done.13.pair_ref
  60.5 0.0 collective-permute-done.14.mid_ref
  60.5 0.0 collective-permute-done.11.near_ref
  60.5 0.0 collective-permute-done.12.far_ref
  60.5 1.7 %blend.1 = f32[16,24,24]{2,1,0:T(8,128)} custom-call(s32[2]{0:T(128)S(1)} %pad_add_fusion.refs_2_.odd_ref, f32[16,576]{1,0:T(8,128)S(1)} %get-tuple-element.45.co_ref, f32[16,576]{1,0:T(8,128)S(1)} %collective-permute-done.11.near_ref, f32[16,576]{1,0:T(8,128)S(1)} %collective-permute-done.12.far_ref, f32[16,96]{1,0:T(8,128)S(1)} %collective-permute-done.13.pair_ref, ...), custom_call_target="tpu_custom_call" | custom-call | tf_op jit(solution)/shard_map/blend/pallas_call | solution.py:482
  (1 shorter events, 0.0 us)
Async XLA Ops:
  0.6 9.0 %copy-start.2 = (s32[1,1,9]{2,1,0:T(1,128)S(1)}, s32[1,1,9]{2,1,0:T(1,128)}, u32[]{:S(2)}) copy-start(s32[1,1,9]{2,1,0:T(1,128)} %param.13) | copy-start | bytes 112
  2.5 11.6 %collective-permute-start = (f32[656,128]{1,0:T(8,128)S(1)}, f32[656,128]{1,0:T(8,128)S(1)}, u32[]{:S(2)}, u32[]{:S(2)}) collective-permute-start(f32[656,128]{1,0:T(8,128)S(1)} %pack.1.refs_3_), channel_id=1, source_target_pairs={{0,4},{4,0},{8,12},{12,8},{16,20},{20,16},{24,28},{28,24},{1,5},{5... | collective-permute-start | bytes 1007624 | tf_op jit(solution)/shard_map/ppermute | solution.py:494
  3.8 8.5 %collective-permute-start.1 = (f32[656,128]{1,0:T(8,128)S(1)}, f32[656,128]{1,0:T(8,128)S(1)}, u32[]{:S(2)}, u32[]{:S(2)}) collective-permute-start(f32[656,128]{1,0:T(8,128)S(1)} %pack.1.refs_3_), channel_id=1, source_target_pairs={{0,2},{1,3},{2,0},{3,1},{4,6},{5,7},{6,4},{7,5},{8,10},{9,11},{10,... | collective-permute-start | bytes 1007624 | tf_op jit(solution)/shard_map/ppermute | solution.py:494
  5.0 13.6 %collective-permute-start.6 = (f32[656,128]{1,0:T(8,128)S(1)}, f32[656,128]{1,0:T(8,128)}, u32[]{:S(2)}, u32[]{:S(2)}) collective-permute-start(f32[656,128]{1,0:T(8,128)S(1)} %pack.1.refs_3_), channel_id=1, source_target_pairs={{0,1},{1,0},{2,3},{3,2},{4,5},{5,4},{6,7},{7,6},{8,9},{9,8},{10,11... | collective-permute-start | bytes 1007624 | tf_op jit(solution)/shard_map/ppermute | solution.py:494
  7.6 1.7 %copy-start = (f32[1,1,576,1024]{3,2,1,0:T(8,128)S(1)}, f32[1,1,576,1024]{3,2,1,0:T(8,128)}, u32[]{:S(2)}) copy-start(f32[1,1,576,1024]{3,2,1,0:T(8,128)} %t_ref.1) | copy-start | bytes 7077892
  12.3 6.3 %collective-permute-start.2 = (f32[656,128]{1,0:T(8,128)S(1)}, f32[656,128]{1,0:T(8,128)S(1)}, u32[]{:S(2)}, u32[]{:S(2)}) collective-permute-start(f32[656,128]{1,0:T(8,128)S(1)} %collective-permute-done.1.refs_5_), channel_id=1, source_target_pairs={{0,1},{1,0},{2,3},{3,2},{4,5},{5,4},{6,7},{7,6},{8,9},{9,8},{10,11... | collective-permute-start | bytes 1007624 | tf_op jit(solution)/shard_map/ppermute | solution.py:494
  14.1 4.5 %collective-permute-start.3 = (f32[656,128]{1,0:T(8,128)S(1)}, f32[656,128]{1,0:T(8,128)S(1)}, u32[]{:S(2)}, u32[]{:S(2)}) collective-permute-start(f32[656,128]{1,0:T(8,128)S(1)} %collective-permute-done.refs_6_.refs_3_), channel_id=1, source_target_pairs={{0,1},{1,0},{2,3},{3,2},{4,5},{5,4},{6,7},{7,6},{8,9},{9,8},{10,11... | collective-permute-start | bytes 1007624 | tf_op jit(solution)/shard_map/ppermute | solution.py:494
  14.2 12.8 %collective-permute-start.4 = (f32[656,128]{1,0:T(8,128)S(1)}, f32[656,128]{1,0:T(8,128)S(1)}, u32[]{:S(2)}, u32[]{:S(2)}) collective-permute-start(f32[656,128]{1,0:T(8,128)S(1)} %collective-permute-done.refs_6_.refs_3_), channel_id=1, source_target_pairs={{0,2},{1,3},{2,0},{3,1},{4,6},{5,7},{6,4},{7,5},{8,10},{9,11},{10,... | collective-permute-start | bytes 1007624 | tf_op jit(solution)/shard_map/ppermute | solution.py:494
  15.4 11.6 %collective-permute-start.5 = (f32[656,128]{1,0:T(8,128)S(1)}, f32[656,128]{1,0:T(8,128)S(1)}, u32[]{:S(2)}, u32[]{:S(2)}) collective-permute-start(f32[656,128]{1,0:T(8,128)S(1)} %collective-permute-done.refs_6_.refs_3_), channel_id=1, source_target_pairs={{0,8},{8,16},{16,24},{12,4},{20,12},{28,20},{1,9},{9,17},{17,25},{... | collective-permute-start | bytes 1007624 | tf_op jit(solution)/shard_map/ppermute | solution.py:506
  27.0 2.4 %collective-permute-start.7 = (f32[656,128]{1,0:T(8,128)S(1)}, f32[656,128]{1,0:T(8,128)S(1)}, u32[]{:S(2)}, u32[]{:S(2)}) collective-permute-start(f32[656,128]{1,0:T(8,128)S(1)} %collective-permute-done.4.refs_6_.refs_4_), channel_id=1, source_target_pairs={{0,1},{1,0},{2,3},{3,2},{4,5},{5,4},{6,7},{7,6},{8,9},{9,8},{10,11... | collective-permute-start | bytes 1007624 | tf_op jit(solution)/shard_map/ppermute | solution.py:494
  28.1 11.3 %collective-permute-start.8 = (f32[656,128]{1,0:T(8,128)S(1)}, f32[656,128]{1,0:T(8,128)S(1)}, u32[]{:S(2)}, u32[]{:S(2)}) collective-permute-start(f32[656,128]{1,0:T(8,128)S(1)} %collective-permute-done.5.refs_7_.refs_5_), channel_id=1, source_target_pairs={{0,1},{1,0},{2,3},{3,2},{4,5},{5,4},{6,7},{7,6},{8,9},{9,8},{10,11... | collective-permute-start | bytes 1007624 | tf_op jit(solution)/shard_map/ppermute | solution.py:494
  28.2 10.7 %collective-permute-start.9 = (f32[656,128]{1,0:T(8,128)S(1)}, f32[656,128]{1,0:T(8,128)S(1)}, u32[]{:S(2)}, u32[]{:S(2)}) collective-permute-start(f32[656,128]{1,0:T(8,128)S(1)} %collective-permute-done.5.refs_7_.refs_5_), channel_id=1, source_target_pairs={{0,2},{1,3},{2,0},{3,1},{4,6},{5,7},{6,4},{7,5},{8,10},{9,11},{10,... | collective-permute-start | bytes 1007624 | tf_op jit(solution)/shard_map/ppermute | solution.py:494
  29.4 11.2 %copy-start.1 = (f32[4,576]{1,0:T(4,128)S(1)}, f32[4,576]{1,0:T(4,128)}, u32[]{:S(2)}) copy-start(f32[4,576]{1,0:T(4,128)} %constant.43.clone.refs_3_) | copy-start | bytes 27652
  38.9 1.7 %collective-permute-start.10 = (f32[656,128]{1,0:T(8,128)S(1)}, f32[656,128]{1,0:T(8,128)S(1)}, u32[]{:S(2)}, u32[]{:S(2)}) collective-permute-start(f32[656,128]{1,0:T(8,128)S(1)} %collective-permute-done.9.refs_8_), channel_id=1, source_target_pairs={{0,1},{1,0},{2,3},{3,2},{4,5},{5,4},{6,7},{7,6},{8,9},{9,8},{10,11... | collective-permute-start | bytes 1007624 | tf_op jit(solution)/shard_map/ppermute | solution.py:494
  50.4 10.0 %collective-permute-start.11 = (f32[16,576]{1,0:T(8,128)S(1)}, f32[16,576]{1,0:T(8,128)S(1)}, u32[]{:S(2)}, u32[]{:S(2)}) collective-permute-start(f32[16,576]{1,0:T(8,128)S(1)} %get-tuple-element.46), channel_id=1, source_target_pairs={{0,4},{4,0},{8,12},{12,8},{16,20},{20,16},{24,28},{28,24},{1,5},{5... | collective-permute-start | bytes 110600 | tf_op jit(solution)/shard_map/ppermute | solution.py:494
  50.5 10.0 %collective-permute-start.12 = (f32[16,576]{1,0:T(8,128)S(1)}, f32[16,576]{1,0:T(8,128)S(1)}, u32[]{:S(2)}, u32[]{:S(2)}) collective-permute-start(f32[16,576]{1,0:T(8,128)S(1)} %get-tuple-element.47), channel_id=1, source_target_pairs={{4,8},{12,16},{20,24},{8,4},{16,12},{24,20},{5,9},{13,17},{21,25},... | collective-permute-start | bytes 110600 | tf_op jit(solution)/shard_map/ppermute | solution.py:500
  53.7 6.7 %collective-permute-start.13 = (f32[16,96]{1,0:T(8,128)S(1)}, f32[16,96]{1,0:T(8,128)S(1)}, u32[]{:S(2)}, u32[]{:S(2)}) collective-permute-start(f32[16,96]{1,0:T(8,128)S(1)} %get-tuple-element.48), channel_id=1, source_target_pairs={{0,1},{1,0},{2,3},{3,2},{4,5},{5,4},{6,7},{7,6},{8,9},{9,8},{10,11... | collective-permute-start | bytes 18440 | tf_op jit(solution)/shard_map/ppermute | solution.py:494
  54.7 5.7 %collective-permute-start.14 = (f32[16,96]{1,0:T(8,128)S(1)}, f32[16,96]{1,0:T(8,128)S(1)}, u32[]{:S(2)}, u32[]{:S(2)}) collective-permute-start(f32[16,96]{1,0:T(8,128)S(1)} %get-tuple-element.49), channel_id=1, source_target_pairs={{1,2},{2,1},{5,6},{6,5},{9,10},{10,9},{13,14},{14,13},{17,18},{18,... | collective-permute-start | bytes 18440 | tf_op jit(solution)/shard_map/ppermute | solution.py:500

commit v4 on v3

--- a/solution.py
+++ b/solution.py
@@ -233,7 +233,7 @@
         r_ref[:, cut] = r_ref[:, cut] - dot3(g, split2(old_w[rows, cut]))
 
     for cut in chunks(nout):
-        for deep in chunks(feat):
+        for deep in chunks(feat, feat):
             work.append(functools.partial(right_sides, cut, deep, deep.start == 0))
         for rows, g in cross:
             work.append(functools.partial(cross_right, cut, rows, g))

time: 62.5 us -> 62.3 us (level)
  no operation moved by 1% of the time
where the time goes in v4:
time: 62.3 us; the launch traced here: 62 us
  Pallas kernels  32.9 us (53%)
  starting transfers between devices  18.6 us (30%)
  waiting for transfers between devices  4.51 us (7%)
  local copies, waits for them, and re-layouts  3.45 us (6%)
  between operations  1.45 us (2%)
  other arithmetic  1.16 us (2%)
    pallas_call x3, Pallas kernels, phase(): pl.pallas_call(functools.partial(phase_kernel, done=done, narr=len(arrs),...  27.5 us
    ppermute x12, starting transfers between devices, swap(): return lax.ppermute(value, axis, [(i, i ^ bit) for i in range(count)])  9.73 us
    ppermute x2, starting transfers between devices, between(): return lax.ppermute(value, axis, pairs + [(j, i) for i, j in pairs])  5.67 us
    ppermute x12, waiting for transfers between devices, swap(): return lax.ppermute(value, axis, [(i, i ^ bit) for i in range(count)])  4.5 us
    unnamed x7, local copies, waits for them, and re-layouts  3.45 us
    ppermute x1, starting transfers between devices, hop_two(): return lax.ppermute(value, 'sky', pairs)  3.19 us
    pallas_call x1, Pallas kernels, pack(): pl.pallas_call(pack_kernel, out_shape=jax.ShapeDtypeStruct((feat // LANE...  1.81 us
    pallas_call x1, Pallas kernels, blend(): pl.pallas_call(blend_kernel, out_shape=jax.ShapeDtypeStruct((co.shape[0],...  1.72 us
  transfers between devices with their start and end apart: 15, of which 3 were waited for; matrix products, arithmetic and copies ran while one was open for 5% of the time, Pallas kernels for 32%

profile of v4, /device:TPU:9, one launch (start us, length us, event | category | flops | bytes accessed | tf_op | source)
XLA Modules:
  0.0 62.0 jit_solution(2261512311280865782)
XLA Ops:
  0.6 0.0 copy-start.2
  0.6 1.8 %pack.1.refs_3_ = f32[656,128]{1,0:T(8,128)S(1)} custom-call(s32[1,1,16]{2,1,0:T(1,128)} %mask_ref.1, f32[1,1,80,1024]{3,2,1,0:T(8,128)} %feat_in.1, f32[1,1,16,80]{3,2,1,0:T(8,128)} %img_in.1), custom_call_target="tpu_custom_call" | custom-call | tf_op jit(solution)/shard_map/pack/pallas_call | solution.py:111
  2.5 1.3 %collective-permute-start = (f32[656,128]{1,0:T(8,128)S(1)}, f32[656,128]{1,0:T(8,128)S(1)}, u32[]{:S(2)}, u32[]{:S(2)}) collective-permute-start(f32[656,128]{1,0:T(8,128)S(1)} %pack.1.refs_3_), channel_id=1, source_target_pairs={{0,4},{4,0},{8,12},{12,8},{16,20},{20,16},{24,28},{28,24},{1,5},{5... | collective-permute-start | bytes 1007624 | tf_op jit(solution)/shard_map/ppermute | solution.py:494
  3.8 1.2 %collective-permute-start.1 = (f32[656,128]{1,0:T(8,128)S(1)}, f32[656,128]{1,0:T(8,128)S(1)}, u32[]{:S(2)}, u32[]{:S(2)}) collective-permute-start(f32[656,128]{1,0:T(8,128)S(1)} %pack.1.refs_3_), channel_id=1, source_target_pairs={{0,2},{1,3},{2,0},{3,1},{4,6},{5,7},{6,4},{7,5},{8,10},{9,11},{10,... | collective-permute-start | bytes 1007624 | tf_op jit(solution)/shard_map/ppermute | solution.py:494
  5.0 1.2 %collective-permute-start.6 = (f32[656,128]{1,0:T(8,128)S(1)}, f32[656,128]{1,0:T(8,128)}, u32[]{:S(2)}, u32[]{:S(2)}) collective-permute-start(f32[656,128]{1,0:T(8,128)S(1)} %pack.1.refs_3_), channel_id=1, source_target_pairs={{0,1},{1,0},{2,3},{3,2},{4,5},{5,4},{6,7},{7,6},{8,9},{9,8},{10,11... | collective-permute-start | bytes 1007624 | tf_op jit(solution)/shard_map/ppermute | solution.py:494
  6.2 0.7 %fusion.3 = s32[12]{0:T(128)S(1)} fusion(pred[12]{0:T(512)(128)(4,1)} %constant.50, pred[12]{0:T(512)(128)(4,1)} %constant.51, pred[]{:T(512)S(6)} %eq.35, s32[12]{0:T(128)} %constant.42.clone, s32[]{:T(128)S(6)} %axis_index.22), kind=kLoop, calls=%fused_computation.9 | loop fusion | flops 72 | bytes 125 | tf_op jit(solution)/shard_map/add | solution.py:525
  7.6 0.0 copy-start
  7.6 1.7 %copy-done = f32[1,1,576,1024]{3,2,1,0:T(8,128)S(1)} copy-done((f32[1,1,576,1024]{3,2,1,0:T(8,128)S(1)}, f32[1,1,576,1024]{3,2,1,0:T(8,128)}, u32[]{:S(2)}) %copy-start) | copy-done | bytes 2359320
  9.2 0.3 halve.1
  9.6 0.0 copy-done.2
  9.6 0.2 fusion
  9.8 0.1 select_reduce_fusion
  9.9 2.4 %collective-permute-done.1.refs_5_ = f32[656,128]{1,0:T(8,128)S(1)} collective-permute-done((f32[656,128]{1,0:T(8,128)S(1)}, f32[656,128]{1,0:T(8,128)S(1)}, u32[]{:S(2)}, u32[]{:S(2)}) %collective-permute-start.1) | collective-permute-done | bytes 335904 | tf_op jit(solution)/shard_map/ppermute | solution.py:494
  12.3 1.8 %collective-permute-start.2 = (f32[656,128]{1,0:T(8,128)S(1)}, f32[656,128]{1,0:T(8,128)S(1)}, u32[]{:S(2)}, u32[]{:S(2)}) collective-permute-start(f32[656,128]{1,0:T(8,128)S(1)} %collective-permute-done.1.refs_5_), channel_id=1, source_target_pairs={{0,1},{1,0},{2,3},{3,2},{4,5},{5,4},{6,7},{7,6},{8,9},{9,8},{10,11... | collective-permute-start | bytes 1007624 | tf_op jit(solution)/shard_map/ppermute | solution.py:494
  14.1 0.0 collective-permute-done.refs_6_.refs_3_
  14.1 0.0 collective-permute-start.3
  14.1 0.1 pad_add_fusion.refs_2_.odd_ref
  14.2 1.2 %collective-permute-start.4 = (f32[656,128]{1,0:T(8,128)S(1)}, f32[656,128]{1,0:T(8,128)S(1)}, u32[]{:S(2)}, u32[]{:S(2)}) collective-permute-start(f32[656,128]{1,0:T(8,128)S(1)} %collective-permute-done.refs_6_.refs_3_), channel_id=1, source_target_pairs={{0,2},{1,3},{2,0},{3,1},{4,6},{5,7},{6,4},{7,5},{8,10},{9,11},{10,... | collective-permute-start | bytes 1007624 | tf_op jit(solution)/shard_map/ppermute | solution.py:494
  15.4 3.2 %collective-permute-start.5 = (f32[656,128]{1,0:T(8,128)S(1)}, f32[656,128]{1,0:T(8,128)S(1)}, u32[]{:S(2)}, u32[]{:S(2)}) collective-permute-start(f32[656,128]{1,0:T(8,128)S(1)} %collective-permute-done.refs_6_.refs_3_), channel_id=1, source_target_pairs={{0,8},{8,16},{16,24},{12,4},{20,12},{28,20},{1,9},{9,17},{17,25},{... | collective-permute-start | bytes 1007624 | tf_op jit(solution)/shard_map/ppermute | solution.py:506
  18.6 0.0 collective-permute-done.6.refs_4_
  18.6 0.0 collective-permute-done.2.refs_7_.refs_4_
  18.6 0.0 collective-permute-done.3.refs_8_.refs_5_
  18.6 8.3 %phase0.1 = (bf16[240,1024]{1,0:T(8,128)(2,1)S(1)}, bf16[240,1024]{1,0:T(8,128)(2,1)S(1)}, f32[240,240]{1,0:T(8,128)S(1)}, f32[240,576]{1,0:T(8,128)S(1)}, f32[3,16,128]{2,1,0:T(8,128)S(1)}) custom-call(s32[12]{0:T(128)S(1)} %compare_select_fusion.1.refs_0_, f32[1,1]{1,0:T(1,128)S(6)} %copy.13.refs_1_, s32[2]{0:T(128)S(1)} %pad_add_fusion.refs_2_.odd_ref, ...), custom_call_target="tpu_custom_call" | custom-call | flops 6000000000 | bytes 4000000 | tf_op jit(solution)/shard_map/phase0/pallas_call | solution.py:412
  26.9 0.0 collective-permute-done.4.refs_6_.refs_4_
  26.9 0.0 collective-permute-done.5.refs_7_.refs_5_
  27.0 1.1 %collective-permute-start.7 = (f32[656,128]{1,0:T(8,128)S(1)}, f32[656,128]{1,0:T(8,128)S(1)}, u32[]{:S(2)}, u32[]{:S(2)}) collective-permute-start(f32[656,128]{1,0:T(8,128)S(1)} %collective-permute-done.4.refs_6_.refs_4_), channel_id=1, source_target_pairs={{0,1},{1,0},{2,3},{3,2},{4,5},{5,4},{6,7},{7,6},{8,9},{9,8},{10,11... | collective-permute-start | bytes 1007624 | tf_op jit(solution)/shard_map/ppermute | solution.py:494
  28.1 0.1 collective-permute-start.8
  28.2 0.3 collective-permute-start.9
  28.4 0.9 %collective-permute-done.7.refs_8_.refs_6_ = f32[656,128]{1,0:T(8,128)S(1)} collective-permute-done((f32[656,128]{1,0:T(8,128)S(1)}, f32[656,128]{1,0:T(8,128)S(1)}, u32[]{:S(2)}, u32[]{:S(2)}) %collective-permute-start.7) | collective-permute-done | bytes 335904 | tf_op jit(solution)/shard_map/ppermute | solution.py:494
  29.4 0.0 copy-start.1
  29.4 9.5 %phase1.1 = (bf16[240,1024]{1,0:T(8,128)(2,1)S(1)}, bf16[240,1024]{1,0:T(8,128)(2,1)S(1)}, f32[480,480]{1,0:T(8,128)S(1)}, f32[480,576]{1,0:T(8,128)S(1)}, f32[3,16,128]{2,1,0:T(8,128)S(1)}) custom-call(s32[12]{0:T(128)S(1)} %compare_select_fusion.1.refs_0_, f32[1,1]{1,0:T(1,128)S(6)} %copy.13.refs_1_, s32[2]{0:T(128)S(1)} %pad_add_fusion.refs_2_.odd_ref, ...), custom_call_target="tpu_custom_call" | custom-call | flops 6000000000 | bytes 4000000 | tf_op jit(solution)/shard_map/phase1/pallas_call | solution.py:412
  38.9 0.0 collective-permute-done.9.refs_8_
  38.9 0.4 collective-permute-start.10
  39.4 0.1 fusion.1.pos_ref
  39.4 0.0 collective-permute-done.8.refs_7_
  39.4 1.2 %collective-permute-done.10.refs_9_ = f32[656,128]{1,0:T(8,128)S(1)} collective-permute-done((f32[656,128]{1,0:T(8,128)S(1)}, f32[656,128]{1,0:T(8,128)S(1)}, u32[]{:S(2)}, u32[]{:S(2)}) %collective-permute-start.10) | collective-permute-done | bytes 335904 | tf_op jit(solution)/shard_map/ppermute | solution.py:494
  40.6 0.0 copy-done.1
  40.6 9.6 %phase2.1 = (f32[240,576]{1,0:T(8,128)S(1)}, f32[480,240]{1,0:T(8,128)S(1)}, f32[16,576]{1,0:T(8,128)S(1)}, f32[16,576]{1,0:T(8,128)S(1)}, f32[16,576]{1,0:T(8,1...) custom-call(s32[12]{0:T(128)S(1)} %compare_select_fusion.1.refs_0_, f32[1,1]{1,0:T(1,128)S(6)} %copy.13.refs_1_, ...), custom_call_target="tpu_custom_call" | custom-call | flops 6000000000 | bytes 4000000 | tf_op jit(solution)/shard_map/phase2/pallas_call | solution.py:412
  50.2 0.1 collective-permute-start.11
  50.3 3.2 %collective-permute-start.12 = (f32[16,576]{1,0:T(8,128)S(1)}, f32[16,576]{1,0:T(8,128)S(1)}, u32[]{:S(2)}, u32[]{:S(2)}) collective-permute-start(f32[16,576]{1,0:T(8,128)S(1)} %get-tuple-element.47), channel_id=1, source_target_pairs={{4,8},{12,16},{20,24},{8,4},{16,12},{24,20},{5,9},{13,17},{21,25},... | collective-permute-start | bytes 110600 | tf_op jit(solution)/shard_map/ppermute | solution.py:500
  53.6 1.0 %collective-permute-start.13 = (f32[16,96]{1,0:T(8,128)S(1)}, f32[16,96]{1,0:T(8,128)S(1)}, u32[]{:S(2)}, u32[]{:S(2)}) collective-permute-start(f32[16,96]{1,0:T(8,128)S(1)} %get-tuple-element.48), channel_id=1, source_target_pairs={{0,1},{1,0},{2,3},{3,2},{4,5},{5,4},{6,7},{7,6},{8,9},{9,8},{10,11... | collective-permute-start | bytes 18440 | tf_op jit(solution)/shard_map/ppermute | solution.py:494
  54.5 2.4 %collective-permute-start.14 = (f32[16,96]{1,0:T(8,128)S(1)}, f32[16,96]{1,0:T(8,128)S(1)}, u32[]{:S(2)}, u32[]{:S(2)}) collective-permute-start(f32[16,96]{1,0:T(8,128)S(1)} %get-tuple-element.49), channel_id=1, source_target_pairs={{1,2},{2,1},{5,6},{6,5},{9,10},{10,9},{13,14},{14,13},{17,18},{18,... | collective-permute-start | bytes 18440 | tf_op jit(solution)/shard_map/ppermute | solution.py:500
  57.0 1.5 %close.1 = f32[720,576]{1,0:T(8,128)S(1)} custom-call(s32[9]{0:T(128)S(1)} %fusion.1.pos_ref, f32[480,576]{1,0:T(8,128)S(1)} %get-tuple-element.35.refs_17_.w_ref, f32[480,240]{1,0:T(8,128)S(1)} %get-tuple-element.43.v_ref, f32[240,576]{1,0:T(8,128)S(1)} %get-tuple-element.44.z_ref), custom_call_target="tpu_custom_call" | custom-call | flops 500000000 | bytes 6000000 | tf_op jit(solution)/shard_map/close/pallas_call | solution.py:452
  58.5 1.8 %copy.12 = f32[1,1,720,576]{2,3,1,0:T(8,128)} copy(f32[1,1,720,576]{3,2,1,0:T(8,128)S(1)} %bitcast.4) | data formatting | bytes 3317760
  60.3 0.0 collective-permute-done.13.pair_ref
  60.3 0.0 collective-permute-done.14.mid_ref
  60.3 0.0 collective-permute-done.11.near_ref
  60.3 0.0 collective-permute-done.12.far_ref
  60.3 1.7 %blend.1 = f32[16,24,24]{2,1,0:T(8,128)} custom-call(s32[2]{0:T(128)S(1)} %pad_add_fusion.refs_2_.odd_ref, f32[16,576]{1,0:T(8,128)S(1)} %get-tuple-element.45.co_ref, f32[16,576]{1,0:T(8,128)S(1)} %collective-permute-done.11.near_ref, f32[16,576]{1,0:T(8,128)S(1)} %collective-permute-done.12.far_ref, f32[16,96]{1,0:T(8,128)S(1)} %collective-permute-done.13.pair_ref, ...), custom_call_target="tpu_custom_call" | custom-call | tf_op jit(solution)/shard_map/blend/pallas_call | solution.py:482
  (1 shorter events, 0.0 us)
Async XLA Ops:
  0.6 9.0 %copy-start.2 = (s32[1,1,9]{2,1,0:T(1,128)S(1)}, s32[1,1,9]{2,1,0:T(1,128)}, u32[]{:S(2)}) copy-start(s32[1,1,9]{2,1,0:T(1,128)} %param.13) | copy-start | bytes 112
  2.5 11.6 %collective-permute-start = (f32[656,128]{1,0:T(8,128)S(1)}, f32[656,128]{1,0:T(8,128)S(1)}, u32[]{:S(2)}, u32[]{:S(2)}) collective-permute-start(f32[656,128]{1,0:T(8,128)S(1)} %pack.1.refs_3_), channel_id=1, source_target_pairs={{0,4},{4,0},{8,12},{12,8},{16,20},{20,16},{24,28},{28,24},{1,5},{5... | collective-permute-start | bytes 1007624 | tf_op jit(solution)/shard_map/ppermute | solution.py:494
  3.8 8.5 %collective-permute-start.1 = (f32[656,128]{1,0:T(8,128)S(1)}, f32[656,128]{1,0:T(8,128)S(1)}, u32[]{:S(2)}, u32[]{:S(2)}) collective-permute-start(f32[656,128]{1,0:T(8,128)S(1)} %pack.1.refs_3_), channel_id=1, source_target_pairs={{0,2},{1,3},{2,0},{3,1},{4,6},{5,7},{6,4},{7,5},{8,10},{9,11},{10,... | collective-permute-start | bytes 1007624 | tf_op jit(solution)/shard_map/ppermute | solution.py:494
  5.0 13.6 %collective-permute-start.6 = (f32[656,128]{1,0:T(8,128)S(1)}, f32[656,128]{1,0:T(8,128)}, u32[]{:S(2)}, u32[]{:S(2)}) collective-permute-start(f32[656,128]{1,0:T(8,128)S(1)} %pack.1.refs_3_), channel_id=1, source_target_pairs={{0,1},{1,0},{2,3},{3,2},{4,5},{5,4},{6,7},{7,6},{8,9},{9,8},{10,11... | collective-permute-start | bytes 1007624 | tf_op jit(solution)/shard_map/ppermute | solution.py:494
  7.6 1.7 %copy-start = (f32[1,1,576,1024]{3,2,1,0:T(8,128)S(1)}, f32[1,1,576,1024]{3,2,1,0:T(8,128)}, u32[]{:S(2)}) copy-start(f32[1,1,576,1024]{3,2,1,0:T(8,128)} %t_ref.1) | copy-start | bytes 7077892
  12.3 6.3 %collective-permute-start.2 = (f32[656,128]{1,0:T(8,128)S(1)}, f32[656,128]{1,0:T(8,128)S(1)}, u32[]{:S(2)}, u32[]{:S(2)}) collective-permute-start(f32[656,128]{1,0:T(8,128)S(1)} %collective-permute-done.1.refs_5_), channel_id=1, source_target_pairs={{0,1},{1,0},{2,3},{3,2},{4,5},{5,4},{6,7},{7,6},{8,9},{9,8},{10,11... | collective-permute-start | bytes 1007624 | tf_op jit(solution)/shard_map/ppermute | solution.py:494
  14.1 4.5 %collective-permute-start.3 = (f32[656,128]{1,0:T(8,128)S(1)}, f32[656,128]{1,0:T(8,128)S(1)}, u32[]{:S(2)}, u32[]{:S(2)}) collective-permute-start(f32[656,128]{1,0:T(8,128)S(1)} %collective-permute-done.refs_6_.refs_3_), channel_id=1, source_target_pairs={{0,1},{1,0},{2,3},{3,2},{4,5},{5,4},{6,7},{7,6},{8,9},{9,8},{10,11... | collective-permute-start | bytes 1007624 | tf_op jit(solution)/shard_map/ppermute | solution.py:494
  14.2 12.8 %collective-permute-start.4 = (f32[656,128]{1,0:T(8,128)S(1)}, f32[656,128]{1,0:T(8,128)S(1)}, u32[]{:S(2)}, u32[]{:S(2)}) collective-permute-start(f32[656,128]{1,0:T(8,128)S(1)} %collective-permute-done.refs_6_.refs_3_), channel_id=1, source_target_pairs={{0,2},{1,3},{2,0},{3,1},{4,6},{5,7},{6,4},{7,5},{8,10},{9,11},{10,... | collective-permute-start | bytes 1007624 | tf_op jit(solution)/shard_map/ppermute | solution.py:494
  15.4 11.6 %collective-permute-start.5 = (f32[656,128]{1,0:T(8,128)S(1)}, f32[656,128]{1,0:T(8,128)S(1)}, u32[]{:S(2)}, u32[]{:S(2)}) collective-permute-start(f32[656,128]{1,0:T(8,128)S(1)} %collective-permute-done.refs_6_.refs_3_), channel_id=1, source_target_pairs={{0,8},{8,16},{16,24},{12,4},{20,12},{28,20},{1,9},{9,17},{17,25},{... | collective-permute-start | bytes 1007624 | tf_op jit(solution)/shard_map/ppermute | solution.py:506
  27.0 2.4 %collective-permute-start.7 = (f32[656,128]{1,0:T(8,128)S(1)}, f32[656,128]{1,0:T(8,128)S(1)}, u32[]{:S(2)}, u32[]{:S(2)}) collective-permute-start(f32[656,128]{1,0:T(8,128)S(1)} %collective-permute-done.4.refs_6_.refs_4_), channel_id=1, source_target_pairs={{0,1},{1,0},{2,3},{3,2},{4,5},{5,4},{6,7},{7,6},{8,9},{9,8},{10,11... | collective-permute-start | bytes 1007624 | tf_op jit(solution)/shard_map/ppermute | solution.py:494
  28.1 11.4 %collective-permute-start.8 = (f32[656,128]{1,0:T(8,128)S(1)}, f32[656,128]{1,0:T(8,128)S(1)}, u32[]{:S(2)}, u32[]{:S(2)}) collective-permute-start(f32[656,128]{1,0:T(8,128)S(1)} %collective-permute-done.5.refs_7_.refs_5_), channel_id=1, source_target_pairs={{0,1},{1,0},{2,3},{3,2},{4,5},{5,4},{6,7},{7,6},{8,9},{9,8},{10,11... | collective-permute-start | bytes 1007624 | tf_op jit(solution)/shard_map/ppermute | solution.py:494
  28.2 10.7 %collective-permute-start.9 = (f32[656,128]{1,0:T(8,128)S(1)}, f32[656,128]{1,0:T(8,128)S(1)}, u32[]{:S(2)}, u32[]{:S(2)}) collective-permute-start(f32[656,128]{1,0:T(8,128)S(1)} %collective-permute-done.5.refs_7_.refs_5_), channel_id=1, source_target_pairs={{0,2},{1,3},{2,0},{3,1},{4,6},{5,7},{6,4},{7,5},{8,10},{9,11},{10,... | collective-permute-start | bytes 1007624 | tf_op jit(solution)/shard_map/ppermute | solution.py:494
  29.4 11.3 %copy-start.1 = (f32[4,576]{1,0:T(4,128)S(1)}, f32[4,576]{1,0:T(4,128)}, u32[]{:S(2)}) copy-start(f32[4,576]{1,0:T(4,128)} %constant.43.clone.refs_3_) | copy-start | bytes 27652
  38.9 1.7 %collective-permute-start.10 = (f32[656,128]{1,0:T(8,128)S(1)}, f32[656,128]{1,0:T(8,128)S(1)}, u32[]{:S(2)}, u32[]{:S(2)}) collective-permute-start(f32[656,128]{1,0:T(8,128)S(1)} %collective-permute-done.9.refs_8_), channel_id=1, source_target_pairs={{0,1},{1,0},{2,3},{3,2},{4,5},{5,4},{6,7},{7,6},{8,9},{9,8},{10,11... | collective-permute-start | bytes 1007624 | tf_op jit(solution)/shard_map/ppermute | solution.py:494
  50.2 10.0 %collective-permute-start.11 = (f32[16,576]{1,0:T(8,128)S(1)}, f32[16,576]{1,0:T(8,128)S(1)}, u32[]{:S(2)}, u32[]{:S(2)}) collective-permute-start(f32[16,576]{1,0:T(8,128)S(1)} %get-tuple-element.46), channel_id=1, source_target_pairs={{0,4},{4,0},{8,12},{12,8},{16,20},{20,16},{24,28},{28,24},{1,5},{5... | collective-permute-start | bytes 110600 | tf_op jit(solution)/shard_map/ppermute | solution.py:494
  50.3 10.0 %collective-permute-start.12 = (f32[16,576]{1,0:T(8,128)S(1)}, f32[16,576]{1,0:T(8,128)S(1)}, u32[]{:S(2)}, u32[]{:S(2)}) collective-permute-start(f32[16,576]{1,0:T(8,128)S(1)} %get-tuple-element.47), channel_id=1, source_target_pairs={{4,8},{12,16},{20,24},{8,4},{16,12},{24,20},{5,9},{13,17},{21,25},... | collective-permute-start | bytes 110600 | tf_op jit(solution)/shard_map/ppermute | solution.py:500
  53.6 6.7 %collective-permute-start.13 = (f32[16,96]{1,0:T(8,128)S(1)}, f32[16,96]{1,0:T(8,128)S(1)}, u32[]{:S(2)}, u32[]{:S(2)}) collective-permute-start(f32[16,96]{1,0:T(8,128)S(1)} %get-tuple-element.48), channel_id=1, source_target_pairs={{0,1},{1,0},{2,3},{3,2},{4,5},{5,4},{6,7},{7,6},{8,9},{9,8},{10,11... | collective-permute-start | bytes 18440 | tf_op jit(solution)/shard_map/ppermute | solution.py:494
  54.5 5.7 %collective-permute-start.14 = (f32[16,96]{1,0:T(8,128)S(1)}, f32[16,96]{1,0:T(8,128)S(1)}, u32[]{:S(2)}, u32[]{:S(2)}) collective-permute-start(f32[16,96]{1,0:T(8,128)S(1)} %get-tuple-element.49), channel_id=1, source_target_pairs={{1,2},{2,1},{5,6},{6,5},{9,10},{10,9},{13,14},{14,13},{17,18},{18,... | collective-permute-start | bytes 18440 | tf_op jit(solution)/shard_map/ppermute | solution.py:500

commit v5 on v4

--- a/solution.py
+++ b/solution.py
@@ -432,17 +432,18 @@
     )(*args)
 
 
-def close_kernel(pos_ref, w_ref, v_ref, z_ref, out_ref, x_ref):
+def close_kernel(pos_ref, w_ref, v_ref, z_ref, out_ref):
     before = w_ref.shape[0]
     n = z_ref.shape[0]
     count = pos_ref.shape[0]
     npix = (before + n) // count
     z = z_ref[...]
-    x_ref[before : before + n, :] = z
-    x_ref[0:before, :] = w_ref[...] - dot3(split2(v_ref[...]), split2(z))
-    for i in range(count):
-        src = pl.multiple_of(pos_ref[i] * npix, SUB)
-        out_ref[i * npix : (i + 1) * npix, :] = x_ref[pl.ds(src, npix), :]
+    front = w_ref[...] - dot3(split2(v_ref[...]), split2(z))
+    for r in range(count):
+        to = sum(jnp.where(pos_ref[k] == r, k, 0) for k in range(count))
+        top = r * npix
+        block = front[top : top + npix] if top < before else z[top - before : top - before + npix]
+        out_ref[pl.ds(pl.multiple_of(to * npix, SUB), npix), :] = block
 
 
 def close(pos, w, v, z):
@@ -454,7 +455,6 @@
         out_shape=jax.ShapeDtypeStruct((before + n, nout), f32),
         in_specs=[pl.BlockSpec(memory_space=pltpu.SMEM), vm, vm, vm],
         out_specs=vm,
-        scratch_shapes=[pltpu.VMEM((before + n, nout), f32)],
         compiler_params=pltpu.CompilerParams(vmem_limit_bytes=20 << 20),
         cost_estimate=pl.CostEstimate(
             flops=500_000_000, transcendentals=0, bytes_accessed=6_000_000

time: 62.3 us -> 62.2 us (level)
  no operation moved by 1% of the time
where the time goes in v5:
time: 62.2 us; the launch traced here: 61.9 us
  Pallas kernels  32.7 us (53%)
  starting transfers between devices  18.6 us (30%)
  waiting for transfers between devices  4.5 us (7%)
  local copies, waits for them, and re-layouts  3.45 us (6%)
  between operations  1.45 us (2%)
  other arithmetic  1.16 us (2%)
    pallas_call x3, Pallas kernels, phase(): pl.pallas_call(functools.partial(phase_kernel, done=done, narr=len(arrs),...  27.5 us
    ppermute x12, starting transfers between devices, swap(): return lax.ppermute(value, axis, [(i, i ^ bit) for i in range(count)])  9.76 us
    ppermute x2, starting transfers between devices, between(): return lax.ppermute(value, axis, pairs + [(j, i) for i, j in pairs])  5.66 us
    ppermute x12, waiting for transfers between devices, swap(): return lax.ppermute(value, axis, [(i, i ^ bit) for i in range(count)])  4.5 us
    unnamed x7, local copies, waits for them, and re-layouts  3.45 us
    ppermute x1, starting transfers between devices, hop_two(): return lax.ppermute(value, 'sky', pairs)  3.19 us
    pallas_call x1, Pallas kernels, pack(): pl.pallas_call(pack_kernel, out_shape=jax.ShapeDtypeStruct((feat // LANE...  1.81 us
    pallas_call x1, Pallas kernels, blend(): pl.pallas_call(blend_kernel, out_shape=jax.ShapeDtypeStruct((co.shape[0],...  1.72 us
  transfers between devices with their start and end apart: 15, of which 3 were waited for; matrix products, arithmetic and copies ran while one was open for 5% of the time, Pallas kernels for 32%

profile of v5, /device:TPU:9, one launch (start us, length us, event | category | flops | bytes accessed | tf_op | source)
XLA Modules:
  0.0 61.9 jit_solution(18132491033060896256)
XLA Ops:
  0.6 0.0 copy-start.2
  0.6 1.8 %pack.1.refs_3_ = f32[656,128]{1,0:T(8,128)S(1)} custom-call(s32[1,1,16]{2,1,0:T(1,128)} %mask_ref.1, f32[1,1,80,1024]{3,2,1,0:T(8,128)} %feat_in.1, f32[1,1,16,80]{3,2,1,0:T(8,128)} %img_in.1), custom_call_target="tpu_custom_call" | custom-call | tf_op jit(solution)/shard_map/pack/pallas_call | solution.py:111
  2.5 1.3 %collective-permute-start = (f32[656,128]{1,0:T(8,128)S(1)}, f32[656,128]{1,0:T(8,128)S(1)}, u32[]{:S(2)}, u32[]{:S(2)}) collective-permute-start(f32[656,128]{1,0:T(8,128)S(1)} %pack.1.refs_3_), channel_id=1, source_target_pairs={{0,4},{4,0},{8,12},{12,8},{16,20},{20,16},{24,28},{28,24},{1,5},{5... | collective-permute-start | bytes 1007624 | tf_op jit(solution)/shard_map/ppermute | solution.py:494
  3.8 1.2 %collective-permute-start.1 = (f32[656,128]{1,0:T(8,128)S(1)}, f32[656,128]{1,0:T(8,128)S(1)}, u32[]{:S(2)}, u32[]{:S(2)}) collective-permute-start(f32[656,128]{1,0:T(8,128)S(1)} %pack.1.refs_3_), channel_id=1, source_target_pairs={{0,2},{1,3},{2,0},{3,1},{4,6},{5,7},{6,4},{7,5},{8,10},{9,11},{10,... | collective-permute-start | bytes 1007624 | tf_op jit(solution)/shard_map/ppermute | solution.py:494
  5.0 1.2 %collective-permute-start.6 = (f32[656,128]{1,0:T(8,128)S(1)}, f32[656,128]{1,0:T(8,128)}, u32[]{:S(2)}, u32[]{:S(2)}) collective-permute-start(f32[656,128]{1,0:T(8,128)S(1)} %pack.1.refs_3_), channel_id=1, source_target_pairs={{0,1},{1,0},{2,3},{3,2},{4,5},{5,4},{6,7},{7,6},{8,9},{9,8},{10,11... | collective-permute-start | bytes 1007624 | tf_op jit(solution)/shard_map/ppermute | solution.py:494
  6.2 0.7 %fusion.3 = s32[12]{0:T(128)S(1)} fusion(pred[12]{0:T(512)(128)(4,1)} %constant.50, pred[12]{0:T(512)(128)(4,1)} %constant.51, pred[]{:T(512)S(6)} %eq.35, s32[12]{0:T(128)} %constant.42.clone, s32[]{:T(128)S(6)} %axis_index.22), kind=kLoop, calls=%fused_computation.9 | loop fusion | flops 72 | bytes 125 | tf_op jit(solution)/shard_map/add | solution.py:525
  7.6 0.0 copy-start
  7.6 1.7 %copy-done = f32[1,1,576,1024]{3,2,1,0:T(8,128)S(1)} copy-done((f32[1,1,576,1024]{3,2,1,0:T(8,128)S(1)}, f32[1,1,576,1024]{3,2,1,0:T(8,128)}, u32[]{:S(2)}) %copy-start) | copy-done | bytes 2359320
  9.2 0.3 halve.1
  9.6 0.0 copy-done.2
  9.6 0.2 fusion
  9.8 0.1 select_reduce_fusion
  9.9 2.4 %collective-permute-done.1.refs_5_ = f32[656,128]{1,0:T(8,128)S(1)} collective-permute-done((f32[656,128]{1,0:T(8,128)S(1)}, f32[656,128]{1,0:T(8,128)S(1)}, u32[]{:S(2)}, u32[]{:S(2)}) %collective-permute-start.1) | collective-permute-done | bytes 335904 | tf_op jit(solution)/shard_map/ppermute | solution.py:494
  12.3 1.8 %collective-permute-start.2 = (f32[656,128]{1,0:T(8,128)S(1)}, f32[656,128]{1,0:T(8,128)S(1)}, u32[]{:S(2)}, u32[]{:S(2)}) collective-permute-start(f32[656,128]{1,0:T(8,128)S(1)} %collective-permute-done.1.refs_5_), channel_id=1, source_target_pairs={{0,1},{1,0},{2,3},{3,2},{4,5},{5,4},{6,7},{7,6},{8,9},{9,8},{10,11... | collective-permute-start | bytes 1007624 | tf_op jit(solution)/shard_map/ppermute | solution.py:494
  14.1 0.0 collective-permute-done.refs_6_.refs_3_
  14.1 0.0 collective-permute-start.3
  14.1 0.1 pad_add_fusion.refs_2_.odd_ref
  14.2 1.2 %collective-permute-start.4 = (f32[656,128]{1,0:T(8,128)S(1)}, f32[656,128]{1,0:T(8,128)S(1)}, u32[]{:S(2)}, u32[]{:S(2)}) collective-permute-start(f32[656,128]{1,0:T(8,128)S(1)} %collective-permute-done.refs_6_.refs_3_), channel_id=1, source_target_pairs={{0,2},{1,3},{2,0},{3,1},{4,6},{5,7},{6,4},{7,5},{8,10},{9,11},{10,... | collective-permute-start | bytes 1007624 | tf_op jit(solution)/shard_map/ppermute | solution.py:494
  15.4 3.2 %collective-permute-start.5 = (f32[656,128]{1,0:T(8,128)S(1)}, f32[656,128]{1,0:T(8,128)S(1)}, u32[]{:S(2)}, u32[]{:S(2)}) collective-permute-start(f32[656,128]{1,0:T(8,128)S(1)} %collective-permute-done.refs_6_.refs_3_), channel_id=1, source_target_pairs={{0,8},{8,16},{16,24},{12,4},{20,12},{28,20},{1,9},{9,17},{17,25},{... | collective-permute-start | bytes 1007624 | tf_op jit(solution)/shard_map/ppermute | solution.py:506
  18.6 0.0 collective-permute-done.6.refs_4_
  18.6 0.0 collective-permute-done.2.refs_7_.refs_4_
  18.6 0.0 collective-permute-done.3.refs_8_.refs_5_
  18.6 8.3 %phase0.1 = (bf16[240,1024]{1,0:T(8,128)(2,1)S(1)}, bf16[240,1024]{1,0:T(8,128)(2,1)S(1)}, f32[240,240]{1,0:T(8,128)S(1)}, f32[240,576]{1,0:T(8,128)S(1)}, f32[3,16,128]{2,1,0:T(8,128)S(1)}) custom-call(s32[12]{0:T(128)S(1)} %compare_select_fusion.1.refs_0_, f32[1,1]{1,0:T(1,128)S(6)} %copy.13.refs_1_, s32[2]{0:T(128)S(1)} %pad_add_fusion.refs_2_.odd_ref, ...), custom_call_target="tpu_custom_call" | custom-call | flops 6000000000 | bytes 4000000 | tf_op jit(solution)/shard_map/phase0/pallas_call | solution.py:412
  26.9 0.0 collective-permute-done.4.refs_6_.refs_4_
  26.9 0.0 collective-permute-done.5.refs_7_.refs_5_
  27.0 1.1 %collective-permute-start.7 = (f32[656,128]{1,0:T(8,128)S(1)}, f32[656,128]{1,0:T(8,128)S(1)}, u32[]{:S(2)}, u32[]{:S(2)}) collective-permute-start(f32[656,128]{1,0:T(8,128)S(1)} %collective-permute-done.4.refs_6_.refs_4_), channel_id=1, source_target_pairs={{0,1},{1,0},{2,3},{3,2},{4,5},{5,4},{6,7},{7,6},{8,9},{9,8},{10,11... | collective-permute-start | bytes 1007624 | tf_op jit(solution)/shard_map/ppermute | solution.py:494
  28.1 0.1 collective-permute-start.8
  28.2 0.3 collective-permute-start.9
  28.4 0.9 %collective-permute-done.7.refs_8_.refs_6_ = f32[656,128]{1,0:T(8,128)S(1)} collective-permute-done((f32[656,128]{1,0:T(8,128)S(1)}, f32[656,128]{1,0:T(8,128)S(1)}, u32[]{:S(2)}, u32[]{:S(2)}) %collective-permute-start.7) | collective-permute-done | bytes 335904 | tf_op jit(solution)/shard_map/ppermute | solution.py:494
  29.4 0.0 copy-start.1
  29.4 9.5 %phase1.1 = (bf16[240,1024]{1,0:T(8,128)(2,1)S(1)}, bf16[240,1024]{1,0:T(8,128)(2,1)S(1)}, f32[480,480]{1,0:T(8,128)S(1)}, f32[480,576]{1,0:T(8,128)S(1)}, f32[3,16,128]{2,1,0:T(8,128)S(1)}) custom-call(s32[12]{0:T(128)S(1)} %compare_select_fusion.1.refs_0_, f32[1,1]{1,0:T(1,128)S(6)} %copy.13.refs_1_, s32[2]{0:T(128)S(1)} %pad_add_fusion.refs_2_.odd_ref, ...), custom_call_target="tpu_custom_call" | custom-call | flops 6000000000 | bytes 4000000 | tf_op jit(solution)/shard_map/phase1/pallas_call | solution.py:412
  38.9 0.0 collective-permute-done.9.refs_8_
  38.9 0.4 collective-permute-start.10
  39.4 0.1 fusion.1.pos_ref
  39.4 0.0 collective-permute-done.8.refs_7_
  39.4 1.2 %collective-permute-done.10.refs_9_ = f32[656,128]{1,0:T(8,128)S(1)} collective-permute-done((f32[656,128]{1,0:T(8,128)S(1)}, f32[656,128]{1,0:T(8,128)S(1)}, u32[]{:S(2)}, u32[]{:S(2)}) %collective-permute-start.10) | collective-permute-done | bytes 335904 | tf_op jit(solution)/shard_map/ppermute | solution.py:494
  40.6 0.0 copy-done.1
  40.6 9.6 %phase2.1 = (f32[240,576]{1,0:T(8,128)S(1)}, f32[480,240]{1,0:T(8,128)S(1)}, f32[16,576]{1,0:T(8,128)S(1)}, f32[16,576]{1,0:T(8,128)S(1)}, f32[16,576]{1,0:T(8,1...) custom-call(s32[12]{0:T(128)S(1)} %compare_select_fusion.1.refs_0_, f32[1,1]{1,0:T(1,128)S(6)} %copy.13.refs_1_, ...), custom_call_target="tpu_custom_call" | custom-call | flops 6000000000 | bytes 4000000 | tf_op jit(solution)/shard_map/phase2/pallas_call | solution.py:412
  50.2 0.1 collective-permute-start.11
  50.3 3.2 %collective-permute-start.12 = (f32[16,576]{1,0:T(8,128)S(1)}, f32[16,576]{1,0:T(8,128)S(1)}, u32[]{:S(2)}, u32[]{:S(2)}) collective-permute-start(f32[16,576]{1,0:T(8,128)S(1)} %get-tuple-element.47), channel_id=1, source_target_pairs={{4,8},{12,16},{20,24},{8,4},{16,12},{24,20},{5,9},{13,17},{21,25},... | collective-permute-start | bytes 110600 | tf_op jit(solution)/shard_map/ppermute | solution.py:500
  53.5 1.0 %collective-permute-start.13 = (f32[16,96]{1,0:T(8,128)S(1)}, f32[16,96]{1,0:T(8,128)S(1)}, u32[]{:S(2)}, u32[]{:S(2)}) collective-permute-start(f32[16,96]{1,0:T(8,128)S(1)} %get-tuple-element.48), channel_id=1, source_target_pairs={{0,1},{1,0},{2,3},{3,2},{4,5},{5,4},{6,7},{7,6},{8,9},{9,8},{10,11... | collective-permute-start | bytes 18440 | tf_op jit(solution)/shard_map/ppermute | solution.py:494
  54.6 2.4 %collective-permute-start.14 = (f32[16,96]{1,0:T(8,128)S(1)}, f32[16,96]{1,0:T(8,128)S(1)}, u32[]{:S(2)}, u32[]{:S(2)}) collective-permute-start(f32[16,96]{1,0:T(8,128)S(1)} %get-tuple-element.49), channel_id=1, source_target_pairs={{1,2},{2,1},{5,6},{6,5},{9,10},{10,9},{13,14},{14,13},{17,18},{18,... | collective-permute-start | bytes 18440 | tf_op jit(solution)/shard_map/ppermute | solution.py:500
  57.0 1.4 %close.1 = f32[720,576]{1,0:T(8,128)S(1)} custom-call(s32[9]{0:T(128)S(1)} %fusion.1.pos_ref, f32[480,576]{1,0:T(8,128)S(1)} %get-tuple-element.35.refs_17_.w_ref, f32[480,240]{1,0:T(8,128)S(1)} %get-tuple-element.43.v_ref, f32[240,576]{1,0:T(8,128)S(1)} %get-tuple-element.44.z_ref), custom_call_target="tpu_custom_call" | custom-call | flops 500000000 | bytes 6000000 | tf_op jit(solution)/shard_map/close/pallas_call | solution.py:453
  58.4 1.8 %copy.12 = f32[1,1,720,576]{2,3,1,0:T(8,128)} copy(f32[1,1,720,576]{3,2,1,0:T(8,128)S(1)} %bitcast.4) | data formatting | bytes 3317760
  60.1 0.0 collective-permute-done.13.pair_ref
  60.1 0.0 collective-permute-done.14.mid_ref
  60.1 0.0 collective-permute-done.11.near_ref
  60.1 0.0 collective-permute-done.12.far_ref
  60.2 1.7 %blend.1 = f32[16,24,24]{2,1,0:T(8,128)} custom-call(s32[2]{0:T(128)S(1)} %pad_add_fusion.refs_2_.odd_ref, f32[16,576]{1,0:T(8,128)S(1)} %get-tuple-element.45.co_ref, f32[16,576]{1,0:T(8,128)S(1)} %collective-permute-done.11.near_ref, f32[16,576]{1,0:T(8,128)S(1)} %collective-permute-done.12.far_ref, f32[16,96]{1,0:T(8,128)S(1)} %collective-permute-done.13.pair_ref, ...), custom_call_target="tpu_custom_call" | custom-call | tf_op jit(solution)/shard_map/blend/pallas_call | solution.py:482
  (1 shorter events, 0.0 us)
Async XLA Ops:
  0.6 9.0 %copy-start.2 = (s32[1,1,9]{2,1,0:T(1,128)S(1)}, s32[1,1,9]{2,1,0:T(1,128)}, u32[]{:S(2)}) copy-start(s32[1,1,9]{2,1,0:T(1,128)} %param.13) | copy-start | bytes 112
  2.5 11.6 %collective-permute-start = (f32[656,128]{1,0:T(8,128)S(1)}, f32[656,128]{1,0:T(8,128)S(1)}, u32[]{:S(2)}, u32[]{:S(2)}) collective-permute-start(f32[656,128]{1,0:T(8,128)S(1)} %pack.1.refs_3_), channel_id=1, source_target_pairs={{0,4},{4,0},{8,12},{12,8},{16,20},{20,16},{24,28},{28,24},{1,5},{5... | collective-permute-start | bytes 1007624 | tf_op jit(solution)/shard_map/ppermute | solution.py:494
  3.8 8.5 %collective-permute-start.1 = (f32[656,128]{1,0:T(8,128)S(1)}, f32[656,128]{1,0:T(8,128)S(1)}, u32[]{:S(2)}, u32[]{:S(2)}) collective-permute-start(f32[656,128]{1,0:T(8,128)S(1)} %pack.1.refs_3_), channel_id=1, source_target_pairs={{0,2},{1,3},{2,0},{3,1},{4,6},{5,7},{6,4},{7,5},{8,10},{9,11},{10,... | collective-permute-start | bytes 1007624 | tf_op jit(solution)/shard_map/ppermute | solution.py:494
  5.0 13.6 %collective-permute-start.6 = (f32[656,128]{1,0:T(8,128)S(1)}, f32[656,128]{1,0:T(8,128)}, u32[]{:S(2)}, u32[]{:S(2)}) collective-permute-start(f32[656,128]{1,0:T(8,128)S(1)} %pack.1.refs_3_), channel_id=1, source_target_pairs={{0,1},{1,0},{2,3},{3,2},{4,5},{5,4},{6,7},{7,6},{8,9},{9,8},{10,11... | collective-permute-start | bytes 1007624 | tf_op jit(solution)/shard_map/ppermute | solution.py:494
  7.6 1.7 %copy-start = (f32[1,1,576,1024]{3,2,1,0:T(8,128)S(1)}, f32[1,1,576,1024]{3,2,1,0:T(8,128)}, u32[]{:S(2)}) copy-start(f32[1,1,576,1024]{3,2,1,0:T(8,128)} %t_ref.1) | copy-start | bytes 7077892
  12.3 6.3 %collective-permute-start.2 = (f32[656,128]{1,0:T(8,128)S(1)}, f32[656,128]{1,0:T(8,128)S(1)}, u32[]{:S(2)}, u32[]{:S(2)}) collective-permute-start(f32[656,128]{1,0:T(8,128)S(1)} %collective-permute-done.1.refs_5_), channel_id=1, source_target_pairs={{0,1},{1,0},{2,3},{3,2},{4,5},{5,4},{6,7},{7,6},{8,9},{9,8},{10,11... | collective-permute-start | bytes 1007624 | tf_op jit(solution)/shard_map/ppermute | solution.py:494
  14.1 4.5 %collective-permute-start.3 = (f32[656,128]{1,0:T(8,128)S(1)}, f32[656,128]{1,0:T(8,128)S(1)}, u32[]{:S(2)}, u32[]{:S(2)}) collective-permute-start(f32[656,128]{1,0:T(8,128)S(1)} %collective-permute-done.refs_6_.refs_3_), channel_id=1, source_target_pairs={{0,1},{1,0},{2,3},{3,2},{4,5},{5,4},{6,7},{7,6},{8,9},{9,8},{10,11... | collective-permute-start | bytes 1007624 | tf_op jit(solution)/shard_map/ppermute | solution.py:494
  14.2 12.8 %collective-permute-start.4 = (f32[656,128]{1,0:T(8,128)S(1)}, f32[656,128]{1,0:T(8,128)S(1)}, u32[]{:S(2)}, u32[]{:S(2)}) collective-permute-start(f32[656,128]{1,0:T(8,128)S(1)} %collective-permute-done.refs_6_.refs_3_), channel_id=1, source_target_pairs={{0,2},{1,3},{2,0},{3,1},{4,6},{5,7},{6,4},{7,5},{8,10},{9,11},{10,... | collective-permute-start | bytes 1007624 | tf_op jit(solution)/shard_map/ppermute | solution.py:494
  15.4 11.6 %collective-permute-start.5 = (f32[656,128]{1,0:T(8,128)S(1)}, f32[656,128]{1,0:T(8,128)S(1)}, u32[]{:S(2)}, u32[]{:S(2)}) collective-permute-start(f32[656,128]{1,0:T(8,128)S(1)} %collective-permute-done.refs_6_.refs_3_), channel_id=1, source_target_pairs={{0,8},{8,16},{16,24},{12,4},{20,12},{28,20},{1,9},{9,17},{17,25},{... | collective-permute-start | bytes 1007624 | tf_op jit(solution)/shard_map/ppermute | solution.py:506
  27.0 2.4 %collective-permute-start.7 = (f32[656,128]{1,0:T(8,128)S(1)}, f32[656,128]{1,0:T(8,128)S(1)}, u32[]{:S(2)}, u32[]{:S(2)}) collective-permute-start(f32[656,128]{1,0:T(8,128)S(1)} %collective-permute-done.4.refs_6_.refs_4_), channel_id=1, source_target_pairs={{0,1},{1,0},{2,3},{3,2},{4,5},{5,4},{6,7},{7,6},{8,9},{9,8},{10,11... | collective-permute-start | bytes 1007624 | tf_op jit(solution)/shard_map/ppermute | solution.py:494
  28.1 11.4 %collective-permute-start.8 = (f32[656,128]{1,0:T(8,128)S(1)}, f32[656,128]{1,0:T(8,128)S(1)}, u32[]{:S(2)}, u32[]{:S(2)}) collective-permute-start(f32[656,128]{1,0:T(8,128)S(1)} %collective-permute-done.5.refs_7_.refs_5_), channel_id=1, source_target_pairs={{0,1},{1,0},{2,3},{3,2},{4,5},{5,4},{6,7},{7,6},{8,9},{9,8},{10,11... | collective-permute-start | bytes 1007624 | tf_op jit(solution)/shard_map/ppermute | solution.py:494
  28.2 10.7 %collective-permute-start.9 = (f32[656,128]{1,0:T(8,128)S(1)}, f32[656,128]{1,0:T(8,128)S(1)}, u32[]{:S(2)}, u32[]{:S(2)}) collective-permute-start(f32[656,128]{1,0:T(8,128)S(1)} %collective-permute-done.5.refs_7_.refs_5_), channel_id=1, source_target_pairs={{0,2},{1,3},{2,0},{3,1},{4,6},{5,7},{6,4},{7,5},{8,10},{9,11},{10,... | collective-permute-start | bytes 1007624 | tf_op jit(solution)/shard_map/ppermute | solution.py:494
  29.4 11.3 %copy-start.1 = (f32[4,576]{1,0:T(4,128)S(1)}, f32[4,576]{1,0:T(4,128)}, u32[]{:S(2)}) copy-start(f32[4,576]{1,0:T(4,128)} %constant.43.clone.refs_3_) | copy-start | bytes 27652
  38.9 1.7 %collective-permute-start.10 = (f32[656,128]{1,0:T(8,128)S(1)}, f32[656,128]{1,0:T(8,128)S(1)}, u32[]{:S(2)}, u32[]{:S(2)}) collective-permute-start(f32[656,128]{1,0:T(8,128)S(1)} %collective-permute-done.9.refs_8_), channel_id=1, source_target_pairs={{0,1},{1,0},{2,3},{3,2},{4,5},{5,4},{6,7},{7,6},{8,9},{9,8},{10,11... | collective-permute-start | bytes 1007624 | tf_op jit(solution)/shard_map/ppermute | solution.py:494
  50.2 9.9 %collective-permute-start.11 = (f32[16,576]{1,0:T(8,128)S(1)}, f32[16,576]{1,0:T(8,128)S(1)}, u32[]{:S(2)}, u32[]{:S(2)}) collective-permute-start(f32[16,576]{1,0:T(8,128)S(1)} %get-tuple-element.46), channel_id=1, source_target_pairs={{0,4},{4,0},{8,12},{12,8},{16,20},{20,16},{24,28},{28,24},{1,5},{5... | collective-permute-start | bytes 110600 | tf_op jit(solution)/shard_map/ppermute | solution.py:494
  50.3 9.9 %collective-permute-start.12 = (f32[16,576]{1,0:T(8,128)S(1)}, f32[16,576]{1,0:T(8,128)S(1)}, u32[]{:S(2)}, u32[]{:S(2)}) collective-permute-start(f32[16,576]{1,0:T(8,128)S(1)} %get-tuple-element.47), channel_id=1, source_target_pairs={{4,8},{12,16},{20,24},{8,4},{16,12},{24,20},{5,9},{13,17},{21,25},... | collective-permute-start | bytes 110600 | tf_op jit(solution)/shard_map/ppermute | solution.py:500
  53.5 6.6 %collective-permute-start.13 = (f32[16,96]{1,0:T(8,128)S(1)}, f32[16,96]{1,0:T(8,128)S(1)}, u32[]{:S(2)}, u32[]{:S(2)}) collective-permute-start(f32[16,96]{1,0:T(8,128)S(1)} %get-tuple-element.48), channel_id=1, source_target_pairs={{0,1},{1,0},{2,3},{3,2},{4,5},{5,4},{6,7},{7,6},{8,9},{9,8},{10,11... | collective-permute-start | bytes 18440 | tf_op jit(solution)/shard_map/ppermute | solution.py:494
  54.6 5.6 %collective-permute-start.14 = (f32[16,96]{1,0:T(8,128)S(1)}, f32[16,96]{1,0:T(8,128)S(1)}, u32[]{:S(2)}, u32[]{:S(2)}) collective-permute-start(f32[16,96]{1,0:T(8,128)S(1)} %get-tuple-element.49), channel_id=1, source_target_pairs={{1,2},{2,1},{5,6},{6,5},{9,10},{10,9},{13,14},{14,13},{17,18},{18,... | collective-permute-start | bytes 18440 | tf_op jit(solution)/shard_map/ppermute | solution.py:500
